TPU v7x, 256 devices: a whole 4x4x8 slice. The times are simulated.
256 devices in a mesh: frame: 32 (over z_hi, y, x), head: 8 (over z_lo, core).
Axes of the slice: x: 4, y: 4, z: 8 (z_hi: 2, z_lo: 4; z = z_hi * 4 + z_lo), core: 2. Of those that a mesh axis runs over, the one named last changes fastest.
Arguments:
- queries: bfloat16 [8192, 5120], P('frame', 'head'), may hold values from -12 to 12
- keys: bfloat16 [8192, 5120], P('frame', 'head'), may hold values from -12 to 12
- values: bfloat16 [8192, 5120], P('frame', 'head'), may hold values from -6 to 6
- policy_grad: bfloat16 [8192, 5120], P('frame', 'head'), may hold values from -6 to 6
- ref_velocity: bfloat16 [8192, 5120], P('frame', 'head'), may hold values from -6 to 6
- key_lists: int32 [64, 6], P('frame'), may hold values from 0 to 63, as said below
- frame_tokens: int32 [64], replicated, may hold values from 32 to 128, as said below
Outputs:
- grad_queries: bfloat16 [8192, 5120], P('frame', 'head')
- grad_keys: bfloat16 [8192, 5120], P('frame', 'head')
- grad_values: bfloat16 [8192, 5120], P('frame', 'head')
Inputs may be any that keep to these rules, and one draw needn't show every extreme that they name: `key_lists`: row b holds 6 distinct blocks: b, the next block of the same index of frame (cyclic over its 2 blocks), and four blocks on indices of frame that differ from b's index by distinct signed powers of two. `frame_tokens`: some block is full.
All inputs are finite; a program needn't handle non-finite values.
Results may differ from a plain program's by a relative error of at most 0.011.
Values may be sent and summed in bfloat16 or wider, within the bound.
No kernel may reach another device: no remote copies, remote signals or barrier semaphores. Data moves between devices by JAX's collectives and lax.ppermute only.
A program may use at most 128 MiB of HBM per device.

v0:
```python
import functools
import math

import jax
import jax.numpy as jnp
import numpy as np
from jax import lax
from jax.experimental import pallas as pl
from jax.experimental.pallas import tpu as pltpu
from jax.sharding import PartitionSpec as P

HEADS = 40
HD = 128
BLK = 128
TAIL = 16

kl_weight = 1.0


WIDE = 2

NT = (((1,), (1,)), ((), ()))
NN = (((1,), (0,)), ((), ()))


def matmul(left, right, dims):
    return lax.dot_general(left, right, dims, preferred_element_type=jnp.float32)


def diagonal():
    return lax.broadcasted_iota(jnp.int32, (BLK, BLK), 0) == lax.broadcasted_iota(
        jnp.int32, (BLK, BLK), 1
    )


def as_row(column, eye):
    return jnp.sum(jnp.where(eye, column, 0.0), axis=0, keepdims=True)


def as_column(row, eye):
    return jnp.sum(jnp.where(eye, row, 0.0), axis=1, keepdims=True)


def bring(sources, targets, sems, first, start):
    for position, (source, target) in enumerate(zip(sources, targets)):
        copy = pltpu.make_async_copy(source, target, sems.at[first + position])
        if start:
            copy.start()
        else:
            copy.wait()


def fetch(sources, pool, sems, used, start):
    height = pool.shape[0] // len(sources)
    for position, source in enumerate(sources):

        @pl.when(used[position] != 0)
        def _():
            copy = pltpu.make_async_copy(
                source, pool.at[pl.ds(position * height, height)], sems.at[position]
            )
            if start:
                copy.start()
            else:
                copy.wait()


def listed(pool, slots, block, list_len, cols):
    return jnp.concatenate(
        [
            pool[pl.ds(pl.multiple_of(slots[block * list_len + s] * BLK, BLK), BLK), cols]
            for s in range(list_len)
        ],
        axis=0,
    )


def block_probs(query, key_block, counts, block, list_len, scale):
    scores = matmul(query, key_block, NT) * scale
    lane = lax.broadcasted_iota(jnp.int32, (BLK, BLK), 1)
    scores = jnp.concatenate(
        [
            jnp.where(
                lane < counts[block * list_len + s], scores[:, s * BLK : (s + 1) * BLK], -1e30
            )
            for s in range(list_len)
        ],
        axis=1,
    )
    highest = jnp.max(scores, axis=-1, keepdims=True)
    expd = jnp.exp(scores - highest)
    total = jnp.sum(expd, axis=-1, keepdims=True)
    return expd * (1.0 / total), highest + jnp.log(total)


def forward_kernel(slots, counts, used, *rest, classes, list_len, scale):
    queries_in, velocity_in = rest[:2]
    key_refs, value_refs = rest[2 : 2 + classes], rest[2 + classes : 2 + 2 * classes]
    (
        attn,
        lse,
        squares,
        queries,
        ref_velocity,
        key_pool,
        value_pool,
        sems,
        key_sems,
        value_sems,
    ) = rest[2 + 2 * classes :]
    bring((queries_in, velocity_in), (queries, ref_velocity), sems, 0, True)
    fetch(key_refs, key_pool, key_sems, used, True)
    fetch(value_refs, value_pool, value_sems, used, True)
    rows, cols = queries.shape
    eye = diagonal()
    bring((queries_in, velocity_in), (queries, ref_velocity), sems, 0, False)
    fetch(key_refs, key_pool, key_sems, used, False)
    for block in range(rows // BLK):
        span = slice(block * BLK, (block + 1) * BLK)
        total = jnp.zeros((BLK, 1), jnp.float32)
        for head in range(cols // HD):
            hs = slice(head * HD, (head + 1) * HD)
            keys = listed(key_pool, slots, block, list_len, hs)
            probs, log_sum = block_probs(queries[span, hs], keys, counts, block, list_len, scale)
            if block == 0 and head == 0:
                fetch(value_refs, value_pool, value_sems, used, False)
            values = listed(value_pool, slots, block, list_len, hs)
            out = matmul(probs.astype(jnp.bfloat16), values, NN)
            attn[span, hs] = out
            diff = out - ref_velocity[span, hs].astype(jnp.float32)
            total = total + jnp.sum(diff * diff, axis=1, keepdims=True)
            lse[block * 8 : block * 8 + 8, hs] = jnp.broadcast_to(as_row(log_sum, eye), (8, HD))
        squares[block : block + 1, :] = as_row(total, eye)


def upstream_kernel(squares, *rest):
    sources = rest[:4]
    grad, lse, attn, policy_grad, ref_velocity, sems = rest[4:]
    bring(sources, (lse, attn, policy_grad, ref_velocity), sems, 0, True)
    rows, cols = attn.shape
    eye = diagonal()
    weights = []
    for block in range(rows // BLK):
        kl = as_column(squares[block : block + 1, :], eye) / (HEADS * HD)
        weights.append(kl_weight / (1.0 + kl))
    bring(sources, (lse, attn, policy_grad, ref_velocity), sems, 0, False)
    row = lax.broadcasted_iota(jnp.int32, (8, HD), 0)
    tails = []
    for block in range(rows // BLK):
        span = slice(block * BLK, (block + 1) * BLK)
        parts = []
        for head in range(cols // HD):
            hs = slice(head * HD, (head + 1) * HD)
            out = attn[span, hs]
            diff = out - ref_velocity[span, hs].astype(jnp.float32)
            upstream = (policy_grad[span, hs].astype(jnp.float32) + diff * weights[block]).astype(
                jnp.bfloat16
            )
            grad[span, hs] = upstream
            delta = jnp.sum(upstream.astype(jnp.float32) * out, axis=1, keepdims=True)
            tail = jnp.zeros((8, HD), jnp.float32)
            stats = (
                lse[block * 8 : block * 8 + 8, hs],
                jnp.broadcast_to(as_row(delta, eye), (8, HD)),
            )
            for base, left in enumerate(stats):
                for piece in range(3):
                    rounded = left.astype(jnp.bfloat16).astype(jnp.float32)
                    tail = jnp.where(row == base * 3 + piece, rounded, tail)
                    left = left - rounded
            parts.append(tail)
        tails.append(jnp.concatenate(parts, axis=1))
    grad[rows : rows + TAIL, :] = jnp.concatenate(tails, axis=0).astype(jnp.bfloat16)


def query_kernel(slots, counts, used, *rest, classes, list_len, scale):
    sources = rest[:3]
    key_refs, value_refs = rest[3 : 3 + classes], rest[3 + classes : 3 + 2 * classes]
    (
        grad_queries,
        queries,
        grad,
        attn,
        key_pool,
        value_pool,
        sems,
        key_sems,
        value_sems,
    ) = rest[3 + 2 * classes :]
    bring(sources, (queries, grad, attn), sems, 0, True)
    fetch(key_refs, key_pool, key_sems, used, True)
    fetch(value_refs, value_pool, value_sems, used, True)
    rows, cols = queries.shape
    bring(sources, (queries, grad, attn), sems, 0, False)
    fetch(key_refs, key_pool, key_sems, used, False)
    for block in range(rows // BLK):
        span = slice(block * BLK, (block + 1) * BLK)
        for head in range(cols // HD):
            hs = slice(head * HD, (head + 1) * HD)
            keys = listed(key_pool, slots, block, list_len, hs)
            probs, _ = block_probs(queries[span, hs], keys, counts, block, list_len, scale)
            if block == 0 and head == 0:
                fetch(value_refs, value_pool, value_sems, used, False)
            values = listed(value_pool, slots, block, list_len, hs)
            upstream = grad[span, hs]
            delta = jnp.sum(upstream.astype(jnp.float32) * attn[span, hs], axis=1, keepdims=True)
            grad_probs = matmul(upstream, values, NT)
            grad_scores = (probs * (grad_probs - delta)).astype(jnp.bfloat16)
            grad_queries[span, hs] = (matmul(grad_scores, keys, NN) * scale).astype(jnp.bfloat16)


def naming_kernel(own, valid, *rest, classes, list_len, blocks, rows):
    query_refs = rest[:classes]
    names, lists, sems = rest[classes:]
    targets = [lists.at[pl.ds(position * TAIL, TAIL)] for position in range(classes)]
    sources = [ref.at[pl.ds(rows, TAIL), pl.ds(0, HD)] for ref in query_refs]
    bring(sources, targets, sems, 0, True)
    bring(sources, targets, sems, 0, False)
    names[...] = jnp.zeros_like(names)
    lane = lax.broadcasted_iota(jnp.int32, (TAIL, HD), 1)
    place = lax.broadcasted_iota(jnp.int32, (1, HD), 1)
    for position in range(classes):
        ids = lists[position * TAIL : (position + 1) * TAIL, :].astype(jnp.float32)
        row = jnp.zeros((1, HD), jnp.float32)
        for block in range(blocks):
            mine = (own[0] + block).astype(jnp.float32)
            hit = jnp.where((ids == mine) & (lane < list_len), 1.0, 0.0)
            hit = jnp.max(hit, axis=1, keepdims=True)
            for part in range(blocks):
                row = jnp.where(place == part * blocks + block, hit[part : part + 1], row)
        row = row * valid[position].astype(jnp.float32)
        names[position : position + 1, :] = row.astype(jnp.int32)


def key_kernel(names, counts, *rest, classes, scale):
    keys_in, values_in = rest[:2]
    query_refs, grad_refs = rest[2 : 2 + classes], rest[2 + classes : 2 + 2 * classes]
    (
        grad_keys,
        grad_values,
        keys,
        values,
        query_pool,
        grad_pool,
        acc_k,
        acc_v,
        entries,
        used,
        sems,
        query_sems,
        grad_sems,
    ) = rest[2 + 2 * classes :]
    rows, cols = keys.shape
    blocks = rows // BLK
    height = rows + TAIL
    bring((keys_in, values_in), (keys, values), sems, 0, True)
    for position in range(classes):
        total = names[position, 0]
        for place in range(1, blocks * blocks):
            total = total + names[position, place]
        used[position] = total
    fetch(query_refs, query_pool, query_sems, used, True)
    fetch(grad_refs, grad_pool, grad_sems, used, True)
    lengths = []
    for block in range(blocks):

        def collect(entry, length, block=block):
            hit = names[entry // blocks, (entry % blocks) * blocks + block]
            entries[block, length] = entry
            return length + hit

        length = lax.fori_loop(0, classes * blocks, collect, jnp.int32(0))
        entries[block, length] = 0
        lengths.append(length)
    acc_k[...] = jnp.zeros_like(acc_k)
    acc_v[...] = jnp.zeros_like(acc_v)
    bring((keys_in, values_in), (keys, values), sems, 0, False)
    fetch(query_refs, query_pool, query_sems, used, False)
    fetch(grad_refs, grad_pool, grad_sems, used, False)
    row_in_block = lax.broadcasted_iota(jnp.int32, (BLK, WIDE * BLK), 0)
    for block in range(blocks):
        key_rows = slice(block * BLK, (block + 1) * BLK)
        valid = row_in_block < counts[block]
        length = lengths[block]

        def step(chunk, carry, block=block, key_rows=key_rows, valid=valid, length=length):
            places = []
            for lane in range(WIDE):
                index = chunk * WIDE + lane
                live = index < length
                entry = jnp.where(live, entries[block, jnp.minimum(index, length)], 0)
                position, part = entry // blocks, entry % blocks
                places.append(
                    (
                        pl.ds(pl.multiple_of(position * height + part * BLK, 16), BLK),
                        pl.ds(pl.multiple_of(position * height + rows, 16), TAIL),
                        part == 0,
                        jnp.where(live, 0.0, 1e30),
                    )
                )
            for head in range(cols // HD):
                hs = slice(head * HD, (head + 1) * HD)
                query = jnp.concatenate([query_pool[p[0], hs] for p in places], axis=0)
                upstream = jnp.concatenate([grad_pool[p[0], hs] for p in places], axis=0)
                sums, deltas = [], []
                for _, stat_rows, first, extra in places:
                    stats = grad_pool[stat_rows, hs].astype(jnp.float32)
                    stats = jnp.where(first, stats[:8], stats[8:])
                    sums.append(stats[0:1] + stats[1:2] + stats[2:3] + extra)
                    deltas.append(stats[3:4] + stats[4:5] + stats[5:6])
                log_sum = jnp.concatenate(sums, axis=1)
                delta = jnp.concatenate(deltas, axis=1)
                scores = matmul(keys[key_rows, hs], query, NT) * scale - log_sum
                probs = jnp.exp(jnp.where(valid, scores, -1e30))
                grad_probs = matmul(values[key_rows, hs], upstream, NT)
                grad_scores = (probs * (grad_probs - delta)).astype(jnp.bfloat16)
                acc_v[key_rows, hs] += matmul(probs.astype(jnp.bfloat16), upstream, NN)
                acc_k[key_rows, hs] += matmul(grad_scores, query, NN)
            return carry

        lax.fori_loop(0, (length + WIDE - 1) // WIDE, step, 0)
        grad_keys[key_rows, :] = (acc_k[key_rows, :] * scale).astype(jnp.bfloat16)
        grad_values[key_rows, :] = acc_v[key_rows, :].astype(jnp.bfloat16)


SMEM = pl.BlockSpec(memory_space=pltpu.SMEM)
VMEM = pl.BlockSpec(memory_space=pltpu.VMEM)
ANY = pl.BlockSpec(memory_space=pltpu.HBM)


FRAMES = 32
GRID = [(z, y, x) for z in range(2) for y in range(4) for x in range(4)]


def at(z, y, x):
    return z * 16 + y * 4 + x


def flip(bit):
    return [(f, f ^ bit) for f in range(FRAMES)]


def carry_pairs(bit, keep):
    pairs = []
    for f in range(FRAMES):
        if f & bit and f + bit < FRAMES and keep(f, f + bit):
            pairs += [(f, f + bit), (f + bit, f)]
    return pairs


def any_pair(f, g):
    return True


def same_half(f, g):
    return f >> 4 == g >> 4


DIRECT = [
    ("half", "own", flip(16)),
    ("step8", "own", carry_pairs(8, any_pair)),
    ("flip8", "own", flip(8)),
    ("flip4", "own", flip(4)),
    ("step4", "own", carry_pairs(4, same_half)),
    ("flip2", "own", flip(2)),
    ("flip1", "own", flip(1)),
    ("step1", "own", carry_pairs(1, same_half)),
]
RELAYED = [
    (
        "wrap4",
        "half",
        [(at(1, 3, x), at(1, 0, x)) for x in range(4)]
        + [(at(0, 0, x), at(0, 3, x)) for x in range(4)],
    ),
    (
        "wrap2",
        "step8",
        [
            (at(1, 1, 2), at(1, 0, 0)),
            (at(1, 1, 3), at(1, 0, 1)),
            (at(0, 2, 0), at(0, 3, 2)),
            (at(0, 2, 1), at(0, 3, 3)),
        ],
    ),
    ("wrap1", "step8", [(at(1, 1, 3), at(1, 0, 0)), (at(0, 2, 0), at(0, 3, 3))]),
    (
        "row2",
        "turn",
        [(at(z, y, x), at(z, y, x - 2)) for z, y, x in GRID if y > 0 and x > 1]
        + [(at(z, y, x), at(z, y, x + 2)) for z, y, x in GRID if y < 3 and x < 2],
    ),
]
NAMES = ["own"] + [name for name, _, _ in DIRECT + RELAYED]


def turn_takes_flip(f):
    return (f & 3 >= 2) == (f >> 2 & 1 == 1)


def owners():
    held = {"own": list(range(FRAMES))}
    for name, sent, pairs in DIRECT + RELAYED:
        if sent == "turn":
            held["turn"] = [
                held["flip4" if turn_takes_flip(f) else "step4"][f] for f in range(FRAMES)
            ]
        held[name] = [-1] * FRAMES
        for source, target in pairs:
            held[name][target] = held[sent][source]
    table = np.array([held[name] for name in NAMES])
    for f in range(FRAMES):
        got = sorted(o for o in table[:, f] if o >= 0)
        near = {f + s * (1 << level) for level in range(5) for s in (1, -1)} | {f}
        assert got == sorted(o for o in near if 0 <= o < FRAMES)
    return table


def spread(value, turn_flip):
    held = {"own": value}
    for name, sent, pairs in DIRECT + RELAYED:
        if sent == "turn" and "turn" not in held:
            held["turn"] = jnp.where(turn_flip, held["flip4"], held["step4"])
        held[name] = lax.ppermute(held[sent], "frame", pairs)
    return [held[name] for name in NAMES]


def step(queries, keys, values, policy_grad, ref_velocity, key_lists, frame_tokens):
    rows, cols = queries.shape
    blocks = rows // BLK
    list_len = key_lists.shape[1]
    all_blocks = frame_tokens.shape[0]
    scale = 1.0 / math.sqrt(HD)
    assert lax.axis_size("frame") == FRAMES
    me = lax.axis_index("frame")
    classes = len(NAMES)
    f32 = jnp.float32
    turn_flip = (me % 4 >= 2) == (me // 4 % 2 == 1)

    key_pool = spread(keys, turn_flip)
    value_pool = spread(values, turn_flip)

    owner_here = lax.dynamic_slice(
        jnp.asarray(owners().T.astype(np.int32)), (me, 0), (1, classes)
    ).reshape(-1)
    owner = key_lists // blocks
    hits = owner[..., None] == owner_here
    slots = jnp.sum(jnp.where(hits, jnp.arange(classes, dtype=jnp.int32), 0), axis=-1)
    slots = (slots * blocks + key_lists % blocks).reshape(-1)
    used = jnp.any(hits, axis=(0, 1)).astype(jnp.int32)
    valid = (owner_here >= 0).astype(jnp.int32)
    ids = jnp.arange(all_blocks, dtype=jnp.int32)
    counts = jnp.sum(jnp.where(key_lists[..., None] == ids, frame_tokens, 0), axis=-1).reshape(-1)
    own = me * blocks + jnp.arange(blocks, dtype=jnp.int32)
    own_counts = jnp.sum(jnp.where(own[:, None] == ids, frame_tokens, 0), axis=-1)

    lists16 = jnp.pad(
        key_lists.astype(jnp.bfloat16), ((0, TAIL - blocks), (0, cols - list_len))
    )
    tailed = jnp.concatenate([queries, lists16], axis=0)
    tailed, slots, counts, used, valid, own, own_counts = lax.optimization_barrier(
        (tailed, slots, counts, used, valid, own, own_counts)
    )
    query_pool = spread(tailed, turn_flip)

    def shard(dtype=jnp.bfloat16, height=rows):
        return pltpu.VMEM((height, cols), dtype)

    def dma(count):
        return pltpu.SemaphoreType.DMA((count,))

    pools = [shard(height=classes * rows)] * 2
    params = pltpu.CompilerParams(vmem_limit_bytes=48 << 20)
    attn, lse, squares = pl.pallas_call(
        functools.partial(forward_kernel, classes=classes, list_len=list_len, scale=scale),
        out_shape=(
            jax.ShapeDtypeStruct((rows, cols), f32),
            jax.ShapeDtypeStruct((blocks * 8, cols), f32),
            jax.ShapeDtypeStruct((blocks, BLK), f32),
        ),
        in_specs=[SMEM] * 3 + [ANY] * (2 + 2 * classes),
        out_specs=(VMEM, VMEM, VMEM),
        scratch_shapes=[shard(), shard()] + pools + [dma(2), dma(classes), dma(classes)],
        compiler_params=params,
        name="forward",
    )(slots, counts, used, queries, ref_velocity, *key_pool, *value_pool)

    heads = lax.axis_size("head")
    hop = 1
    while hop < heads:
        squares = squares + lax.ppermute(squares, "head", [(i, i ^ hop) for i in range(heads)])
        hop *= 2

    grad = pl.pallas_call(
        upstream_kernel,
        out_shape=jax.ShapeDtypeStruct((rows + TAIL, cols), jnp.bfloat16),
        in_specs=[VMEM] + [ANY] * 4,
        out_specs=VMEM,
        scratch_shapes=[shard(f32, blocks * 8), shard(f32), shard(), shard(), dma(4)],
        compiler_params=params,
        name="upstream",
    )(squares, lse, attn, policy_grad, ref_velocity)

    grad_pool = spread(grad, turn_flip)

    names = pl.pallas_call(
        functools.partial(
            naming_kernel, classes=classes, list_len=list_len, blocks=blocks, rows=rows
        ),
        out_shape=jax.ShapeDtypeStruct((16, HD), jnp.int32),
        in_specs=[SMEM, SMEM] + [ANY] * classes,
        out_specs=VMEM,
        scratch_shapes=[pltpu.VMEM((classes * TAIL, HD), jnp.bfloat16), dma(classes)],
        compiler_params=params,
        name="naming",
    )(own, valid, *query_pool)

    grad_queries = pl.pallas_call(
        functools.partial(query_kernel, classes=classes, list_len=list_len, scale=scale),
        out_shape=jax.ShapeDtypeStruct((rows, cols), jnp.bfloat16),
        in_specs=[SMEM] * 3 + [ANY] * (3 + 2 * classes),
        out_specs=VMEM,
        scratch_shapes=[shard(), shard(height=rows + TAIL), shard(f32)]
        + pools
        + [dma(3), dma(classes), dma(classes)],
        compiler_params=params,
        name="grad_queries",
    )(slots, counts, used, queries, grad, attn, *key_pool, *value_pool)

    grad_keys, grad_values = pl.pallas_call(
        functools.partial(key_kernel, classes=classes, scale=scale),
        out_shape=(
            jax.ShapeDtypeStruct((rows, cols), jnp.bfloat16),
            jax.ShapeDtypeStruct((rows, cols), jnp.bfloat16),
        ),
        in_specs=[SMEM, SMEM] + [ANY] * (2 + 2 * classes),
        out_specs=(VMEM, VMEM),
        scratch_shapes=[shard(), shard()]
        + [shard(height=classes * (rows + TAIL))] * 2
        + [
            shard(f32),
            shard(f32),
            pltpu.SMEM((blocks, 32), jnp.int32),
            pltpu.SMEM((classes,), jnp.int32),
            dma(2),
            dma(classes),
            dma(classes),
        ],
        compiler_params=params,
        name="grad_keys_values",
    )(names, own_counts, keys, values, *query_pool, *grad_pool)
    return grad_queries, grad_keys, grad_values


def solution(mesh):
    in_specs = (
        P("frame", "head"),
        P("frame", "head"),
        P("frame", "head"),
        P("frame", "head"),
        P("frame", "head"),
        P("frame", None),
        P(),
    )
    out_specs = (P("frame", "head"), P("frame", "head"), P("frame", "head"))
    return jax.shard_map(step, mesh=mesh, in_specs=in_specs, out_specs=out_specs, check_vma=False)
```

profile of v0, /device:TPU:94, one launch (start us, length us, event | category | flops | bytes accessed | tf_op | source)
XLA Modules:
  0.0 266.3 jit_solution(14350398525729616742)
XLA Ops:
  0.6 5.5 %collective-permute-start = (bf16[256,640]{1,0:T(8,128)(2,1)}, bf16[256,640]{1,0:T(8,128)(2,1)S(1)}, u32[]{:S(2)}, u32[]{:S(2)}) collective-permute-start(bf16[256,640]{1,0:T(8,128)(2,1)} %rest_0_.5), channel_id=1, source_target_pairs={{0,128},{8,136},{16,144},{24,152},{32,160},{40,168},{48,176},{56,1... | collective-permute-start | bytes 983048 | tf_op jit(solution)/shard_map/ppermute | solution.py:424
  6.1 3.1 %collective-permute-start.1 = (bf16[256,640]{1,0:T(8,128)(2,1)}, bf16[256,640]{1,0:T(8,128)(2,1)S(1)}, u32[]{:S(2)}, u32[]{:S(2)}) collective-permute-start(bf16[256,640]{1,0:T(8,128)(2,1)} %rest_0_.5), channel_id=1, source_target_pairs={{64,128},{128,64},{72,136},{136,72},{80,144},{144,80},{88,152},{15... | collective-permute-start | bytes 983048 | tf_op jit(solution)/shard_map/ppermute | solution.py:424
  9.4 0.7 collective-permute-start.4
  10.1 0.8 copy.11
  10.9 19.0 %collective-permute-done.rest_3_.rest_4_ = bf16[256,640]{1,0:T(8,128)(2,1)S(1)} collective-permute-done((bf16[256,640]{1,0:T(8,128)(2,1)}, bf16[256,640]{1,0:T(8,128)(2,1)S(1)}, u32[]{:S(2)}, u32[]{:S(2)}) %collective-permute-start) | collective-permute-done | bytes 327712 | tf_op jit(solution)/shard_map/ppermute | solution.py:424
  29.9 8.8 %collective-permute-done.1.rest_4_.rest_5_ = bf16[256,640]{1,0:T(8,128)(2,1)S(1)} collective-permute-done((bf16[256,640]{1,0:T(8,128)(2,1)}, bf16[256,640]{1,0:T(8,128)(2,1)S(1)}, u32[]{:S(2)}, u32[]{:S(2)}) %collective-permute-start.1) | collective-permute-done | bytes 327712 | tf_op jit(solution)/shard_map/ppermute | solution.py:424
  38.8 0.7 dynamic-slice_bitcast_fusion
  39.5 0.7 collective-permute-start.7
  40.6 10.5 %collective-permute-start.13 = (bf16[256,640]{1,0:T(8,128)(2,1)}, bf16[256,640]{1,0:T(8,128)(2,1)S(1)}, u32[]{:S(2)}, u32[]{:S(2)}) collective-permute-start(bf16[256,640]{1,0:T(8,128)(2,1)} %rest_1_.3), channel_id=1, source_target_pairs={{64,128},{128,64},{72,136},{136,72},{80,144},{144,80},{88,152},{15... | collective-permute-start | bytes 983048 | tf_op jit(solution)/shard_map/ppermute | solution.py:424
  51.5 1.4 collective-permute-start.16
  53.5 3.0 %collective-permute-done.12.rest_16_.rest_17_ = bf16[256,640]{1,0:T(8,128)(2,1)S(1)} collective-permute-done((bf16[256,640]{1,0:T(8,128)(2,1)}, bf16[256,640]{1,0:T(8,128)(2,1)S(1)}, u32[]{:S(2)}, u32[]{:S(2)}) %collective-permute-start.12) | collective-permute-done | bytes 327712 | tf_op jit(solution)/shard_map/ppermute | solution.py:424
  56.4 3.6 %collective-permute-start.17 = (bf16[256,640]{1,0:T(8,128)(2,1)}, bf16[256,640]{1,0:T(8,128)(2,1)S(1)}, u32[]{:S(2)}, u32[]{:S(2)}) collective-permute-start(bf16[256,640]{1,0:T(8,128)(2,1)} %rest_1_.3), channel_id=1, source_target_pairs={{0,16},{8,24},{16,0},{24,8},{32,48},{40,56},{48,32},{56,40},{64,80... | collective-permute-start | bytes 983048 | tf_op jit(solution)/shard_map/ppermute | solution.py:424
  60.1 18.4 %collective-permute-done.13.rest_17_.rest_18_ = bf16[256,640]{1,0:T(8,128)(2,1)S(1)} collective-permute-done((bf16[256,640]{1,0:T(8,128)(2,1)}, bf16[256,640]{1,0:T(8,128)(2,1)S(1)}, u32[]{:S(2)}, u32[]{:S(2)}) %collective-permute-start.13) | collective-permute-done | bytes 327712 | tf_op jit(solution)/shard_map/ppermute | solution.py:424
  78.5 0.7 collective-permute-start.19
  79.2 1.3 collective-permute-start.8
  80.5 1.4 collective-permute-start.9
  82.0 6.6 %collective-permute-start.11 = (bf16[256,640]{1,0:T(8,128)(2,1)S(1)}, bf16[256,640]{1,0:T(8,128)(2,1)S(1)}, u32[]{:S(2)}, u32[]{:S(2)}) collective-permute-start(bf16[256,640]{1,0:T(8,128)(2,1)S(1)} %broadcast_select_fusion.3), channel_id=1, source_target_pairs={{48,32},{56,40},{80,64},{88,72},{112,96},{120,104},{176,160},{184,... | collective-permute-start | bytes 983048 | tf_op jit(solution)/shard_map/ppermute | solution.py:424
  88.7 0.5 collective-permute-done.18.rest_22_.rest_23_
  89.1 1.3 collective-permute-start.10
  90.4 1.3 collective-permute-start.20
  91.8 1.3 collective-permute-start.21
  93.3 2.3 collective-permute-done.9.rest_12_.rest_13_
  95.6 1.3 collective-permute-start.22
  96.9 0.7 compare_convert_fusion.valid
  97.6 17.7 %collective-permute-done.10.rest_13_.rest_14_ = bf16[256,640]{1,0:T(8,128)(2,1)S(1)} collective-permute-done((bf16[256,640]{1,0:T(8,128)(2,1)S(1)}, bf16[256,640]{1,0:T(8,128)(2,1)S(1)}, u32[]{:S(2)}, u32[]{:S(2)}) %collective-permute-start.10) | collective-permute-done | bytes 327712 | tf_op jit(solution)/shard_map/ppermute | solution.py:424
  115.4 4.7 %collective-permute-start.28 = (bf16[272,640]{1,0:T(8,128)(2,1)S(1)}, bf16[272,640]{1,0:T(8,128)(2,1)S(1)}, u32[]{:S(2)}, u32[]{:S(2)}) collective-permute-start(bf16[272,640]{1,0:T(8,128)(2,1)S(1)} %fusion.1.rest_0_.rest_2_), channel_id=1, source_target_pairs={{64,128},{128,64},{72,136},{136,72},{80,144},{144,80},{88,152},{15... | collective-permute-start | bytes 1044488 | tf_op jit(solution)/shard_map/ppermute | solution.py:424
  120.2 0.7 collective-permute-start.31
  120.9 1.0 broadcast_select_fusion.2
  122.3 1.3 collective-permute-start.23
  123.6 7.4 %collective-permute-done.23.rest_27_.rest_28_ = bf16[256,640]{1,0:T(8,128)(2,1)S(1)} collective-permute-done((bf16[256,640]{1,0:T(8,128)(2,1)S(1)}, bf16[256,640]{1,0:T(8,128)(2,1)S(1)}, u32[]{:S(2)}, u32[]{:S(2)}) %collective-permute-start.23) | collective-permute-done | bytes 327712 | tf_op jit(solution)/shard_map/ppermute | solution.py:424
  131.0 0.7 copy-done.14
  131.7 8.2 %forward.1 = (f32[256,640]{1,0:T(8,128)}, f32[16,640]{1,0:T(8,128)S(1)}, f32[2,128]{1,0:T(2,128)S(1)}) custom-call(s32[12]{0:T(128)S(1)} %reshape.20.slots, s32[12]{0:T(128)S(1)} %reshape.21.counts, s32[13]{0:T(128)S(1)} %convert_element_type.12.used, bf16[256,640]{1,0:T(8,128)(2,1)S(1)} %copy-done.2, bf16[256,640]{1,0:T(8,128)(2,1)S(1)} %copy-done.4, ...), custom_call_target="tpu_custom_call" | custom-call | tf_op jit(solution)/shard_map/forward/pallas_call | solution.py:474
  140.0 1.1 collective-permute-done.24
  141.2 3.6 %collective-permute-done.25 = f32[2,128]{1,0:T(2,128)S(1)} collective-permute-done((f32[2,128]{1,0:T(2,128)S(1)}, f32[2,128]{1,0:T(2,128)S(1)}, u32[]{:S(2)}, u32[]{:S(2)}) %collective-permute-start.25) | collective-permute-done | bytes 1056 | tf_op jit(solution)/shard_map/ppermute | solution.py:491
  144.8 1.2 collective-permute-start.26
  146.0 8.0 %collective-permute-start.29 = (bf16[272,640]{1,0:T(8,128)(2,1)S(1)}, bf16[272,640]{1,0:T(8,128)(2,1)S(1)}, u32[]{:S(2)}, u32[]{:S(2)}) collective-permute-start(bf16[272,640]{1,0:T(8,128)(2,1)S(1)} %fusion.1.rest_0_.rest_2_), channel_id=1, source_target_pairs={{0,64},{8,72},{16,80},{24,88},{32,96},{40,104},{48,112},{56,120},{... | collective-permute-start | bytes 1044488 | tf_op jit(solution)/shard_map/ppermute | solution.py:424
  154.3 3.6 %collective-permute-start.33 = (bf16[272,640]{1,0:T(8,128)(2,1)S(1)}, bf16[272,640]{1,0:T(8,128)(2,1)S(1)}, u32[]{:S(2)}, u32[]{:S(2)}) collective-permute-start(bf16[272,640]{1,0:T(8,128)(2,1)S(1)} %fusion.1.rest_0_.rest_2_), channel_id=1, source_target_pairs={{0,8},{8,0},{16,24},{24,16},{32,40},{40,32},{48,56},{56,48},{64,72... | collective-permute-start | bytes 1044488 | tf_op jit(solution)/shard_map/ppermute | solution.py:424
  157.9 0.7 collective-permute-start.34
  158.6 1.3 collective-permute-start.35
  160.0 1.7 upstream.1.rest_1_.rest_15_
  161.7 1.3 collective-permute-start.36
  163.0 3.6 %collective-permute-done.32.rest_6_.rest_8_ = bf16[272,640]{1,0:T(8,128)(2,1)S(1)} collective-permute-done((bf16[272,640]{1,0:T(8,128)(2,1)S(1)}, bf16[272,640]{1,0:T(8,128)(2,1)S(1)}, u32[]{:S(2)}, u32[]{:S(2)}) %collective-permute-start.32) | collective-permute-done | bytes 348192 | tf_op jit(solution)/shard_map/ppermute | solution.py:424
  166.5 1.3 collective-permute-start.37
  167.8 4.3 %collective-permute-done.33.rest_7_.rest_9_ = bf16[272,640]{1,0:T(8,128)(2,1)S(1)} collective-permute-done((bf16[272,640]{1,0:T(8,128)(2,1)S(1)}, bf16[272,640]{1,0:T(8,128)(2,1)S(1)}, u32[]{:S(2)}, u32[]{:S(2)}) %collective-permute-start.33) | collective-permute-done | bytes 348192 | tf_op jit(solution)/shard_map/ppermute | solution.py:424
  172.1 2.8 %collective-permute-start.38 = (bf16[272,640]{1,0:T(8,128)(2,1)S(1)}, bf16[272,640]{1,0:T(8,128)(2,1)S(1)}, u32[]{:S(2)}, u32[]{:S(2)}) collective-permute-start(bf16[272,640]{1,0:T(8,128)(2,1)S(1)} %broadcast_select_fusion.1), channel_id=1, source_target_pairs={{48,32},{56,40},{80,64},{88,72},{112,96},{120,104},{176,160},{184,... | collective-permute-start | bytes 1044488 | tf_op jit(solution)/shard_map/ppermute | solution.py:424
  175.0 0.6 collective-permute-start.42
  175.5 0.7 collective-permute-start.43
  176.2 3.3 %collective-permute-done.36.rest_10_.rest_12_ = bf16[272,640]{1,0:T(8,128)(2,1)S(1)} collective-permute-done((bf16[272,640]{1,0:T(8,128)(2,1)S(1)}, bf16[272,640]{1,0:T(8,128)(2,1)S(1)}, u32[]{:S(2)}, u32[]{:S(2)}) %collective-permute-start.36) | collective-permute-done | bytes 348192 | tf_op jit(solution)/shard_map/ppermute | solution.py:424
  179.5 16.8 %collective-permute-done.37.rest_11_.rest_13_ = bf16[272,640]{1,0:T(8,128)(2,1)S(1)} collective-permute-done((bf16[272,640]{1,0:T(8,128)(2,1)S(1)}, bf16[272,640]{1,0:T(8,128)(2,1)S(1)}, u32[]{:S(2)}, u32[]{:S(2)}) %collective-permute-start.37) | collective-permute-done | bytes 348192 | tf_op jit(solution)/shard_map/ppermute | solution.py:424
  196.3 3.4 %collective-permute-start.40 = (bf16[272,640]{1,0:T(8,128)(2,1)}, bf16[272,640]{1,0:T(8,128)(2,1)S(1)}, u32[]{:S(2)}, u32[]{:S(2)}) collective-permute-start(bf16[272,640]{1,0:T(8,128)(2,1)} %upstream.1.rest_1_.rest_15_), channel_id=1, source_target_pairs={{64,128},{128,64},{72,136},{136,72},{80,144},{144,80},{88,152},{15... | collective-permute-start | bytes 1044488 | tf_op jit(solution)/shard_map/ppermute | solution.py:424
  200.1 0.5 copy-done.6
  200.6 0.7 collective-permute-start.46
  201.3 23.5 %collective-permute-done.40.rest_17_ = bf16[272,640]{1,0:T(8,128)(2,1)S(1)} collective-permute-done((bf16[272,640]{1,0:T(8,128)(2,1)}, bf16[272,640]{1,0:T(8,128)(2,1)S(1)}, u32[]{:S(2)}, u32[]{:S(2)}) %collective-permute-start.40) | collective-permute-done | bytes 348192 | tf_op jit(solution)/shard_map/ppermute | solution.py:424
  224.8 1.3 collective-permute-start.47
  226.1 1.3 collective-permute-start.48
  227.4 1.3 collective-permute-start.49
  228.8 1.3 collective-permute-start.50
  230.1 8.4 %grad_queries.1 = bf16[256,640]{1,0:T(8,128)(2,1)} custom-call(s32[12]{0:T(128)S(1)} %reshape.20.slots, s32[12]{0:T(128)S(1)} %reshape.21.counts, s32[13]{0:T(128)S(1)} %convert_element_type.12.used, bf16[256,640]{1,0:T(8,128)(2,1)S(1)} %copy-done.2, bf16[272,640]{1,0:T(8,128)(2,1)} %upstream.1.rest_1_.rest_15_, ...), custom_call_target="tpu_custom_call" | custom-call | tf_op jit(solution)/shard_map/grad_queries/pallas_call | solution.py:518
  238.5 0.8 naming.1.names
  239.3 2.2 collective-permute-done.48.rest_25_
  241.5 12.2 %collective-permute-done.49.rest_26_ = bf16[272,640]{1,0:T(8,128)(2,1)S(1)} collective-permute-done((bf16[272,640]{1,0:T(8,128)(2,1)S(1)}, bf16[272,640]{1,0:T(8,128)(2,1)S(1)}, u32[]{:S(2)}, u32[]{:S(2)}) %collective-permute-start.49) | collective-permute-done | bytes 348192 | tf_op jit(solution)/shard_map/ppermute | solution.py:424
  253.7 0.7 copy-done.22
  254.5 0.7 copy-done.23
  255.2 10.9 %grad_keys_values.1 = (bf16[256,640]{1,0:T(8,128)(2,1)}, bf16[256,640]{1,0:T(8,128)(2,1)}) custom-call(s32[16,128]{1,0:T(8,128)S(1)} %naming.1.names, s32[2]{0:T(128)S(1)} %fusion.7.counts, bf16[256,640]{1,0:T(8,128)(2,1)S(1)} %copy-done, bf16[256,640]{1,0:T(8,128)(2,1)S(1)} %copy-done.1, bf16[272,640]{1,0:T(8,128)(2,1)S(1)} %fusion.1.rest_0_.rest_2_, ...), custom_call_target="tpu_custom_call" | custom-call | tf_op jit(solution)/shard_map/grad_keys_values/pallas_call | solution.py:530
  (121 shorter events, 3.4 us)
Async XLA Ops:
  0.6 29.3 %collective-permute-start = (bf16[256,640]{1,0:T(8,128)(2,1)}, bf16[256,640]{1,0:T(8,128)(2,1)S(1)}, u32[]{:S(2)}, u32[]{:S(2)}) collective-permute-start(bf16[256,640]{1,0:T(8,128)(2,1)} %rest_0_.5), channel_id=1, source_target_pairs={{0,128},{8,136},{16,144},{24,152},{32,160},{40,168},{48,176},{56,1... | collective-permute-start | bytes 983048 | tf_op jit(solution)/shard_map/ppermute | solution.py:424
  6.1 32.6 %collective-permute-start.1 = (bf16[256,640]{1,0:T(8,128)(2,1)}, bf16[256,640]{1,0:T(8,128)(2,1)S(1)}, u32[]{:S(2)}, u32[]{:S(2)}) collective-permute-start(bf16[256,640]{1,0:T(8,128)(2,1)} %rest_0_.5), channel_id=1, source_target_pairs={{64,128},{128,64},{72,136},{136,72},{80,144},{144,80},{88,152},{15... | collective-permute-start | bytes 983048 | tf_op jit(solution)/shard_map/ppermute | solution.py:424
  9.2 30.3 %collective-permute-start.2 = (bf16[256,640]{1,0:T(8,128)(2,1)}, bf16[256,640]{1,0:T(8,128)(2,1)S(1)}, u32[]{:S(2)}, u32[]{:S(2)}) collective-permute-start(bf16[256,640]{1,0:T(8,128)(2,1)} %rest_0_.5), channel_id=1, source_target_pairs={{0,64},{8,72},{16,80},{24,88},{32,96},{40,104},{48,112},{56,120},{... | collective-permute-start | bytes 983048 | tf_op jit(solution)/shard_map/ppermute | solution.py:424
  9.3 31.2 %collective-permute-start.3 = (bf16[256,640]{1,0:T(8,128)(2,1)}, bf16[256,640]{1,0:T(8,128)(2,1)S(1)}, u32[]{:S(2)}, u32[]{:S(2)}) collective-permute-start(bf16[256,640]{1,0:T(8,128)(2,1)} %rest_0_.5), channel_id=1, source_target_pairs={{0,32},{8,40},{16,48},{24,56},{32,0},{40,8},{48,16},{56,24},{64,96... | collective-permute-start | bytes 983048 | tf_op jit(solution)/shard_map/ppermute | solution.py:424
  9.4 31.1 %collective-permute-start.4 = (bf16[256,640]{1,0:T(8,128)(2,1)}, bf16[256,640]{1,0:T(8,128)(2,1)S(1)}, u32[]{:S(2)}, u32[]{:S(2)}) collective-permute-start(bf16[256,640]{1,0:T(8,128)(2,1)} %rest_0_.5), channel_id=1, source_target_pairs={{32,64},{64,32},{40,72},{72,40},{48,80},{80,48},{56,88},{88,56},{1... | collective-permute-start | bytes 983048 | tf_op jit(solution)/shard_map/ppermute | solution.py:424
  29.9 21.1 %collective-permute-start.5 = (bf16[256,640]{1,0:T(8,128)(2,1)}, bf16[256,640]{1,0:T(8,128)(2,1)S(1)}, u32[]{:S(2)}, u32[]{:S(2)}) collective-permute-start(bf16[256,640]{1,0:T(8,128)(2,1)} %rest_0_.5), channel_id=1, source_target_pairs={{0,16},{8,24},{16,0},{24,8},{32,48},{40,56},{48,32},{56,40},{64,80... | collective-permute-start | bytes 983048 | tf_op jit(solution)/shard_map/ppermute | solution.py:424
  38.7 12.5 %collective-permute-start.6 = (bf16[256,640]{1,0:T(8,128)(2,1)}, bf16[256,640]{1,0:T(8,128)(2,1)S(1)}, u32[]{:S(2)}, u32[]{:S(2)}) collective-permute-start(bf16[256,640]{1,0:T(8,128)(2,1)} %rest_0_.5), channel_id=1, source_target_pairs={{0,8},{8,0},{16,24},{24,16},{32,40},{40,32},{48,56},{56,48},{64,72... | collective-permute-start | bytes 983048 | tf_op jit(solution)/shard_map/ppermute | solution.py:424
  39.5 12.0 %collective-permute-start.7 = (bf16[256,640]{1,0:T(8,128)(2,1)}, bf16[256,640]{1,0:T(8,128)(2,1)S(1)}, u32[]{:S(2)}, u32[]{:S(2)}) collective-permute-start(bf16[256,640]{1,0:T(8,128)(2,1)} %rest_0_.5), channel_id=1, source_target_pairs={{8,16},{16,8},{24,32},{32,24},{40,48},{48,40},{56,64},{64,56},{72,... | collective-permute-start | bytes 983048 | tf_op jit(solution)/shard_map/ppermute | solution.py:424
  40.5 15.9 %collective-permute-start.12 = (bf16[256,640]{1,0:T(8,128)(2,1)}, bf16[256,640]{1,0:T(8,128)(2,1)S(1)}, u32[]{:S(2)}, u32[]{:S(2)}) collective-permute-start(bf16[256,640]{1,0:T(8,128)(2,1)} %rest_1_.3), channel_id=1, source_target_pairs={{0,128},{8,136},{16,144},{24,152},{32,160},{40,168},{48,176},{56,1... | collective-permute-start | bytes 983048 | tf_op jit(solution)/shard_map/ppermute | solution.py:424
  40.6 37.9 %collective-permute-start.13 = (bf16[256,640]{1,0:T(8,128)(2,1)}, bf16[256,640]{1,0:T(8,128)(2,1)S(1)}, u32[]{:S(2)}, u32[]{:S(2)}) collective-permute-start(bf16[256,640]{1,0:T(8,128)(2,1)} %rest_1_.3), channel_id=1, source_target_pairs={{64,128},{128,64},{72,136},{136,72},{80,144},{144,80},{88,152},{15... | collective-permute-start | bytes 983048 | tf_op jit(solution)/shard_map/ppermute | solution.py:424
  51.1 27.4 %collective-permute-start.14 = (bf16[256,640]{1,0:T(8,128)(2,1)}, bf16[256,640]{1,0:T(8,128)(2,1)}, u32[]{:S(2)}, u32[]{:S(2)}) collective-permute-start(bf16[256,640]{1,0:T(8,128)(2,1)} %rest_1_.3), channel_id=1, source_target_pairs={{0,64},{8,72},{16,80},{24,88},{32,96},{40,104},{48,112},{56,120},{... | collective-permute-start | bytes 983048 | tf_op jit(solution)/shard_map/ppermute | solution.py:424
  51.2 28.0 %collective-permute-start.15 = (bf16[256,640]{1,0:T(8,128)(2,1)}, bf16[256,640]{1,0:T(8,128)(2,1)}, u32[]{:S(2)}, u32[]{:S(2)}) collective-permute-start(bf16[256,640]{1,0:T(8,128)(2,1)} %rest_1_.3), channel_id=1, source_target_pairs={{0,32},{8,40},{16,48},{24,56},{32,0},{40,8},{48,16},{56,24},{64,96... | collective-permute-start | bytes 983048 | tf_op jit(solution)/shard_map/ppermute | solution.py:424
  51.5 29.0 %collective-permute-start.16 = (bf16[256,640]{1,0:T(8,128)(2,1)}, bf16[256,640]{1,0:T(8,128)(2,1)}, u32[]{:S(2)}, u32[]{:S(2)}) collective-permute-start(bf16[256,640]{1,0:T(8,128)(2,1)} %rest_1_.3), channel_id=1, source_target_pairs={{32,64},{64,32},{40,72},{72,40},{48,80},{80,48},{56,88},{88,56},{1... | collective-permute-start | bytes 983048 | tf_op jit(solution)/shard_map/ppermute | solution.py:424
  56.4 25.6 %collective-permute-start.17 = (bf16[256,640]{1,0:T(8,128)(2,1)}, bf16[256,640]{1,0:T(8,128)(2,1)S(1)}, u32[]{:S(2)}, u32[]{:S(2)}) collective-permute-start(bf16[256,640]{1,0:T(8,128)(2,1)} %rest_1_.3), channel_id=1, source_target_pairs={{0,16},{8,24},{16,0},{24,8},{32,48},{40,56},{48,32},{56,40},{64,80... | collective-permute-start | bytes 983048 | tf_op jit(solution)/shard_map/ppermute | solution.py:424
  78.5 10.7 %collective-permute-start.18 = (bf16[256,640]{1,0:T(8,128)(2,1)}, bf16[256,640]{1,0:T(8,128)(2,1)S(1)}, u32[]{:S(2)}, u32[]{:S(2)}) collective-permute-start(bf16[256,640]{1,0:T(8,128)(2,1)} %rest_1_.3), channel_id=1, source_target_pairs={{0,8},{8,0},{16,24},{24,16},{32,40},{40,32},{48,56},{56,48},{64,72... | collective-permute-start | bytes 983048 | tf_op jit(solution)/shard_map/ppermute | solution.py:424
  78.5 11.9 %collective-permute-start.19 = (bf16[256,640]{1,0:T(8,128)(2,1)}, bf16[256,640]{1,0:T(8,128)(2,1)S(1)}, u32[]{:S(2)}, u32[]{:S(2)}) collective-permute-start(bf16[256,640]{1,0:T(8,128)(2,1)} %rest_1_.3), channel_id=1, source_target_pairs={{8,16},{16,8},{24,32},{32,24},{40,48},{48,40},{56,64},{64,56},{72,... | collective-permute-start | bytes 983048 | tf_op jit(solution)/shard_map/ppermute | solution.py:424
  79.2 12.6 %collective-permute-start.8 = (bf16[256,640]{1,0:T(8,128)(2,1)S(1)}, bf16[256,640]{1,0:T(8,128)(2,1)S(1)}, u32[]{:S(2)}, u32[]{:S(2)}) collective-permute-start(bf16[256,640]{1,0:T(8,128)(2,1)S(1)} %collective-permute-done.rest_3_.rest_4_), channel_id=1, source_target_pairs={{224,128},{232,136},{240,144},{248,152},{0,96},{8,104},{16,112},{2... | collective-permute-start | bytes 983048 | tf_op jit(solution)/shard_map/ppermute | solution.py:424
  80.5 12.8 %copy-start.2 = (bf16[256,640]{1,0:T(8,128)(2,1)S(1)}, bf16[256,640]{1,0:T(8,128)(2,1)}, u32[]{:S(2)}) copy-start(bf16[256,640]{1,0:T(8,128)(2,1)} %rest_0_.4) | copy-start | bytes 983044
  80.5 15.1 %collective-permute-start.9 = (bf16[256,640]{1,0:T(8,128)(2,1)S(1)}, bf16[256,640]{1,0:T(8,128)(2,1)S(1)}, u32[]{:S(2)}, u32[]{:S(2)}) collective-permute-start(bf16[256,640]{1,0:T(8,128)(2,1)S(1)} %collective-permute-done.1.rest_4_.rest_5_), channel_id=1, source_target_pairs={{176,128},{184,136},{64,112},{72,120},{177,129},{185,137},{65,113}... | collective-permute-start | bytes 983048 | tf_op jit(solution)/shard_map/ppermute | solution.py:424
  82.0 11.3 %copy-start.8 = (bf16[256,640]{1,0:T(8,128)(2,1)}, bf16[256,640]{1,0:T(8,128)(2,1)S(1)}, u32[]{:S(2)}) copy-start(bf16[256,640]{1,0:T(8,128)(2,1)S(1)} %collective-permute-done.17.rest_21_.rest_22_) | copy-start | bytes 983044
  82.0 33.4 %collective-permute-start.11 = (bf16[256,640]{1,0:T(8,128)(2,1)S(1)}, bf16[256,640]{1,0:T(8,128)(2,1)S(1)}, u32[]{:S(2)}, u32[]{:S(2)}) collective-permute-start(bf16[256,640]{1,0:T(8,128)(2,1)S(1)} %broadcast_select_fusion.3), channel_id=1, source_target_pairs={{48,32},{56,40},{80,64},{88,72},{112,96},{120,104},{176,160},{184,... | collective-permute-start | bytes 983048 | tf_op jit(solution)/shard_map/ppermute | solution.py:424
  89.1 26.2 %collective-permute-start.10 = (bf16[256,640]{1,0:T(8,128)(2,1)S(1)}, bf16[256,640]{1,0:T(8,128)(2,1)S(1)}, u32[]{:S(2)}, u32[]{:S(2)}) collective-permute-start(bf16[256,640]{1,0:T(8,128)(2,1)S(1)} %collective-permute-done.1.rest_4_.rest_5_), channel_id=1, source_target_pairs={{184,128},{64,120},{185,129},{65,121},{186,130},{66,122},{187,131}... | collective-permute-start | bytes 983048 | tf_op jit(solution)/shard_map/ppermute | solution.py:424
  90.4 40.6 %copy-start.10 = (bf16[256,640]{1,0:T(8,128)(2,1)}, bf16[256,640]{1,0:T(8,128)(2,1)S(1)}, u32[]{:S(2)}) copy-start(bf16[256,640]{1,0:T(8,128)(2,1)S(1)} %collective-permute-done.19.rest_23_.rest_24_) | copy-start | bytes 983044
  90.4 29.6 %collective-permute-start.20 = (bf16[256,640]{1,0:T(8,128)(2,1)S(1)}, bf16[256,640]{1,0:T(8,128)(2,1)S(1)}, u32[]{:S(2)}, u32[]{:S(2)}) collective-permute-start(bf16[256,640]{1,0:T(8,128)(2,1)S(1)} %collective-permute-done.12.rest_16_.rest_17_), channel_id=1, source_target_pairs={{224,128},{232,136},{240,144},{248,152},{0,96},{8,104},{16,112},{2... | collective-permute-start | bytes 983048 | tf_op jit(solution)/shard_map/ppermute | solution.py:424
  91.8 28.4 %collective-permute-start.21 = (bf16[256,640]{1,0:T(8,128)(2,1)S(1)}, bf16[256,640]{1,0:T(8,128)(2,1)S(1)}, u32[]{:S(2)}, u32[]{:S(2)}) collective-permute-start(bf16[256,640]{1,0:T(8,128)(2,1)S(1)} %collective-permute-done.13.rest_17_.rest_18_), channel_id=1, source_target_pairs={{176,128},{184,136},{64,112},{72,120},{177,129},{185,137},{65,113}... | collective-permute-start | bytes 983048 | tf_op jit(solution)/shard_map/ppermute | solution.py:424
  95.6 26.7 %collective-permute-start.22 = (bf16[256,640]{1,0:T(8,128)(2,1)S(1)}, bf16[256,640]{1,0:T(8,128)(2,1)S(1)}, u32[]{:S(2)}, u32[]{:S(2)}) collective-permute-start(bf16[256,640]{1,0:T(8,128)(2,1)S(1)} %collective-permute-done.13.rest_17_.rest_18_), channel_id=1, source_target_pairs={{184,128},{64,120},{185,129},{65,121},{186,130},{66,122},{187,131}... | collective-permute-start | bytes 983048 | tf_op jit(solution)/shard_map/ppermute | solution.py:424
  97.6 34.1 %copy-start = (bf16[256,640]{1,0:T(8,128)(2,1)S(1)}, bf16[256,640]{1,0:T(8,128)(2,1)}, u32[]{:S(2)}) copy-start(bf16[256,640]{1,0:T(8,128)(2,1)} %rest_0_.5) | copy-start | bytes 983044
  97.6 34.1 %copy-start.1 = (bf16[256,640]{1,0:T(8,128)(2,1)S(1)}, bf16[256,640]{1,0:T(8,128)(2,1)}, u32[]{:S(2)}) copy-start(bf16[256,640]{1,0:T(8,128)(2,1)} %rest_1_.3) | copy-start | bytes 983044
  97.6 34.1 %copy-start.4 = (bf16[256,640]{1,0:T(8,128)(2,1)S(1)}, bf16[256,640]{1,0:T(8,128)(2,1)}, u32[]{:S(2)}) copy-start(bf16[256,640]{1,0:T(8,128)(2,1)} %rest_3_.2) | copy-start | bytes 983044
  115.4 30.6 %collective-permute-start.27 = (bf16[272,640]{1,0:T(8,128)(2,1)S(1)}, bf16[272,640]{1,0:T(8,128)(2,1)S(1)}, u32[]{:S(2)}, u32[]{:S(2)}) collective-permute-start(bf16[272,640]{1,0:T(8,128)(2,1)S(1)} %fusion.1.rest_0_.rest_2_), channel_id=1, source_target_pairs={{0,128},{8,136},{16,144},{24,152},{32,160},{40,168},{48,176},{56,1... | collective-permute-start | bytes 1044488 | tf_op jit(solution)/shard_map/ppermute | solution.py:424
  115.4 38.6 %collective-permute-start.28 = (bf16[272,640]{1,0:T(8,128)(2,1)S(1)}, bf16[272,640]{1,0:T(8,128)(2,1)S(1)}, u32[]{:S(2)}, u32[]{:S(2)}) collective-permute-start(bf16[272,640]{1,0:T(8,128)(2,1)S(1)} %fusion.1.rest_0_.rest_2_), channel_id=1, source_target_pairs={{64,128},{128,64},{72,136},{136,72},{80,144},{144,80},{88,152},{15... | collective-permute-start | bytes 1044488 | tf_op jit(solution)/shard_map/ppermute | solution.py:424
  120.1 34.2 %collective-permute-start.30 = (bf16[272,640]{1,0:T(8,128)(2,1)S(1)}, bf16[272,640]{1,0:T(8,128)(2,1)S(1)}, u32[]{:S(2)}, u32[]{:S(2)}) collective-permute-start(bf16[272,640]{1,0:T(8,128)(2,1)S(1)} %fusion.1.rest_0_.rest_2_), channel_id=1, source_target_pairs={{0,32},{8,40},{16,48},{24,56},{32,0},{40,8},{48,16},{56,24},{64,96... | collective-permute-start | bytes 1044488 | tf_op jit(solution)/shard_map/ppermute | solution.py:424
  120.2 37.7 %collective-permute-start.31 = (bf16[272,640]{1,0:T(8,128)(2,1)S(1)}, bf16[272,640]{1,0:T(8,128)(2,1)S(1)}, u32[]{:S(2)}, u32[]{:S(2)}) collective-permute-start(bf16[272,640]{1,0:T(8,128)(2,1)S(1)} %fusion.1.rest_0_.rest_2_), channel_id=1, source_target_pairs={{32,64},{64,32},{40,72},{72,40},{48,80},{80,48},{56,88},{88,56},{1... | collective-permute-start | bytes 1044488 | tf_op jit(solution)/shard_map/ppermute | solution.py:424
  122.3 8.7 %collective-permute-start.23 = (bf16[256,640]{1,0:T(8,128)(2,1)S(1)}, bf16[256,640]{1,0:T(8,128)(2,1)S(1)}, u32[]{:S(2)}, u32[]{:S(2)}) collective-permute-start(bf16[256,640]{1,0:T(8,128)(2,1)S(1)} %broadcast_select_fusion.2), channel_id=1, source_target_pairs={{48,32},{56,40},{80,64},{88,72},{112,96},{120,104},{176,160},{184,... | collective-permute-start | bytes 983048 | tf_op jit(solution)/shard_map/ppermute | solution.py:424
  139.9 20.0 %copy-start.3 = (f32[256,640]{1,0:T(8,128)S(1)}, f32[256,640]{1,0:T(8,128)}, u32[]{:S(2)}) copy-start(f32[256,640]{1,0:T(8,128)} %get-tuple-element.20.rest_1_.rest_2_) | copy-start | bytes 1966084
  139.9 1.2 collective-permute-start.24
  141.2 3.6 %collective-permute-start.25 = (f32[2,128]{1,0:T(2,128)S(1)}, f32[2,128]{1,0:T(2,128)S(1)}, u32[]{:S(2)}, u32[]{:S(2)}) collective-permute-start(f32[2,128]{1,0:T(2,128)S(1)} %add.49), channel_id=1, source_target_pairs={{0,2},{1,3},{2,0},{3,1},{4,6},{5,7},{6,4},{7,5},{8,10},{9,11},{10,... | collective-permute-start | bytes 3080 | tf_op jit(solution)/shard_map/ppermute | solution.py:491
  144.8 15.2 %copy-start.5 = (bf16[256,640]{1,0:T(8,128)(2,1)S(1)}, bf16[256,640]{1,0:T(8,128)(2,1)}, u32[]{:S(2)}) copy-start(bf16[256,640]{1,0:T(8,128)(2,1)} %rest_2_.3) | copy-start | bytes 983044
  144.8 13.8 %collective-permute-start.26 = (f32[2,128]{1,0:T(2,128)S(1)}, f32[2,128]{1,0:T(2,128)S(1)}, u32[]{:S(2)}, u32[]{:S(2)}) collective-permute-start(f32[2,128]{1,0:T(2,128)S(1)} %add.50), channel_id=1, source_target_pairs={{0,4},{1,5},{2,6},{3,7},{4,0},{5,1},{6,2},{7,3},{8,12},{9,13},{10,... | collective-permute-start | bytes 3080 | tf_op jit(solution)/shard_map/ppermute | solution.py:491
  146.0 15.7 %collective-permute-start.29 = (bf16[272,640]{1,0:T(8,128)(2,1)S(1)}, bf16[272,640]{1,0:T(8,128)(2,1)S(1)}, u32[]{:S(2)}, u32[]{:S(2)}) collective-permute-start(bf16[272,640]{1,0:T(8,128)(2,1)S(1)} %fusion.1.rest_0_.rest_2_), channel_id=1, source_target_pairs={{0,64},{8,72},{16,80},{24,88},{32,96},{40,104},{48,112},{56,120},{... | collective-permute-start | bytes 1044488 | tf_op jit(solution)/shard_map/ppermute | solution.py:424
  154.0 12.6 %collective-permute-start.32 = (bf16[272,640]{1,0:T(8,128)(2,1)S(1)}, bf16[272,640]{1,0:T(8,128)(2,1)S(1)}, u32[]{:S(2)}, u32[]{:S(2)}) collective-permute-start(bf16[272,640]{1,0:T(8,128)(2,1)S(1)} %fusion.1.rest_0_.rest_2_), channel_id=1, source_target_pairs={{0,16},{8,24},{16,0},{24,8},{32,48},{40,56},{48,32},{56,40},{64,80... | collective-permute-start | bytes 1044488 | tf_op jit(solution)/shard_map/ppermute | solution.py:424
  154.3 17.8 %collective-permute-start.33 = (bf16[272,640]{1,0:T(8,128)(2,1)S(1)}, bf16[272,640]{1,0:T(8,128)(2,1)S(1)}, u32[]{:S(2)}, u32[]{:S(2)}) collective-permute-start(bf16[272,640]{1,0:T(8,128)(2,1)S(1)} %fusion.1.rest_0_.rest_2_), channel_id=1, source_target_pairs={{0,8},{8,0},{16,24},{24,16},{32,40},{40,32},{48,56},{56,48},{64,72... | collective-permute-start | bytes 1044488 | tf_op jit(solution)/shard_map/ppermute | solution.py:424
  157.9 17.1 %collective-permute-start.34 = (bf16[272,640]{1,0:T(8,128)(2,1)S(1)}, bf16[272,640]{1,0:T(8,128)(2,1)S(1)}, u32[]{:S(2)}, u32[]{:S(2)}) collective-permute-start(bf16[272,640]{1,0:T(8,128)(2,1)S(1)} %fusion.1.rest_0_.rest_2_), channel_id=1, source_target_pairs={{8,16},{16,8},{24,32},{32,24},{40,48},{48,40},{56,64},{64,56},{72,... | collective-permute-start | bytes 1044488 | tf_op jit(solution)/shard_map/ppermute | solution.py:424
  158.6 17.0 %collective-permute-start.35 = (bf16[272,640]{1,0:T(8,128)(2,1)S(1)}, bf16[272,640]{1,0:T(8,128)(2,1)S(1)}, u32[]{:S(2)}, u32[]{:S(2)}) collective-permute-start(bf16[272,640]{1,0:T(8,128)(2,1)S(1)} %collective-permute-done.27.rest_1_.rest_3_), channel_id=1, source_target_pairs={{224,128},{232,136},{240,144},{248,152},{0,96},{8,104},{16,112},{2... | collective-permute-start | bytes 1044488 | tf_op jit(solution)/shard_map/ppermute | solution.py:424
  161.7 17.8 %collective-permute-start.36 = (bf16[272,640]{1,0:T(8,128)(2,1)S(1)}, bf16[272,640]{1,0:T(8,128)(2,1)S(1)}, u32[]{:S(2)}, u32[]{:S(2)}) collective-permute-start(bf16[272,640]{1,0:T(8,128)(2,1)S(1)} %collective-permute-done.28.rest_2_.rest_4_), channel_id=1, source_target_pairs={{176,128},{184,136},{64,112},{72,120},{177,129},{185,137},{65,113}... | collective-permute-start | bytes 1044488 | tf_op jit(solution)/shard_map/ppermute | solution.py:424
  166.5 29.8 %collective-permute-start.37 = (bf16[272,640]{1,0:T(8,128)(2,1)S(1)}, bf16[272,640]{1,0:T(8,128)(2,1)S(1)}, u32[]{:S(2)}, u32[]{:S(2)}) collective-permute-start(bf16[272,640]{1,0:T(8,128)(2,1)S(1)} %collective-permute-done.28.rest_2_.rest_4_), channel_id=1, source_target_pairs={{184,128},{64,120},{185,129},{65,121},{186,130},{66,122},{187,131}... | collective-permute-start | bytes 1044488 | tf_op jit(solution)/shard_map/ppermute | solution.py:424
  172.1 27.6 %collective-permute-start.38 = (bf16[272,640]{1,0:T(8,128)(2,1)S(1)}, bf16[272,640]{1,0:T(8,128)(2,1)S(1)}, u32[]{:S(2)}, u32[]{:S(2)}) collective-permute-start(bf16[272,640]{1,0:T(8,128)(2,1)S(1)} %broadcast_select_fusion.1), channel_id=1, source_target_pairs={{48,32},{56,40},{80,64},{88,72},{112,96},{120,104},{176,160},{184,... | collective-permute-start | bytes 1044488 | tf_op jit(solution)/shard_map/ppermute | solution.py:424
  175.0 24.8 %collective-permute-start.42 = (bf16[272,640]{1,0:T(8,128)(2,1)}, bf16[272,640]{1,0:T(8,128)(2,1)S(1)}, u32[]{:S(2)}, u32[]{:S(2)}) collective-permute-start(bf16[272,640]{1,0:T(8,128)(2,1)} %upstream.1.rest_1_.rest_15_), channel_id=1, source_target_pairs={{0,32},{8,40},{16,48},{24,56},{32,0},{40,8},{48,16},{56,24},{64,96... | collective-permute-start | bytes 1044488 | tf_op jit(solution)/shard_map/ppermute | solution.py:424
  175.5 24.3 %collective-permute-start.43 = (bf16[272,640]{1,0:T(8,128)(2,1)}, bf16[272,640]{1,0:T(8,128)(2,1)S(1)}, u32[]{:S(2)}, u32[]{:S(2)}) collective-permute-start(bf16[272,640]{1,0:T(8,128)(2,1)} %upstream.1.rest_1_.rest_15_), channel_id=1, source_target_pairs={{32,64},{64,32},{40,72},{72,40},{48,80},{80,48},{56,88},{88,56},{1... | collective-permute-start | bytes 1044488 | tf_op jit(solution)/shard_map/ppermute | solution.py:424
  179.5 21.1 %collective-permute-start.39 = (bf16[272,640]{1,0:T(8,128)(2,1)}, bf16[272,640]{1,0:T(8,128)(2,1)S(1)}, u32[]{:S(2)}, u32[]{:S(2)}) collective-permute-start(bf16[272,640]{1,0:T(8,128)(2,1)} %upstream.1.rest_1_.rest_15_), channel_id=1, source_target_pairs={{0,128},{8,136},{16,144},{24,152},{32,160},{40,168},{48,176},{56,1... | collective-permute-start | bytes 1044488 | tf_op jit(solution)/shard_map/ppermute | solution.py:424
  196.3 28.5 %collective-permute-start.40 = (bf16[272,640]{1,0:T(8,128)(2,1)}, bf16[272,640]{1,0:T(8,128)(2,1)S(1)}, u32[]{:S(2)}, u32[]{:S(2)}) collective-permute-start(bf16[272,640]{1,0:T(8,128)(2,1)} %upstream.1.rest_1_.rest_15_), channel_id=1, source_target_pairs={{64,128},{128,64},{72,136},{136,72},{80,144},{144,80},{88,152},{15... | collective-permute-start | bytes 1044488 | tf_op jit(solution)/shard_map/ppermute | solution.py:424
  199.7 26.4 %collective-permute-start.41 = (bf16[272,640]{1,0:T(8,128)(2,1)}, bf16[272,640]{1,0:T(8,128)(2,1)S(1)}, u32[]{:S(2)}, u32[]{:S(2)}) collective-permute-start(bf16[272,640]{1,0:T(8,128)(2,1)} %upstream.1.rest_1_.rest_15_), channel_id=1, source_target_pairs={{0,64},{8,72},{16,80},{24,88},{32,96},{40,104},{48,112},{56,120},{... | collective-permute-start | bytes 1044488 | tf_op jit(solution)/shard_map/ppermute | solution.py:424
  199.8 27.6 %collective-permute-start.44 = (bf16[272,640]{1,0:T(8,128)(2,1)}, bf16[272,640]{1,0:T(8,128)(2,1)S(1)}, u32[]{:S(2)}, u32[]{:S(2)}) collective-permute-start(bf16[272,640]{1,0:T(8,128)(2,1)} %upstream.1.rest_1_.rest_15_), channel_id=1, source_target_pairs={{0,16},{8,24},{16,0},{24,8},{32,48},{40,56},{48,32},{56,40},{64,80... | collective-permute-start | bytes 1044488 | tf_op jit(solution)/shard_map/ppermute | solution.py:424
  199.9 28.8 %collective-permute-start.45 = (bf16[272,640]{1,0:T(8,128)(2,1)}, bf16[272,640]{1,0:T(8,128)(2,1)S(1)}, u32[]{:S(2)}, u32[]{:S(2)}) collective-permute-start(bf16[272,640]{1,0:T(8,128)(2,1)} %upstream.1.rest_1_.rest_15_), channel_id=1, source_target_pairs={{0,8},{8,0},{16,24},{24,16},{32,40},{40,32},{48,56},{56,48},{64,72... | collective-permute-start | bytes 1044488 | tf_op jit(solution)/shard_map/ppermute | solution.py:424
  200.6 38.7 %collective-permute-start.46 = (bf16[272,640]{1,0:T(8,128)(2,1)}, bf16[272,640]{1,0:T(8,128)(2,1)S(1)}, u32[]{:S(2)}, u32[]{:S(2)}) collective-permute-start(bf16[272,640]{1,0:T(8,128)(2,1)} %upstream.1.rest_1_.rest_15_), channel_id=1, source_target_pairs={{8,16},{16,8},{24,32},{32,24},{40,48},{48,40},{56,64},{64,56},{72,... | collective-permute-start | bytes 1044488 | tf_op jit(solution)/shard_map/ppermute | solution.py:424
  224.8 13.6 %copy-start.15 = (bf16[272,640]{1,0:T(8,128)(2,1)}, bf16[272,640]{1,0:T(8,128)(2,1)S(1)}, u32[]{:S(2)}) copy-start(bf16[272,640]{1,0:T(8,128)(2,1)S(1)} %collective-permute-done.40.rest_17_) | copy-start | bytes 1044484
  224.8 14.5 %collective-permute-start.47 = (bf16[272,640]{1,0:T(8,128)(2,1)S(1)}, bf16[272,640]{1,0:T(8,128)(2,1)S(1)}, u32[]{:S(2)}, u32[]{:S(2)}) collective-permute-start(bf16[272,640]{1,0:T(8,128)(2,1)S(1)} %collective-permute-done.39.rest_16_), channel_id=1, source_target_pairs={{224,128},{232,136},{240,144},{248,152},{0,96},{8,104},{16,112},{2... | collective-permute-start | bytes 1044488 | tf_op jit(solution)/shard_map/ppermute | solution.py:424
  226.1 12.4 %copy-start.16 = (bf16[272,640]{1,0:T(8,128)(2,1)}, bf16[272,640]{1,0:T(8,128)(2,1)S(1)}, u32[]{:S(2)}) copy-start(bf16[272,640]{1,0:T(8,128)(2,1)S(1)} %collective-permute-done.41.rest_18_) | copy-start | bytes 1044484
  226.1 15.4 %collective-permute-start.48 = (bf16[272,640]{1,0:T(8,128)(2,1)S(1)}, bf16[272,640]{1,0:T(8,128)(2,1)S(1)}, u32[]{:S(2)}, u32[]{:S(2)}) collective-permute-start(bf16[272,640]{1,0:T(8,128)(2,1)S(1)} %collective-permute-done.40.rest_17_), channel_id=1, source_target_pairs={{176,128},{184,136},{64,112},{72,120},{177,129},{185,137},{65,113}... | collective-permute-start | bytes 1044488 | tf_op jit(solution)/shard_map/ppermute | solution.py:424
  227.4 26.3 %collective-permute-start.49 = (bf16[272,640]{1,0:T(8,128)(2,1)S(1)}, bf16[272,640]{1,0:T(8,128)(2,1)S(1)}, u32[]{:S(2)}, u32[]{:S(2)}) collective-permute-start(bf16[272,640]{1,0:T(8,128)(2,1)S(1)} %collective-permute-done.40.rest_17_), channel_id=1, source_target_pairs={{184,128},{64,120},{185,129},{65,121},{186,130},{66,122},{187,131}... | collective-permute-start | bytes 1044488 | tf_op jit(solution)/shard_map/ppermute | solution.py:424
  228.8 25.0 %collective-permute-start.50 = (bf16[272,640]{1,0:T(8,128)(2,1)S(1)}, bf16[272,640]{1,0:T(8,128)(2,1)S(1)}, u32[]{:S(2)}, u32[]{:S(2)}) collective-permute-start(bf16[272,640]{1,0:T(8,128)(2,1)S(1)} %broadcast_select_fusion), channel_id=1, source_target_pairs={{48,32},{56,40},{80,64},{88,72},{112,96},{120,104},{176,160},{184,... | collective-permute-start | bytes 1044488 | tf_op jit(solution)/shard_map/ppermute | solution.py:424
  239.3 14.4 %copy-start.19 = (bf16[272,640]{1,0:T(8,128)(2,1)}, bf16[272,640]{1,0:T(8,128)(2,1)S(1)}, u32[]{:S(2)}) copy-start(bf16[272,640]{1,0:T(8,128)(2,1)S(1)} %collective-permute-done.46.rest_23_) | copy-start | bytes 1044484
  239.3 14.4 %copy-start.20 = (bf16[272,640]{1,0:T(8,128)(2,1)}, bf16[272,640]{1,0:T(8,128)(2,1)S(1)}, u32[]{:S(2)}) copy-start(bf16[272,640]{1,0:T(8,128)(2,1)S(1)} %collective-permute-done.47.rest_24_) | copy-start | bytes 1044484
  241.5 12.2 %copy-start.21 = (bf16[272,640]{1,0:T(8,128)(2,1)}, bf16[272,640]{1,0:T(8,128)(2,1)S(1)}, u32[]{:S(2)}) copy-start(bf16[272,640]{1,0:T(8,128)(2,1)S(1)} %collective-permute-done.48.rest_25_) | copy-start | bytes 1044484
  (13 other events, 53.2 us)
where the time goes:
time: 269 us; the launch traced here: 266 us
  waiting for transfers between devices  148 us (55%)
  starting transfers between devices  79.1 us (29%)
  Pallas kernels  29.9 us (11%)
  local copies, waits for them, and re-layouts  4.85 us (2%)
    ppermute x48, waiting for transfers between devices, spread(): held[name] = lax.ppermute(held[sent], 'frame', pairs)  143 us
    ppermute x48, starting transfers between devices, spread(): held[name] = lax.ppermute(held[sent], 'frame', pairs)  77.8 us
    pallas_call x1, Pallas kernels, step(): pl.pallas_call(functools.partial(key_kernel, classes=classes, scale=scale...  10.9 us
    pallas_call x1, Pallas kernels, step(): pl.pallas_call(functools.partial(query_kernel, classes=classes, list_len=...  8.37 us
    pallas_call x1, Pallas kernels, step(): pl.pallas_call(functools.partial(forward_kernel, classes=classes, list_le...  8.16 us
  transfers between devices with their start and end apart: 51, of which 18 were waited for; matrix products, arithmetic and copies ran while one was open for 2% of the time, Pallas kernels for 7%

commit v1 on v0

--- a/solution.py
+++ b/solution.py
@@ -15,9 +15,10 @@
 TAIL = 16
 
 kl_weight = 1.0
-
-
-WIDE = 2
+LOG2E = 1.4426950408889634
+
+
+WIDE = 4
 
 NT = (((1,), (1,)), ((), ()))
 NN = (((1,), (0,)), ((), ()))
@@ -75,8 +76,8 @@
     )
 
 
-def block_probs(query, key_block, counts, block, list_len, scale):
-    scores = matmul(query, key_block, NT) * scale
+def block_exps(query, key_block, counts, block, list_len, scale):
+    scores = matmul(query, key_block, NT)
     lane = lax.broadcasted_iota(jnp.int32, (BLK, BLK), 1)
     scores = jnp.concatenate(
         [
@@ -87,10 +88,11 @@
         ],
         axis=1,
     )
-    highest = jnp.max(scores, axis=-1, keepdims=True)
-    expd = jnp.exp(scores - highest)
+    factor = scale * LOG2E
+    highest = jnp.max(scores, axis=-1, keepdims=True) * factor
+    expd = jnp.exp2(scores * factor - highest)
     total = jnp.sum(expd, axis=-1, keepdims=True)
-    return expd * (1.0 / total), highest + jnp.log(total)
+    return expd, 1.0 / total, highest + jnp.log2(total)
 
 
 def forward_kernel(slots, counts, used, *rest, classes, list_len, scale):
@@ -121,11 +123,13 @@
         for head in range(cols // HD):
             hs = slice(head * HD, (head + 1) * HD)
             keys = listed(key_pool, slots, block, list_len, hs)
-            probs, log_sum = block_probs(queries[span, hs], keys, counts, block, list_len, scale)
+            expd, share, log_sum = block_exps(
+                queries[span, hs], keys, counts, block, list_len, scale
+            )
             if block == 0 and head == 0:
                 fetch(value_refs, value_pool, value_sems, used, False)
             values = listed(value_pool, slots, block, list_len, hs)
-            out = matmul(probs.astype(jnp.bfloat16), values, NN)
+            out = matmul(expd.astype(jnp.bfloat16), values, NN) * share
             attn[span, hs] = out
             diff = out - ref_velocity[span, hs].astype(jnp.float32)
             total = total + jnp.sum(diff * diff, axis=1, keepdims=True)
@@ -198,15 +202,17 @@
         for head in range(cols // HD):
             hs = slice(head * HD, (head + 1) * HD)
             keys = listed(key_pool, slots, block, list_len, hs)
-            probs, _ = block_probs(queries[span, hs], keys, counts, block, list_len, scale)
+            expd, share, _ = block_exps(queries[span, hs], keys, counts, block, list_len, scale)
             if block == 0 and head == 0:
                 fetch(value_refs, value_pool, value_sems, used, False)
             values = listed(value_pool, slots, block, list_len, hs)
             upstream = grad[span, hs]
             delta = jnp.sum(upstream.astype(jnp.float32) * attn[span, hs], axis=1, keepdims=True)
             grad_probs = matmul(upstream, values, NT)
-            grad_scores = (probs * (grad_probs - delta)).astype(jnp.bfloat16)
-            grad_queries[span, hs] = (matmul(grad_scores, keys, NN) * scale).astype(jnp.bfloat16)
+            grad_scores = (expd * (grad_probs - delta)).astype(jnp.bfloat16)
+            grad_queries[span, hs] = (matmul(grad_scores, keys, NN) * (share * scale)).astype(
+                jnp.bfloat16
+            )
 
 
 def naming_kernel(own, valid, *rest, classes, list_len, blocks, rows):
@@ -277,13 +283,12 @@
     bring((keys_in, values_in), (keys, values), sems, 0, False)
     fetch(query_refs, query_pool, query_sems, used, False)
     fetch(grad_refs, grad_pool, grad_sems, used, False)
-    row_in_block = lax.broadcasted_iota(jnp.int32, (BLK, WIDE * BLK), 0)
+    row_in_block = lax.broadcasted_iota(jnp.int32, (BLK, cols), 0)
     for block in range(blocks):
         key_rows = slice(block * BLK, (block + 1) * BLK)
-        valid = row_in_block < counts[block]
         length = lengths[block]
 
-        def step(chunk, carry, block=block, key_rows=key_rows, valid=valid, length=length):
+        def step(chunk, carry, block=block, key_rows=key_rows, length=length):
             places = []
             for lane in range(WIDE):
                 index = chunk * WIDE + lane
@@ -310,8 +315,8 @@
                     deltas.append(stats[3:4] + stats[4:5] + stats[5:6])
                 log_sum = jnp.concatenate(sums, axis=1)
                 delta = jnp.concatenate(deltas, axis=1)
-                scores = matmul(keys[key_rows, hs], query, NT) * scale - log_sum
-                probs = jnp.exp(jnp.where(valid, scores, -1e30))
+                scores = matmul(keys[key_rows, hs], query, NT)
+                probs = jnp.exp2(scores * (scale * LOG2E) - log_sum)
                 grad_probs = matmul(values[key_rows, hs], upstream, NT)
                 grad_scores = (probs * (grad_probs - delta)).astype(jnp.bfloat16)
                 acc_v[key_rows, hs] += matmul(probs.astype(jnp.bfloat16), upstream, NN)
@@ -319,8 +324,11 @@
             return carry
 
         lax.fori_loop(0, (length + WIDE - 1) // WIDE, step, 0)
-        grad_keys[key_rows, :] = (acc_k[key_rows, :] * scale).astype(jnp.bfloat16)
-        grad_values[key_rows, :] = acc_v[key_rows, :].astype(jnp.bfloat16)
+        valid = row_in_block < counts[block]
+        grad_keys[key_rows, :] = jnp.where(valid, acc_k[key_rows, :] * scale, 0.0).astype(
+            jnp.bfloat16
+        )
+        grad_values[key_rows, :] = jnp.where(valid, acc_v[key_rows, :], 0.0).astype(jnp.bfloat16)
 
 
 SMEM = pl.BlockSpec(memory_space=pltpu.SMEM)
@@ -470,7 +478,7 @@
         return pltpu.SemaphoreType.DMA((count,))
 
     pools = [shard(height=classes * rows)] * 2
-    params = pltpu.CompilerParams(vmem_limit_bytes=48 << 20)
+    params = pltpu.CompilerParams(vmem_limit_bytes=20 << 20)
     attn, lse, squares = pl.pallas_call(
         functools.partial(forward_kernel, classes=classes, list_len=list_len, scale=scale),
         out_shape=(

time: 269 us -> 263 us (0.978)
  Pallas kernels: 29.9 us -> 24.3 us
  waiting for transfers between devices: 148 us -> 152 us
  local copies, waits for them, and re-layouts: 4.85 us -> 2.03 us
    ppermute x48, waiting for transfers between devices: 143 us -> 147 us  [spread(): held[name] = lax.ppermute(held[sent], 'frame', pairs)]
    unnamed x54 -> x16, local copies, waits for them, and re-layouts: 3.71 us -> 0.89 us
    ppermute x48, starting transfers between devices: 77.8 us -> 75.1 us  [spread(): held[name] = lax.ppermute(held[sent], 'frame', pairs)]
  transfers between devices with their start and end apart: 51 -> 51, of which waited for: 18 -> 19; matrix products, arithmetic and copies ran while one was open for 2% -> 1% of each run, Pallas kernels for 7% -> 6%
where the time goes in v1:
time: 263 us; the launch traced here: 259 us
  waiting for transfers between devices  152 us (58%)
  starting transfers between devices  77.8 us (30%)
  Pallas kernels  24.3 us (9%)
    ppermute x48, waiting for transfers between devices, spread(): held[name] = lax.ppermute(held[sent], 'frame', pairs)  147 us
    ppermute x48, starting transfers between devices, spread(): held[name] = lax.ppermute(held[sent], 'frame', pairs)  75.1 us
    pallas_call x1, Pallas kernels, step(): pl.pallas_call(functools.partial(key_kernel, classes=classes, scale=scale...  8.73 us
    pallas_call x1, Pallas kernels, step(): pl.pallas_call(functools.partial(query_kernel, classes=classes, list_len=...  7.45 us
    pallas_call x1, Pallas kernels, step(): pl.pallas_call(functools.partial(forward_kernel, classes=classes, list_le...  6.41 us
  transfers between devices with their start and end apart: 51, of which 19 were waited for; matrix products, arithmetic and copies ran while one was open for 1% of the time, Pallas kernels for 6%

profile of v1, /device:TPU:94, one launch (start us, length us, event | category | flops | bytes accessed | tf_op | source)
XLA Modules:
  0.0 259.2 jit_solution(11984551617426130773)
XLA Ops:
  0.6 5.5 %collective-permute-start = (bf16[256,640]{1,0:T(8,128)(2,1)}, bf16[256,640]{1,0:T(8,128)(2,1)S(1)}, u32[]{:S(2)}, u32[]{:S(2)}) collective-permute-start(bf16[256,640]{1,0:T(8,128)(2,1)} %rest_0_.5), channel_id=1, source_target_pairs={{0,128},{8,136},{16,144},{24,152},{32,160},{40,168},{48,176},{56,1... | collective-permute-start | bytes 983048 | tf_op jit(solution)/shard_map/ppermute | solution.py:432
  6.1 3.1 %collective-permute-start.1 = (bf16[256,640]{1,0:T(8,128)(2,1)}, bf16[256,640]{1,0:T(8,128)(2,1)S(1)}, u32[]{:S(2)}, u32[]{:S(2)}) collective-permute-start(bf16[256,640]{1,0:T(8,128)(2,1)} %rest_0_.5), channel_id=1, source_target_pairs={{64,128},{128,64},{72,136},{136,72},{80,144},{144,80},{88,152},{15... | collective-permute-start | bytes 983048 | tf_op jit(solution)/shard_map/ppermute | solution.py:432
  9.4 0.7 collective-permute-start.4
  10.1 0.8 copy.11
  10.9 19.0 %collective-permute-done.rest_3_.rest_4_ = bf16[256,640]{1,0:T(8,128)(2,1)S(1)} collective-permute-done((bf16[256,640]{1,0:T(8,128)(2,1)}, bf16[256,640]{1,0:T(8,128)(2,1)S(1)}, u32[]{:S(2)}, u32[]{:S(2)}) %collective-permute-start) | collective-permute-done | bytes 327712 | tf_op jit(solution)/shard_map/ppermute | solution.py:432
  29.9 8.8 %collective-permute-done.1.rest_4_.rest_5_ = bf16[256,640]{1,0:T(8,128)(2,1)S(1)} collective-permute-done((bf16[256,640]{1,0:T(8,128)(2,1)}, bf16[256,640]{1,0:T(8,128)(2,1)S(1)}, u32[]{:S(2)}, u32[]{:S(2)}) %collective-permute-start.1) | collective-permute-done | bytes 327712 | tf_op jit(solution)/shard_map/ppermute | solution.py:432
  38.8 0.7 dynamic-slice_bitcast_fusion
  39.5 0.7 collective-permute-start.7
  40.2 0.2 fusion.2
  40.6 10.5 %collective-permute-start.13 = (bf16[256,640]{1,0:T(8,128)(2,1)}, bf16[256,640]{1,0:T(8,128)(2,1)}, u32[]{:S(2)}, u32[]{:S(2)}) collective-permute-start(bf16[256,640]{1,0:T(8,128)(2,1)} %rest_1_.3), channel_id=1, source_target_pairs={{64,128},{128,64},{72,136},{136,72},{80,144},{144,80},{88,152},{15... | collective-permute-start | bytes 983048 | tf_op jit(solution)/shard_map/ppermute | solution.py:432
  51.5 0.7 collective-permute-start.16
  52.2 0.2 fusion.3
  52.8 3.8 %collective-permute-done.12.rest_16_.rest_17_ = bf16[256,640]{1,0:T(8,128)(2,1)} collective-permute-done((bf16[256,640]{1,0:T(8,128)(2,1)}, bf16[256,640]{1,0:T(8,128)(2,1)}, u32[]{:S(2)}, u32[]{:S(2)}) %collective-permute-start.12) | collective-permute-done | bytes 327712 | tf_op jit(solution)/shard_map/ppermute | solution.py:432
  56.5 3.6 %collective-permute-start.17 = (bf16[256,640]{1,0:T(8,128)(2,1)}, bf16[256,640]{1,0:T(8,128)(2,1)S(1)}, u32[]{:S(2)}, u32[]{:S(2)}) collective-permute-start(bf16[256,640]{1,0:T(8,128)(2,1)} %rest_1_.3), channel_id=1, source_target_pairs={{0,16},{8,24},{16,0},{24,8},{32,48},{40,56},{48,32},{56,40},{64,80... | collective-permute-start | bytes 983048 | tf_op jit(solution)/shard_map/ppermute | solution.py:432
  60.2 18.3 %collective-permute-done.13.rest_17_.rest_18_ = bf16[256,640]{1,0:T(8,128)(2,1)} collective-permute-done((bf16[256,640]{1,0:T(8,128)(2,1)}, bf16[256,640]{1,0:T(8,128)(2,1)}, u32[]{:S(2)}, u32[]{:S(2)}) %collective-permute-start.13) | collective-permute-done | bytes 327712 | tf_op jit(solution)/shard_map/ppermute | solution.py:432
  78.5 0.7 collective-permute-start.19
  79.2 1.3 collective-permute-start.8
  80.5 1.4 collective-permute-start.9
  82.0 6.6 %collective-permute-start.11 = (bf16[256,640]{1,0:T(8,128)(2,1)S(1)}, bf16[256,640]{1,0:T(8,128)(2,1)S(1)}, u32[]{:S(2)}, u32[]{:S(2)}) collective-permute-start(bf16[256,640]{1,0:T(8,128)(2,1)S(1)} %broadcast_select_fusion.3), channel_id=1, source_target_pairs={{48,32},{56,40},{80,64},{88,72},{112,96},{120,104},{176,160},{184,... | collective-permute-start | bytes 983048 | tf_op jit(solution)/shard_map/ppermute | solution.py:432
  88.7 0.4 collective-permute-done.18.rest_22_.rest_23_
  89.1 1.3 collective-permute-start.10
  90.4 1.3 collective-permute-start.20
  91.7 1.3 collective-permute-start.21
  93.0 0.2 fusion.7.counts
  93.2 2.4 collective-permute-done.9.rest_12_.rest_13_
  95.6 1.3 collective-permute-start.22
  96.9 0.7 compare_convert_fusion.valid
  97.6 17.7 %collective-permute-done.10.rest_13_.rest_14_ = bf16[256,640]{1,0:T(8,128)(2,1)S(1)} collective-permute-done((bf16[256,640]{1,0:T(8,128)(2,1)S(1)}, bf16[256,640]{1,0:T(8,128)(2,1)S(1)}, u32[]{:S(2)}, u32[]{:S(2)}) %collective-permute-start.10) | collective-permute-done | bytes 327712 | tf_op jit(solution)/shard_map/ppermute | solution.py:432
  115.3 4.9 %collective-permute-start.28 = (bf16[272,640]{1,0:T(8,128)(2,1)S(1)}, bf16[272,640]{1,0:T(8,128)(2,1)S(1)}, u32[]{:S(2)}, u32[]{:S(2)}) collective-permute-start(bf16[272,640]{1,0:T(8,128)(2,1)S(1)} %fusion.1.rest_0_.rest_2_), channel_id=1, source_target_pairs={{64,128},{128,64},{72,136},{136,72},{80,144},{144,80},{88,152},{15... | collective-permute-start | bytes 1044488 | tf_op jit(solution)/shard_map/ppermute | solution.py:432
  120.3 0.7 collective-permute-start.31
  121.0 1.2 collective-permute-done.22.rest_26_.rest_27_
  122.2 1.3 collective-permute-start.23
  123.5 7.4 %collective-permute-done.23.rest_27_.rest_28_ = bf16[256,640]{1,0:T(8,128)(2,1)S(1)} collective-permute-done((bf16[256,640]{1,0:T(8,128)(2,1)S(1)}, bf16[256,640]{1,0:T(8,128)(2,1)S(1)}, u32[]{:S(2)}, u32[]{:S(2)}) %collective-permute-start.23) | collective-permute-done | bytes 327712 | tf_op jit(solution)/shard_map/ppermute | solution.py:432
  130.9 6.4 %forward.1 = (f32[256,640]{1,0:T(8,128)S(1)}, f32[16,640]{1,0:T(8,128)S(1)}, f32[2,128]{1,0:T(2,128)S(1)}) custom-call(s32[12]{0:T(128)S(1)} %reshape.20.slots, s32[12]{0:T(128)S(1)} %reshape.21.counts, s32[13]{0:T(128)S(1)} %convert_element_type.12.used, bf16[256,640]{1,0:T(8,128)(2,1)S(1)} %copy-done.2, bf16[256,640]{1,0:T(8,128)(2,1)S(1)} %copy-done.3, ...), custom_call_target="tpu_custom_call" | custom-call | tf_op jit(solution)/shard_map/forward/pallas_call | solution.py:482
  137.5 1.1 collective-permute-done.24
  138.6 3.6 %collective-permute-done.25 = f32[2,128]{1,0:T(2,128)S(1)} collective-permute-done((f32[2,128]{1,0:T(2,128)S(1)}, f32[2,128]{1,0:T(2,128)S(1)}, u32[]{:S(2)}, u32[]{:S(2)}) %collective-permute-start.25) | collective-permute-done | bytes 1056 | tf_op jit(solution)/shard_map/ppermute | solution.py:499
  142.2 2.6 %collective-permute-start.26 = (f32[2,128]{1,0:T(2,128)S(1)}, f32[2,128]{1,0:T(2,128)S(1)}, u32[]{:S(2)}, u32[]{:S(2)}) collective-permute-start(f32[2,128]{1,0:T(2,128)S(1)} %add.50), channel_id=1, source_target_pairs={{0,4},{1,5},{2,6},{3,7},{4,0},{5,1},{6,2},{7,3},{8,12},{9,13},{10,... | collective-permute-start | bytes 3080 | tf_op jit(solution)/shard_map/ppermute | solution.py:499
  144.8 6.1 %collective-permute-start.29 = (bf16[272,640]{1,0:T(8,128)(2,1)S(1)}, bf16[272,640]{1,0:T(8,128)(2,1)S(1)}, u32[]{:S(2)}, u32[]{:S(2)}) collective-permute-start(bf16[272,640]{1,0:T(8,128)(2,1)S(1)} %fusion.1.rest_0_.rest_2_), channel_id=1, source_target_pairs={{0,64},{8,72},{16,80},{24,88},{32,96},{40,104},{48,112},{56,120},{... | collective-permute-start | bytes 1044488 | tf_op jit(solution)/shard_map/ppermute | solution.py:432
  151.1 3.5 %collective-permute-start.33 = (bf16[272,640]{1,0:T(8,128)(2,1)S(1)}, bf16[272,640]{1,0:T(8,128)(2,1)S(1)}, u32[]{:S(2)}, u32[]{:S(2)}) collective-permute-start(bf16[272,640]{1,0:T(8,128)(2,1)S(1)} %fusion.1.rest_0_.rest_2_), channel_id=1, source_target_pairs={{0,8},{8,0},{16,24},{24,16},{32,40},{40,32},{48,56},{56,48},{64,72... | collective-permute-start | bytes 1044488 | tf_op jit(solution)/shard_map/ppermute | solution.py:432
  154.6 0.7 collective-permute-start.34
  155.3 1.3 collective-permute-start.35
  156.6 0.9 upstream.1.rest_1_.rest_15_
  157.6 0.6 collective-permute-done.29.rest_3_.rest_5_
  158.2 1.3 collective-permute-start.36
  159.5 4.0 %collective-permute-done.32.rest_6_.rest_8_ = bf16[272,640]{1,0:T(8,128)(2,1)S(1)} collective-permute-done((bf16[272,640]{1,0:T(8,128)(2,1)S(1)}, bf16[272,640]{1,0:T(8,128)(2,1)S(1)}, u32[]{:S(2)}, u32[]{:S(2)}) %collective-permute-start.32) | collective-permute-done | bytes 348192 | tf_op jit(solution)/shard_map/ppermute | solution.py:432
  163.5 1.3 collective-permute-start.37
  164.7 4.0 %collective-permute-done.33.rest_7_.rest_9_ = bf16[272,640]{1,0:T(8,128)(2,1)S(1)} collective-permute-done((bf16[272,640]{1,0:T(8,128)(2,1)S(1)}, bf16[272,640]{1,0:T(8,128)(2,1)S(1)}, u32[]{:S(2)}, u32[]{:S(2)}) %collective-permute-start.33) | collective-permute-done | bytes 348192 | tf_op jit(solution)/shard_map/ppermute | solution.py:432
  168.8 2.8 %collective-permute-start.38 = (bf16[272,640]{1,0:T(8,128)(2,1)S(1)}, bf16[272,640]{1,0:T(8,128)(2,1)S(1)}, u32[]{:S(2)}, u32[]{:S(2)}) collective-permute-start(bf16[272,640]{1,0:T(8,128)(2,1)S(1)} %broadcast_select_fusion.1), channel_id=1, source_target_pairs={{48,32},{56,40},{80,64},{88,72},{112,96},{120,104},{176,160},{184,... | collective-permute-start | bytes 1044488 | tf_op jit(solution)/shard_map/ppermute | solution.py:432
  171.7 0.6 collective-permute-start.42
  172.3 0.7 collective-permute-start.43
  173.0 3.1 %collective-permute-done.36.rest_10_.rest_12_ = bf16[272,640]{1,0:T(8,128)(2,1)S(1)} collective-permute-done((bf16[272,640]{1,0:T(8,128)(2,1)S(1)}, bf16[272,640]{1,0:T(8,128)(2,1)S(1)}, u32[]{:S(2)}, u32[]{:S(2)}) %collective-permute-start.36) | collective-permute-done | bytes 348192 | tf_op jit(solution)/shard_map/ppermute | solution.py:432
  176.1 16.9 %collective-permute-done.37.rest_11_.rest_13_ = bf16[272,640]{1,0:T(8,128)(2,1)S(1)} collective-permute-done((bf16[272,640]{1,0:T(8,128)(2,1)S(1)}, bf16[272,640]{1,0:T(8,128)(2,1)S(1)}, u32[]{:S(2)}, u32[]{:S(2)}) %collective-permute-start.37) | collective-permute-done | bytes 348192 | tf_op jit(solution)/shard_map/ppermute | solution.py:432
  193.0 3.2 %collective-permute-start.40 = (bf16[272,640]{1,0:T(8,128)(2,1)S(1)}, bf16[272,640]{1,0:T(8,128)(2,1)S(1)}, u32[]{:S(2)}, u32[]{:S(2)}) collective-permute-start(bf16[272,640]{1,0:T(8,128)(2,1)S(1)} %upstream.1.rest_1_.rest_15_), channel_id=1, source_target_pairs={{64,128},{128,64},{72,136},{136,72},{80,144},{144,80},{88,152},{15... | collective-permute-start | bytes 1044488 | tf_op jit(solution)/shard_map/ppermute | solution.py:432
  196.6 0.7 collective-permute-start.46
  197.3 24.0 %collective-permute-done.40.rest_17_ = bf16[272,640]{1,0:T(8,128)(2,1)S(1)} collective-permute-done((bf16[272,640]{1,0:T(8,128)(2,1)S(1)}, bf16[272,640]{1,0:T(8,128)(2,1)S(1)}, u32[]{:S(2)}, u32[]{:S(2)}) %collective-permute-start.40) | collective-permute-done | bytes 348192 | tf_op jit(solution)/shard_map/ppermute | solution.py:432
  221.3 1.3 collective-permute-start.47
  222.6 1.3 collective-permute-start.48
  223.9 1.3 collective-permute-start.49
  225.2 1.3 collective-permute-start.50
  226.6 7.5 %grad_queries.1 = bf16[256,640]{1,0:T(8,128)(2,1)} custom-call(s32[12]{0:T(128)S(1)} %reshape.20.slots, s32[12]{0:T(128)S(1)} %reshape.21.counts, s32[13]{0:T(128)S(1)} %convert_element_type.12.used, bf16[256,640]{1,0:T(8,128)(2,1)S(1)} %copy-done.2, bf16[272,640]{1,0:T(8,128)(2,1)S(1)} %upstream.1.rest_1_.rest_15_, ...), custom_call_target="tpu_custom_call" | custom-call | tf_op jit(solution)/shard_map/grad_queries/pallas_call | solution.py:526
  234.0 0.8 naming.1.names
  234.9 3.2 %collective-permute-done.48.rest_25_ = bf16[272,640]{1,0:T(8,128)(2,1)S(1)} collective-permute-done((bf16[272,640]{1,0:T(8,128)(2,1)S(1)}, bf16[272,640]{1,0:T(8,128)(2,1)S(1)}, u32[]{:S(2)}, u32[]{:S(2)}) %collective-permute-start.48) | collective-permute-done | bytes 348192 | tf_op jit(solution)/shard_map/ppermute | solution.py:432
  238.0 12.3 %collective-permute-done.49.rest_26_ = bf16[272,640]{1,0:T(8,128)(2,1)S(1)} collective-permute-done((bf16[272,640]{1,0:T(8,128)(2,1)S(1)}, bf16[272,640]{1,0:T(8,128)(2,1)S(1)}, u32[]{:S(2)}, u32[]{:S(2)}) %collective-permute-start.49) | collective-permute-done | bytes 348192 | tf_op jit(solution)/shard_map/ppermute | solution.py:432
  250.3 8.7 %grad_keys_values.1 = (bf16[256,640]{1,0:T(8,128)(2,1)}, bf16[256,640]{1,0:T(8,128)(2,1)}) custom-call(s32[16,128]{1,0:T(8,128)S(1)} %naming.1.names, s32[2]{0:T(128)S(1)} %fusion.7.counts, bf16[256,640]{1,0:T(8,128)(2,1)S(1)} %copy-done, bf16[256,640]{1,0:T(8,128)(2,1)S(1)} %copy-done.1, bf16[272,640]{1,0:T(8,128)(2,1)S(1)} %fusion.1.rest_0_.rest_2_, ...), custom_call_target="tpu_custom_call" | custom-call | tf_op jit(solution)/shard_map/grad_keys_values/pallas_call | solution.py:538
  (83 shorter events, 2.1 us)
Async XLA Ops:
  0.6 29.3 %collective-permute-start = (bf16[256,640]{1,0:T(8,128)(2,1)}, bf16[256,640]{1,0:T(8,128)(2,1)S(1)}, u32[]{:S(2)}, u32[]{:S(2)}) collective-permute-start(bf16[256,640]{1,0:T(8,128)(2,1)} %rest_0_.5), channel_id=1, source_target_pairs={{0,128},{8,136},{16,144},{24,152},{32,160},{40,168},{48,176},{56,1... | collective-permute-start | bytes 983048 | tf_op jit(solution)/shard_map/ppermute | solution.py:432
  6.1 32.6 %collective-permute-start.1 = (bf16[256,640]{1,0:T(8,128)(2,1)}, bf16[256,640]{1,0:T(8,128)(2,1)S(1)}, u32[]{:S(2)}, u32[]{:S(2)}) collective-permute-start(bf16[256,640]{1,0:T(8,128)(2,1)} %rest_0_.5), channel_id=1, source_target_pairs={{64,128},{128,64},{72,136},{136,72},{80,144},{144,80},{88,152},{15... | collective-permute-start | bytes 983048 | tf_op jit(solution)/shard_map/ppermute | solution.py:432
  9.2 30.3 %collective-permute-start.2 = (bf16[256,640]{1,0:T(8,128)(2,1)}, bf16[256,640]{1,0:T(8,128)(2,1)S(1)}, u32[]{:S(2)}, u32[]{:S(2)}) collective-permute-start(bf16[256,640]{1,0:T(8,128)(2,1)} %rest_0_.5), channel_id=1, source_target_pairs={{0,64},{8,72},{16,80},{24,88},{32,96},{40,104},{48,112},{56,120},{... | collective-permute-start | bytes 983048 | tf_op jit(solution)/shard_map/ppermute | solution.py:432
  9.3 31.2 %collective-permute-start.3 = (bf16[256,640]{1,0:T(8,128)(2,1)}, bf16[256,640]{1,0:T(8,128)(2,1)S(1)}, u32[]{:S(2)}, u32[]{:S(2)}) collective-permute-start(bf16[256,640]{1,0:T(8,128)(2,1)} %rest_0_.5), channel_id=1, source_target_pairs={{0,32},{8,40},{16,48},{24,56},{32,0},{40,8},{48,16},{56,24},{64,96... | collective-permute-start | bytes 983048 | tf_op jit(solution)/shard_map/ppermute | solution.py:432
  9.4 31.1 %collective-permute-start.4 = (bf16[256,640]{1,0:T(8,128)(2,1)}, bf16[256,640]{1,0:T(8,128)(2,1)S(1)}, u32[]{:S(2)}, u32[]{:S(2)}) collective-permute-start(bf16[256,640]{1,0:T(8,128)(2,1)} %rest_0_.5), channel_id=1, source_target_pairs={{32,64},{64,32},{40,72},{72,40},{48,80},{80,48},{56,88},{88,56},{1... | collective-permute-start | bytes 983048 | tf_op jit(solution)/shard_map/ppermute | solution.py:432
  29.9 21.1 %collective-permute-start.5 = (bf16[256,640]{1,0:T(8,128)(2,1)}, bf16[256,640]{1,0:T(8,128)(2,1)S(1)}, u32[]{:S(2)}, u32[]{:S(2)}) collective-permute-start(bf16[256,640]{1,0:T(8,128)(2,1)} %rest_0_.5), channel_id=1, source_target_pairs={{0,16},{8,24},{16,0},{24,8},{32,48},{40,56},{48,32},{56,40},{64,80... | collective-permute-start | bytes 983048 | tf_op jit(solution)/shard_map/ppermute | solution.py:432
  38.7 12.5 %collective-permute-start.6 = (bf16[256,640]{1,0:T(8,128)(2,1)}, bf16[256,640]{1,0:T(8,128)(2,1)S(1)}, u32[]{:S(2)}, u32[]{:S(2)}) collective-permute-start(bf16[256,640]{1,0:T(8,128)(2,1)} %rest_0_.5), channel_id=1, source_target_pairs={{0,8},{8,0},{16,24},{24,16},{32,40},{40,32},{48,56},{56,48},{64,72... | collective-permute-start | bytes 983048 | tf_op jit(solution)/shard_map/ppermute | solution.py:432
  39.5 12.0 %collective-permute-start.7 = (bf16[256,640]{1,0:T(8,128)(2,1)}, bf16[256,640]{1,0:T(8,128)(2,1)S(1)}, u32[]{:S(2)}, u32[]{:S(2)}) collective-permute-start(bf16[256,640]{1,0:T(8,128)(2,1)} %rest_0_.5), channel_id=1, source_target_pairs={{8,16},{16,8},{24,32},{32,24},{40,48},{48,40},{56,64},{64,56},{72,... | collective-permute-start | bytes 983048 | tf_op jit(solution)/shard_map/ppermute | solution.py:432
  40.5 10.8 %copy-start.5 = (s32[2,6]{1,0:T(2,128)S(1)}, s32[2,6]{1,0:T(2,128)}, u32[]{:S(2)}) copy-start(s32[2,6]{1,0:T(2,128)} %param.13) | copy-start | bytes 148
  40.5 16.0 %collective-permute-start.12 = (bf16[256,640]{1,0:T(8,128)(2,1)}, bf16[256,640]{1,0:T(8,128)(2,1)}, u32[]{:S(2)}, u32[]{:S(2)}) collective-permute-start(bf16[256,640]{1,0:T(8,128)(2,1)} %rest_1_.3), channel_id=1, source_target_pairs={{0,128},{8,136},{16,144},{24,152},{32,160},{40,168},{48,176},{56,1... | collective-permute-start | bytes 983048 | tf_op jit(solution)/shard_map/ppermute | solution.py:432
  40.6 37.9 %collective-permute-start.13 = (bf16[256,640]{1,0:T(8,128)(2,1)}, bf16[256,640]{1,0:T(8,128)(2,1)}, u32[]{:S(2)}, u32[]{:S(2)}) collective-permute-start(bf16[256,640]{1,0:T(8,128)(2,1)} %rest_1_.3), channel_id=1, source_target_pairs={{64,128},{128,64},{72,136},{136,72},{80,144},{144,80},{88,152},{15... | collective-permute-start | bytes 983048 | tf_op jit(solution)/shard_map/ppermute | solution.py:432
  51.1 27.4 %collective-permute-start.14 = (bf16[256,640]{1,0:T(8,128)(2,1)}, bf16[256,640]{1,0:T(8,128)(2,1)}, u32[]{:S(2)}, u32[]{:S(2)}) collective-permute-start(bf16[256,640]{1,0:T(8,128)(2,1)} %rest_1_.3), channel_id=1, source_target_pairs={{0,64},{8,72},{16,80},{24,88},{32,96},{40,104},{48,112},{56,120},{... | collective-permute-start | bytes 983048 | tf_op jit(solution)/shard_map/ppermute | solution.py:432
  51.2 28.0 %collective-permute-start.15 = (bf16[256,640]{1,0:T(8,128)(2,1)}, bf16[256,640]{1,0:T(8,128)(2,1)S(1)}, u32[]{:S(2)}, u32[]{:S(2)}) collective-permute-start(bf16[256,640]{1,0:T(8,128)(2,1)} %rest_1_.3), channel_id=1, source_target_pairs={{0,32},{8,40},{16,48},{24,56},{32,0},{40,8},{48,16},{56,24},{64,96... | collective-permute-start | bytes 983048 | tf_op jit(solution)/shard_map/ppermute | solution.py:432
  51.4 0.8 copy-start.6
  51.5 29.0 %collective-permute-start.16 = (bf16[256,640]{1,0:T(8,128)(2,1)}, bf16[256,640]{1,0:T(8,128)(2,1)S(1)}, u32[]{:S(2)}, u32[]{:S(2)}) collective-permute-start(bf16[256,640]{1,0:T(8,128)(2,1)} %rest_1_.3), channel_id=1, source_target_pairs={{32,64},{64,32},{40,72},{72,40},{48,80},{80,48},{56,88},{88,56},{1... | collective-permute-start | bytes 983048 | tf_op jit(solution)/shard_map/ppermute | solution.py:432
  56.5 25.5 %collective-permute-start.17 = (bf16[256,640]{1,0:T(8,128)(2,1)}, bf16[256,640]{1,0:T(8,128)(2,1)S(1)}, u32[]{:S(2)}, u32[]{:S(2)}) collective-permute-start(bf16[256,640]{1,0:T(8,128)(2,1)} %rest_1_.3), channel_id=1, source_target_pairs={{0,16},{8,24},{16,0},{24,8},{32,48},{40,56},{48,32},{56,40},{64,80... | collective-permute-start | bytes 983048 | tf_op jit(solution)/shard_map/ppermute | solution.py:432
  78.5 10.6 %collective-permute-start.18 = (bf16[256,640]{1,0:T(8,128)(2,1)}, bf16[256,640]{1,0:T(8,128)(2,1)S(1)}, u32[]{:S(2)}, u32[]{:S(2)}) collective-permute-start(bf16[256,640]{1,0:T(8,128)(2,1)} %rest_1_.3), channel_id=1, source_target_pairs={{0,8},{8,0},{16,24},{24,16},{32,40},{40,32},{48,56},{56,48},{64,72... | collective-permute-start | bytes 983048 | tf_op jit(solution)/shard_map/ppermute | solution.py:432
  78.5 11.9 %collective-permute-start.19 = (bf16[256,640]{1,0:T(8,128)(2,1)}, bf16[256,640]{1,0:T(8,128)(2,1)S(1)}, u32[]{:S(2)}, u32[]{:S(2)}) collective-permute-start(bf16[256,640]{1,0:T(8,128)(2,1)} %rest_1_.3), channel_id=1, source_target_pairs={{8,16},{16,8},{24,32},{32,24},{40,48},{48,40},{56,64},{64,56},{72,... | collective-permute-start | bytes 983048 | tf_op jit(solution)/shard_map/ppermute | solution.py:432
  79.2 12.5 %collective-permute-start.8 = (bf16[256,640]{1,0:T(8,128)(2,1)S(1)}, bf16[256,640]{1,0:T(8,128)(2,1)S(1)}, u32[]{:S(2)}, u32[]{:S(2)}) collective-permute-start(bf16[256,640]{1,0:T(8,128)(2,1)S(1)} %collective-permute-done.rest_3_.rest_4_), channel_id=1, source_target_pairs={{224,128},{232,136},{240,144},{248,152},{0,96},{8,104},{16,112},{2... | collective-permute-start | bytes 983048 | tf_op jit(solution)/shard_map/ppermute | solution.py:432
  80.5 12.7 %copy-start.2 = (bf16[256,640]{1,0:T(8,128)(2,1)S(1)}, bf16[256,640]{1,0:T(8,128)(2,1)}, u32[]{:S(2)}) copy-start(bf16[256,640]{1,0:T(8,128)(2,1)} %rest_0_.4) | copy-start | bytes 983044
  80.5 15.1 %collective-permute-start.9 = (bf16[256,640]{1,0:T(8,128)(2,1)S(1)}, bf16[256,640]{1,0:T(8,128)(2,1)S(1)}, u32[]{:S(2)}, u32[]{:S(2)}) collective-permute-start(bf16[256,640]{1,0:T(8,128)(2,1)S(1)} %collective-permute-done.1.rest_4_.rest_5_), channel_id=1, source_target_pairs={{176,128},{184,136},{64,112},{72,120},{177,129},{185,137},{65,113}... | collective-permute-start | bytes 983048 | tf_op jit(solution)/shard_map/ppermute | solution.py:432
  82.0 33.3 %collective-permute-start.11 = (bf16[256,640]{1,0:T(8,128)(2,1)S(1)}, bf16[256,640]{1,0:T(8,128)(2,1)S(1)}, u32[]{:S(2)}, u32[]{:S(2)}) collective-permute-start(bf16[256,640]{1,0:T(8,128)(2,1)S(1)} %broadcast_select_fusion.3), channel_id=1, source_target_pairs={{48,32},{56,40},{80,64},{88,72},{112,96},{120,104},{176,160},{184,... | collective-permute-start | bytes 983048 | tf_op jit(solution)/shard_map/ppermute | solution.py:432
  89.1 26.2 %collective-permute-start.10 = (bf16[256,640]{1,0:T(8,128)(2,1)S(1)}, bf16[256,640]{1,0:T(8,128)(2,1)S(1)}, u32[]{:S(2)}, u32[]{:S(2)}) collective-permute-start(bf16[256,640]{1,0:T(8,128)(2,1)S(1)} %collective-permute-done.1.rest_4_.rest_5_), channel_id=1, source_target_pairs={{184,128},{64,120},{185,129},{65,121},{186,130},{66,122},{187,131}... | collective-permute-start | bytes 983048 | tf_op jit(solution)/shard_map/ppermute | solution.py:432
  90.4 29.8 %collective-permute-start.20 = (bf16[256,640]{1,0:T(8,128)(2,1)}, bf16[256,640]{1,0:T(8,128)(2,1)S(1)}, u32[]{:S(2)}, u32[]{:S(2)}) collective-permute-start(bf16[256,640]{1,0:T(8,128)(2,1)} %collective-permute-done.12.rest_16_.rest_17_), channel_id=1, source_target_pairs={{224,128},{232,136},{240,144},{248,152},{0,96},{8,104},{16,112},{2... | collective-permute-start | bytes 983048 | tf_op jit(solution)/shard_map/ppermute | solution.py:432
  91.7 28.6 %collective-permute-start.21 = (bf16[256,640]{1,0:T(8,128)(2,1)}, bf16[256,640]{1,0:T(8,128)(2,1)S(1)}, u32[]{:S(2)}, u32[]{:S(2)}) collective-permute-start(bf16[256,640]{1,0:T(8,128)(2,1)} %collective-permute-done.13.rest_17_.rest_18_), channel_id=1, source_target_pairs={{176,128},{184,136},{64,112},{72,120},{177,129},{185,137},{65,113}... | collective-permute-start | bytes 983048 | tf_op jit(solution)/shard_map/ppermute | solution.py:432
  95.6 26.6 %collective-permute-start.22 = (bf16[256,640]{1,0:T(8,128)(2,1)}, bf16[256,640]{1,0:T(8,128)(2,1)S(1)}, u32[]{:S(2)}, u32[]{:S(2)}) collective-permute-start(bf16[256,640]{1,0:T(8,128)(2,1)} %collective-permute-done.13.rest_17_.rest_18_), channel_id=1, source_target_pairs={{184,128},{64,120},{185,129},{65,121},{186,130},{66,122},{187,131}... | collective-permute-start | bytes 983048 | tf_op jit(solution)/shard_map/ppermute | solution.py:432
  97.6 33.3 %copy-start = (bf16[256,640]{1,0:T(8,128)(2,1)S(1)}, bf16[256,640]{1,0:T(8,128)(2,1)}, u32[]{:S(2)}) copy-start(bf16[256,640]{1,0:T(8,128)(2,1)} %rest_0_.5) | copy-start | bytes 983044
  97.6 33.3 %copy-start.1 = (bf16[256,640]{1,0:T(8,128)(2,1)S(1)}, bf16[256,640]{1,0:T(8,128)(2,1)}, u32[]{:S(2)}) copy-start(bf16[256,640]{1,0:T(8,128)(2,1)} %rest_1_.3) | copy-start | bytes 983044
  97.6 33.3 %copy-start.3 = (bf16[256,640]{1,0:T(8,128)(2,1)S(1)}, bf16[256,640]{1,0:T(8,128)(2,1)}, u32[]{:S(2)}) copy-start(bf16[256,640]{1,0:T(8,128)(2,1)} %rest_3_.2) | copy-start | bytes 983044
  115.3 29.5 %collective-permute-start.27 = (bf16[272,640]{1,0:T(8,128)(2,1)S(1)}, bf16[272,640]{1,0:T(8,128)(2,1)S(1)}, u32[]{:S(2)}, u32[]{:S(2)}) collective-permute-start(bf16[272,640]{1,0:T(8,128)(2,1)S(1)} %fusion.1.rest_0_.rest_2_), channel_id=1, source_target_pairs={{0,128},{8,136},{16,144},{24,152},{32,160},{40,168},{48,176},{56,1... | collective-permute-start | bytes 1044488 | tf_op jit(solution)/shard_map/ppermute | solution.py:432
  115.3 35.6 %collective-permute-start.28 = (bf16[272,640]{1,0:T(8,128)(2,1)S(1)}, bf16[272,640]{1,0:T(8,128)(2,1)S(1)}, u32[]{:S(2)}, u32[]{:S(2)}) collective-permute-start(bf16[272,640]{1,0:T(8,128)(2,1)S(1)} %fusion.1.rest_0_.rest_2_), channel_id=1, source_target_pairs={{64,128},{128,64},{72,136},{136,72},{80,144},{144,80},{88,152},{15... | collective-permute-start | bytes 1044488 | tf_op jit(solution)/shard_map/ppermute | solution.py:432
  120.2 30.9 %collective-permute-start.30 = (bf16[272,640]{1,0:T(8,128)(2,1)S(1)}, bf16[272,640]{1,0:T(8,128)(2,1)S(1)}, u32[]{:S(2)}, u32[]{:S(2)}) collective-permute-start(bf16[272,640]{1,0:T(8,128)(2,1)S(1)} %fusion.1.rest_0_.rest_2_), channel_id=1, source_target_pairs={{0,32},{8,40},{16,48},{24,56},{32,0},{40,8},{48,16},{56,24},{64,96... | collective-permute-start | bytes 1044488 | tf_op jit(solution)/shard_map/ppermute | solution.py:432
  120.3 34.3 %collective-permute-start.31 = (bf16[272,640]{1,0:T(8,128)(2,1)S(1)}, bf16[272,640]{1,0:T(8,128)(2,1)S(1)}, u32[]{:S(2)}, u32[]{:S(2)}) collective-permute-start(bf16[272,640]{1,0:T(8,128)(2,1)S(1)} %fusion.1.rest_0_.rest_2_), channel_id=1, source_target_pairs={{32,64},{64,32},{40,72},{72,40},{48,80},{80,48},{56,88},{88,56},{1... | collective-permute-start | bytes 1044488 | tf_op jit(solution)/shard_map/ppermute | solution.py:432
  122.2 8.7 %collective-permute-start.23 = (bf16[256,640]{1,0:T(8,128)(2,1)S(1)}, bf16[256,640]{1,0:T(8,128)(2,1)S(1)}, u32[]{:S(2)}, u32[]{:S(2)}) collective-permute-start(bf16[256,640]{1,0:T(8,128)(2,1)S(1)} %broadcast_select_fusion.2), channel_id=1, source_target_pairs={{48,32},{56,40},{80,64},{88,72},{112,96},{120,104},{176,160},{184,... | collective-permute-start | bytes 983048 | tf_op jit(solution)/shard_map/ppermute | solution.py:432
  137.4 1.2 collective-permute-start.24
  138.6 3.6 %collective-permute-start.25 = (f32[2,128]{1,0:T(2,128)S(1)}, f32[2,128]{1,0:T(2,128)S(1)}, u32[]{:S(2)}, u32[]{:S(2)}) collective-permute-start(f32[2,128]{1,0:T(2,128)S(1)} %add.49), channel_id=1, source_target_pairs={{0,2},{1,3},{2,0},{3,1},{4,6},{5,7},{6,4},{7,5},{8,10},{9,11},{10,... | collective-permute-start | bytes 3080 | tf_op jit(solution)/shard_map/ppermute | solution.py:499
  142.2 14.4 %copy-start.4 = (bf16[256,640]{1,0:T(8,128)(2,1)S(1)}, bf16[256,640]{1,0:T(8,128)(2,1)}, u32[]{:S(2)}) copy-start(bf16[256,640]{1,0:T(8,128)(2,1)} %rest_2_.3) | copy-start | bytes 983044
  142.2 13.1 %collective-permute-start.26 = (f32[2,128]{1,0:T(2,128)S(1)}, f32[2,128]{1,0:T(2,128)S(1)}, u32[]{:S(2)}, u32[]{:S(2)}) collective-permute-start(f32[2,128]{1,0:T(2,128)S(1)} %add.50), channel_id=1, source_target_pairs={{0,4},{1,5},{2,6},{3,7},{4,0},{5,1},{6,2},{7,3},{8,12},{9,13},{10,... | collective-permute-start | bytes 3080 | tf_op jit(solution)/shard_map/ppermute | solution.py:499
  144.8 13.4 %collective-permute-start.29 = (bf16[272,640]{1,0:T(8,128)(2,1)S(1)}, bf16[272,640]{1,0:T(8,128)(2,1)S(1)}, u32[]{:S(2)}, u32[]{:S(2)}) collective-permute-start(bf16[272,640]{1,0:T(8,128)(2,1)S(1)} %fusion.1.rest_0_.rest_2_), channel_id=1, source_target_pairs={{0,64},{8,72},{16,80},{24,88},{32,96},{40,104},{48,112},{56,120},{... | collective-permute-start | bytes 1044488 | tf_op jit(solution)/shard_map/ppermute | solution.py:432
  150.9 12.6 %collective-permute-start.32 = (bf16[272,640]{1,0:T(8,128)(2,1)S(1)}, bf16[272,640]{1,0:T(8,128)(2,1)S(1)}, u32[]{:S(2)}, u32[]{:S(2)}) collective-permute-start(bf16[272,640]{1,0:T(8,128)(2,1)S(1)} %fusion.1.rest_0_.rest_2_), channel_id=1, source_target_pairs={{0,16},{8,24},{16,0},{24,8},{32,48},{40,56},{48,32},{56,40},{64,80... | collective-permute-start | bytes 1044488 | tf_op jit(solution)/shard_map/ppermute | solution.py:432
  151.1 17.7 %collective-permute-start.33 = (bf16[272,640]{1,0:T(8,128)(2,1)S(1)}, bf16[272,640]{1,0:T(8,128)(2,1)S(1)}, u32[]{:S(2)}, u32[]{:S(2)}) collective-permute-start(bf16[272,640]{1,0:T(8,128)(2,1)S(1)} %fusion.1.rest_0_.rest_2_), channel_id=1, source_target_pairs={{0,8},{8,0},{16,24},{24,16},{32,40},{40,32},{48,56},{56,48},{64,72... | collective-permute-start | bytes 1044488 | tf_op jit(solution)/shard_map/ppermute | solution.py:432
  154.6 17.1 %collective-permute-start.34 = (bf16[272,640]{1,0:T(8,128)(2,1)S(1)}, bf16[272,640]{1,0:T(8,128)(2,1)S(1)}, u32[]{:S(2)}, u32[]{:S(2)}) collective-permute-start(bf16[272,640]{1,0:T(8,128)(2,1)S(1)} %fusion.1.rest_0_.rest_2_), channel_id=1, source_target_pairs={{8,16},{16,8},{24,32},{32,24},{40,48},{48,40},{56,64},{64,56},{72,... | collective-permute-start | bytes 1044488 | tf_op jit(solution)/shard_map/ppermute | solution.py:432
  155.3 17.0 %collective-permute-start.35 = (bf16[272,640]{1,0:T(8,128)(2,1)S(1)}, bf16[272,640]{1,0:T(8,128)(2,1)S(1)}, u32[]{:S(2)}, u32[]{:S(2)}) collective-permute-start(bf16[272,640]{1,0:T(8,128)(2,1)S(1)} %collective-permute-done.27.rest_1_.rest_3_), channel_id=1, source_target_pairs={{224,128},{232,136},{240,144},{248,152},{0,96},{8,104},{16,112},{2... | collective-permute-start | bytes 1044488 | tf_op jit(solution)/shard_map/ppermute | solution.py:432
  158.2 17.8 %collective-permute-start.36 = (bf16[272,640]{1,0:T(8,128)(2,1)S(1)}, bf16[272,640]{1,0:T(8,128)(2,1)S(1)}, u32[]{:S(2)}, u32[]{:S(2)}) collective-permute-start(bf16[272,640]{1,0:T(8,128)(2,1)S(1)} %collective-permute-done.28.rest_2_.rest_4_), channel_id=1, source_target_pairs={{176,128},{184,136},{64,112},{72,120},{177,129},{185,137},{65,113}... | collective-permute-start | bytes 1044488 | tf_op jit(solution)/shard_map/ppermute | solution.py:432
  163.5 29.5 %collective-permute-start.37 = (bf16[272,640]{1,0:T(8,128)(2,1)S(1)}, bf16[272,640]{1,0:T(8,128)(2,1)S(1)}, u32[]{:S(2)}, u32[]{:S(2)}) collective-permute-start(bf16[272,640]{1,0:T(8,128)(2,1)S(1)} %collective-permute-done.28.rest_2_.rest_4_), channel_id=1, source_target_pairs={{184,128},{64,120},{185,129},{65,121},{186,130},{66,122},{187,131}... | collective-permute-start | bytes 1044488 | tf_op jit(solution)/shard_map/ppermute | solution.py:432
  168.8 27.4 %collective-permute-start.38 = (bf16[272,640]{1,0:T(8,128)(2,1)S(1)}, bf16[272,640]{1,0:T(8,128)(2,1)S(1)}, u32[]{:S(2)}, u32[]{:S(2)}) collective-permute-start(bf16[272,640]{1,0:T(8,128)(2,1)S(1)} %broadcast_select_fusion.1), channel_id=1, source_target_pairs={{48,32},{56,40},{80,64},{88,72},{112,96},{120,104},{176,160},{184,... | collective-permute-start | bytes 1044488 | tf_op jit(solution)/shard_map/ppermute | solution.py:432
  171.7 24.6 %collective-permute-start.42 = (bf16[272,640]{1,0:T(8,128)(2,1)S(1)}, bf16[272,640]{1,0:T(8,128)(2,1)S(1)}, u32[]{:S(2)}, u32[]{:S(2)}) collective-permute-start(bf16[272,640]{1,0:T(8,128)(2,1)S(1)} %upstream.1.rest_1_.rest_15_), channel_id=1, source_target_pairs={{0,32},{8,40},{16,48},{24,56},{32,0},{40,8},{48,16},{56,24},{64,96... | collective-permute-start | bytes 1044488 | tf_op jit(solution)/shard_map/ppermute | solution.py:432
  172.3 24.1 %collective-permute-start.43 = (bf16[272,640]{1,0:T(8,128)(2,1)S(1)}, bf16[272,640]{1,0:T(8,128)(2,1)S(1)}, u32[]{:S(2)}, u32[]{:S(2)}) collective-permute-start(bf16[272,640]{1,0:T(8,128)(2,1)S(1)} %upstream.1.rest_1_.rest_15_), channel_id=1, source_target_pairs={{32,64},{64,32},{40,72},{72,40},{48,80},{80,48},{56,88},{88,56},{1... | collective-permute-start | bytes 1044488 | tf_op jit(solution)/shard_map/ppermute | solution.py:432
  176.1 20.5 %collective-permute-start.39 = (bf16[272,640]{1,0:T(8,128)(2,1)S(1)}, bf16[272,640]{1,0:T(8,128)(2,1)S(1)}, u32[]{:S(2)}, u32[]{:S(2)}) collective-permute-start(bf16[272,640]{1,0:T(8,128)(2,1)S(1)} %upstream.1.rest_1_.rest_15_), channel_id=1, source_target_pairs={{0,128},{8,136},{16,144},{24,152},{32,160},{40,168},{48,176},{56,1... | collective-permute-start | bytes 1044488 | tf_op jit(solution)/shard_map/ppermute | solution.py:432
  193.0 28.4 %collective-permute-start.40 = (bf16[272,640]{1,0:T(8,128)(2,1)S(1)}, bf16[272,640]{1,0:T(8,128)(2,1)S(1)}, u32[]{:S(2)}, u32[]{:S(2)}) collective-permute-start(bf16[272,640]{1,0:T(8,128)(2,1)S(1)} %upstream.1.rest_1_.rest_15_), channel_id=1, source_target_pairs={{64,128},{128,64},{72,136},{136,72},{80,144},{144,80},{88,152},{15... | collective-permute-start | bytes 1044488 | tf_op jit(solution)/shard_map/ppermute | solution.py:432
  196.2 26.4 %collective-permute-start.41 = (bf16[272,640]{1,0:T(8,128)(2,1)S(1)}, bf16[272,640]{1,0:T(8,128)(2,1)S(1)}, u32[]{:S(2)}, u32[]{:S(2)}) collective-permute-start(bf16[272,640]{1,0:T(8,128)(2,1)S(1)} %upstream.1.rest_1_.rest_15_), channel_id=1, source_target_pairs={{0,64},{8,72},{16,80},{24,88},{32,96},{40,104},{48,112},{56,120},{... | collective-permute-start | bytes 1044488 | tf_op jit(solution)/shard_map/ppermute | solution.py:432
  196.3 27.6 %collective-permute-start.44 = (bf16[272,640]{1,0:T(8,128)(2,1)S(1)}, bf16[272,640]{1,0:T(8,128)(2,1)S(1)}, u32[]{:S(2)}, u32[]{:S(2)}) collective-permute-start(bf16[272,640]{1,0:T(8,128)(2,1)S(1)} %upstream.1.rest_1_.rest_15_), channel_id=1, source_target_pairs={{0,16},{8,24},{16,0},{24,8},{32,48},{40,56},{48,32},{56,40},{64,80... | collective-permute-start | bytes 1044488 | tf_op jit(solution)/shard_map/ppermute | solution.py:432
  196.4 28.8 %collective-permute-start.45 = (bf16[272,640]{1,0:T(8,128)(2,1)S(1)}, bf16[272,640]{1,0:T(8,128)(2,1)S(1)}, u32[]{:S(2)}, u32[]{:S(2)}) collective-permute-start(bf16[272,640]{1,0:T(8,128)(2,1)S(1)} %upstream.1.rest_1_.rest_15_), channel_id=1, source_target_pairs={{0,8},{8,0},{16,24},{24,16},{32,40},{40,32},{48,56},{56,48},{64,72... | collective-permute-start | bytes 1044488 | tf_op jit(solution)/shard_map/ppermute | solution.py:432
  196.6 38.3 %collective-permute-start.46 = (bf16[272,640]{1,0:T(8,128)(2,1)S(1)}, bf16[272,640]{1,0:T(8,128)(2,1)S(1)}, u32[]{:S(2)}, u32[]{:S(2)}) collective-permute-start(bf16[272,640]{1,0:T(8,128)(2,1)S(1)} %upstream.1.rest_1_.rest_15_), channel_id=1, source_target_pairs={{8,16},{16,8},{24,32},{32,24},{40,48},{48,40},{56,64},{64,56},{72,... | collective-permute-start | bytes 1044488 | tf_op jit(solution)/shard_map/ppermute | solution.py:432
  221.3 13.5 %collective-permute-start.47 = (bf16[272,640]{1,0:T(8,128)(2,1)S(1)}, bf16[272,640]{1,0:T(8,128)(2,1)S(1)}, u32[]{:S(2)}, u32[]{:S(2)}) collective-permute-start(bf16[272,640]{1,0:T(8,128)(2,1)S(1)} %collective-permute-done.39.rest_16_), channel_id=1, source_target_pairs={{224,128},{232,136},{240,144},{248,152},{0,96},{8,104},{16,112},{2... | collective-permute-start | bytes 1044488 | tf_op jit(solution)/shard_map/ppermute | solution.py:432
  222.6 15.4 %collective-permute-start.48 = (bf16[272,640]{1,0:T(8,128)(2,1)S(1)}, bf16[272,640]{1,0:T(8,128)(2,1)S(1)}, u32[]{:S(2)}, u32[]{:S(2)}) collective-permute-start(bf16[272,640]{1,0:T(8,128)(2,1)S(1)} %collective-permute-done.40.rest_17_), channel_id=1, source_target_pairs={{176,128},{184,136},{64,112},{72,120},{177,129},{185,137},{65,113}... | collective-permute-start | bytes 1044488 | tf_op jit(solution)/shard_map/ppermute | solution.py:432
  223.9 26.4 %collective-permute-start.49 = (bf16[272,640]{1,0:T(8,128)(2,1)S(1)}, bf16[272,640]{1,0:T(8,128)(2,1)S(1)}, u32[]{:S(2)}, u32[]{:S(2)}) collective-permute-start(bf16[272,640]{1,0:T(8,128)(2,1)S(1)} %collective-permute-done.40.rest_17_), channel_id=1, source_target_pairs={{184,128},{64,120},{185,129},{65,121},{186,130},{66,122},{187,131}... | collective-permute-start | bytes 1044488 | tf_op jit(solution)/shard_map/ppermute | solution.py:432
  225.2 25.1 %collective-permute-start.50 = (bf16[272,640]{1,0:T(8,128)(2,1)S(1)}, bf16[272,640]{1,0:T(8,128)(2,1)S(1)}, u32[]{:S(2)}, u32[]{:S(2)}) collective-permute-start(bf16[272,640]{1,0:T(8,128)(2,1)S(1)} %broadcast_select_fusion), channel_id=1, source_target_pairs={{48,32},{56,40},{80,64},{88,72},{112,96},{120,104},{176,160},{184,... | collective-permute-start | bytes 1044488 | tf_op jit(solution)/shard_map/ppermute | solution.py:432

commit v2 on v1

--- a/solution.py
+++ b/solution.py
@@ -400,15 +400,39 @@
     ),
 ]
 NAMES = ["own"] + [name for name, _, _ in DIRECT + RELAYED]
+LIGHT = [flow for flow in DIRECT if flow[0] != "step8"] + [
+    (
+        "step8",
+        "half",
+        [(at(1, y, x), at(1, y - 2, x)) for y in (2, 3) for x in range(4)]
+        + [(at(0, y, x), at(0, y + 2, x)) for y in (0, 1) for x in range(4)],
+    ),
+    RELAYED[0],
+    (
+        "wrap2",
+        "half",
+        [
+            (at(1, 3, 2), at(1, 0, 0)),
+            (at(1, 3, 3), at(1, 0, 1)),
+            (at(0, 0, 0), at(0, 3, 2)),
+            (at(0, 0, 1), at(0, 3, 3)),
+        ],
+    ),
+    ("wrap1", "half", [(at(1, 3, 3), at(1, 0, 0)), (at(0, 0, 0), at(0, 3, 3))]),
+    RELAYED[3],
+]
+
+
+LIGHT_FLOWS = "q"
 
 
 def turn_takes_flip(f):
     return (f & 3 >= 2) == (f >> 2 & 1 == 1)
 
 
-def owners():
+def owners(flows):
     held = {"own": list(range(FRAMES))}
-    for name, sent, pairs in DIRECT + RELAYED:
+    for name, sent, pairs in flows:
         if sent == "turn":
             held["turn"] = [
                 held["flip4" if turn_takes_flip(f) else "step4"][f] for f in range(FRAMES)
@@ -424,9 +448,9 @@
     return table
 
 
-def spread(value, turn_flip):
+def spread(value, turn_flip, prefix):
     held = {"own": value}
-    for name, sent, pairs in DIRECT + RELAYED:
+    for name, sent, pairs in LIGHT if prefix in LIGHT_FLOWS else DIRECT + RELAYED:
         if sent == "turn" and "turn" not in held:
             held["turn"] = jnp.where(turn_flip, held["flip4"], held["step4"])
         held[name] = lax.ppermute(held[sent], "frame", pairs)
@@ -445,11 +469,13 @@
     f32 = jnp.float32
     turn_flip = (me % 4 >= 2) == (me // 4 % 2 == 1)
 
-    key_pool = spread(keys, turn_flip)
-    value_pool = spread(values, turn_flip)
-
+    key_pool = spread(keys, turn_flip, "k")
+    value_pool = spread(values, turn_flip, "v")
+
+    table = owners(DIRECT + RELAYED)
+    assert (table == owners(LIGHT)).all()
     owner_here = lax.dynamic_slice(
-        jnp.asarray(owners().T.astype(np.int32)), (me, 0), (1, classes)
+        jnp.asarray(table.T.astype(np.int32)), (me, 0), (1, classes)
     ).reshape(-1)
     owner = key_lists // blocks
     hits = owner[..., None] == owner_here
@@ -469,7 +495,7 @@
     tailed, slots, counts, used, valid, own, own_counts = lax.optimization_barrier(
         (tailed, slots, counts, used, valid, own, own_counts)
     )
-    query_pool = spread(tailed, turn_flip)
+    query_pool = spread(tailed, turn_flip, "q")
 
     def shard(dtype=jnp.bfloat16, height=rows):
         return pltpu.VMEM((height, cols), dtype)
@@ -509,7 +535,7 @@
         name="upstream",
     )(squares, lse, attn, policy_grad, ref_velocity)
 
-    grad_pool = spread(grad, turn_flip)
+    grad_pool = spread(grad, turn_flip, "d")
 
     names = pl.pallas_call(
         functools.partial(

time: 263 us -> 257 us (0.977)
  the two profiles are of different devices: /device:TPU:94 before, /device:TPU:225 now
where the time goes in v2:
time: 257 us; the launch traced here: 256 us
  waiting for transfers between devices  128 us (50%)
  starting transfers between devices  96.7 us (38%)
  Pallas kernels  26.9 us (10%)
    ppermute x48, waiting for transfers between devices, spread(): held[name] = lax.ppermute(held[sent], 'frame', pairs)  126 us
    ppermute x48, starting transfers between devices, spread(): held[name] = lax.ppermute(held[sent], 'frame', pairs)  83.9 us
    ppermute x3, starting transfers between devices, step(): lax.ppermute(squares, 'head', [(i, i ^ hop) for i in range(heads)])  12.8 us
    pallas_call x1, Pallas kernels, step(): pl.pallas_call(functools.partial(key_kernel, classes=classes, scale=scale...  10.6 us
    pallas_call x1, Pallas kernels, step(): pl.pallas_call(functools.partial(query_kernel, classes=classes, list_len=...  7.81 us
    pallas_call x1, Pallas kernels, step(): pl.pallas_call(functools.partial(forward_kernel, classes=classes, list_le...  6.75 us
  transfers between devices with their start and end apart: 51, of which 18 were waited for; matrix products, arithmetic and copies ran while one was open for 1% of the time, Pallas kernels for 6%

profile of v2, /device:TPU:225, one launch (start us, length us, event | category | flops | bytes accessed | tf_op | source)
XLA Modules:
  0.0 256.3 jit_solution(3057575293964249524)
XLA Ops:
  0.6 1.2 collective-permute-start
  1.9 8.7 %collective-permute-start.1 = (bf16[256,640]{1,0:T(8,128)(2,1)}, bf16[256,640]{1,0:T(8,128)(2,1)S(1)}, u32[]{:S(2)}, u32[]{:S(2)}) collective-permute-start(bf16[256,640]{1,0:T(8,128)(2,1)} %rest_0_.5), channel_id=1, source_target_pairs={{64,128},{128,64},{72,136},{136,72},{80,144},{144,80},{88,152},{15... | collective-permute-start | bytes 983048 | tf_op jit(solution)/shard_map/ppermute | solution.py:456
  11.2 0.7 collective-permute-start.4
  11.9 0.8 copy.11
  12.7 6.8 %collective-permute-done.rest_3_.rest_4_ = bf16[256,640]{1,0:T(8,128)(2,1)S(1)} collective-permute-done((bf16[256,640]{1,0:T(8,128)(2,1)}, bf16[256,640]{1,0:T(8,128)(2,1)S(1)}, u32[]{:S(2)}, u32[]{:S(2)}) %collective-permute-start) | collective-permute-done | bytes 327712 | tf_op jit(solution)/shard_map/ppermute | solution.py:456
  19.4 2.7 %collective-permute-start.5 = (bf16[256,640]{1,0:T(8,128)(2,1)}, bf16[256,640]{1,0:T(8,128)(2,1)S(1)}, u32[]{:S(2)}, u32[]{:S(2)}) collective-permute-start(bf16[256,640]{1,0:T(8,128)(2,1)} %rest_0_.5), channel_id=1, source_target_pairs={{0,16},{8,24},{16,0},{24,8},{32,48},{40,56},{48,32},{56,40},{64,80... | collective-permute-start | bytes 983048 | tf_op jit(solution)/shard_map/ppermute | solution.py:456
  22.2 7.8 %collective-permute-done.1.rest_4_.rest_5_ = bf16[256,640]{1,0:T(8,128)(2,1)S(1)} collective-permute-done((bf16[256,640]{1,0:T(8,128)(2,1)}, bf16[256,640]{1,0:T(8,128)(2,1)S(1)}, u32[]{:S(2)}, u32[]{:S(2)}) %collective-permute-start.1) | collective-permute-done | bytes 327712 | tf_op jit(solution)/shard_map/ppermute | solution.py:456
  30.0 1.2 collective-permute-start.6
  31.3 0.7 dynamic-slice_bitcast_fusion
  32.0 0.7 collective-permute-start.7
  33.0 6.2 %collective-permute-start.12 = (bf16[256,640]{1,0:T(8,128)(2,1)}, bf16[256,640]{1,0:T(8,128)(2,1)}, u32[]{:S(2)}, u32[]{:S(2)}) collective-permute-start(bf16[256,640]{1,0:T(8,128)(2,1)} %rest_1_.3), channel_id=1, source_target_pairs={{0,128},{8,136},{16,144},{24,152},{32,160},{40,168},{48,176},{56,1... | collective-permute-start | bytes 983048 | tf_op jit(solution)/shard_map/ppermute | solution.py:456
  39.2 5.8 %collective-permute-start.13 = (bf16[256,640]{1,0:T(8,128)(2,1)}, bf16[256,640]{1,0:T(8,128)(2,1)}, u32[]{:S(2)}, u32[]{:S(2)}) collective-permute-start(bf16[256,640]{1,0:T(8,128)(2,1)} %rest_1_.3), channel_id=1, source_target_pairs={{64,128},{128,64},{72,136},{136,72},{80,144},{144,80},{88,152},{15... | collective-permute-start | bytes 983048 | tf_op jit(solution)/shard_map/ppermute | solution.py:456
  45.1 4.5 %collective-permute-start.15 = (bf16[256,640]{1,0:T(8,128)(2,1)}, bf16[256,640]{1,0:T(8,128)(2,1)S(1)}, u32[]{:S(2)}, u32[]{:S(2)}) collective-permute-start(bf16[256,640]{1,0:T(8,128)(2,1)} %rest_1_.3), channel_id=1, source_target_pairs={{0,32},{8,40},{16,48},{24,56},{32,0},{40,8},{48,16},{56,24},{64,96... | collective-permute-start | bytes 983048 | tf_op jit(solution)/shard_map/ppermute | solution.py:456
  49.8 0.7 collective-permute-start.16
  51.2 13.3 %collective-permute-done.13.rest_17_.rest_18_ = bf16[256,640]{1,0:T(8,128)(2,1)} collective-permute-done((bf16[256,640]{1,0:T(8,128)(2,1)}, bf16[256,640]{1,0:T(8,128)(2,1)}, u32[]{:S(2)}, u32[]{:S(2)}) %collective-permute-start.13) | collective-permute-done | bytes 327712 | tf_op jit(solution)/shard_map/ppermute | solution.py:456
  64.5 0.7 collective-permute-start.19
  65.1 1.3 collective-permute-start.8
  66.5 1.4 collective-permute-start.9
  68.0 11.8 %collective-permute-start.11 = (bf16[256,640]{1,0:T(8,128)(2,1)S(1)}, bf16[256,640]{1,0:T(8,128)(2,1)S(1)}, u32[]{:S(2)}, u32[]{:S(2)}) collective-permute-start(bf16[256,640]{1,0:T(8,128)(2,1)S(1)} %broadcast_select_fusion.3), channel_id=1, source_target_pairs={{48,32},{56,40},{80,64},{88,72},{112,96},{120,104},{176,160},{184,... | collective-permute-start | bytes 983048 | tf_op jit(solution)/shard_map/ppermute | solution.py:456
  79.8 1.3 collective-permute-start.10
  81.1 1.3 collective-permute-start.20
  82.4 1.3 collective-permute-start.21
  83.9 2.2 collective-permute-done.9.rest_12_.rest_13_
  86.1 1.3 collective-permute-start.22
  87.4 0.7 compare_convert_fusion.valid
  88.1 20.2 %collective-permute-done.10.rest_13_.rest_14_ = bf16[256,640]{1,0:T(8,128)(2,1)S(1)} collective-permute-done((bf16[256,640]{1,0:T(8,128)(2,1)S(1)}, bf16[256,640]{1,0:T(8,128)(2,1)S(1)}, u32[]{:S(2)}, u32[]{:S(2)}) %collective-permute-start.10) | collective-permute-done | bytes 327712 | tf_op jit(solution)/shard_map/ppermute | solution.py:456
  108.3 4.6 %collective-permute-start.29 = (bf16[272,640]{1,0:T(8,128)(2,1)S(1)}, bf16[272,640]{1,0:T(8,128)(2,1)S(1)}, u32[]{:S(2)}, u32[]{:S(2)}) collective-permute-start(bf16[272,640]{1,0:T(8,128)(2,1)S(1)} %fusion.1.rest_0_.rest_2_), channel_id=1, source_target_pairs={{0,64},{8,72},{16,80},{24,88},{32,96},{40,104},{48,112},{56,120},{... | collective-permute-start | bytes 1044488 | tf_op jit(solution)/shard_map/ppermute | solution.py:456
  113.0 0.7 collective-permute-start.31
  113.7 1.6 collective-permute-done.22.rest_26_.rest_27_
  115.3 1.3 collective-permute-start.23
  116.7 6.3 %collective-permute-done.23.rest_27_.rest_28_ = bf16[256,640]{1,0:T(8,128)(2,1)S(1)} collective-permute-done((bf16[256,640]{1,0:T(8,128)(2,1)S(1)}, bf16[256,640]{1,0:T(8,128)(2,1)S(1)}, u32[]{:S(2)}, u32[]{:S(2)}) %collective-permute-start.23) | collective-permute-done | bytes 327712 | tf_op jit(solution)/shard_map/ppermute | solution.py:456
  123.0 6.8 %forward.1 = (f32[256,640]{1,0:T(8,128)S(1)}, f32[16,640]{1,0:T(8,128)S(1)}, f32[2,128]{1,0:T(2,128)S(1)}) custom-call(s32[12]{0:T(128)S(1)} %reshape.20.slots, s32[12]{0:T(128)S(1)} %reshape.21.counts, s32[13]{0:T(128)S(1)} %convert_element_type.12.used, bf16[256,640]{1,0:T(8,128)(2,1)S(1)} %copy-done.2, bf16[256,640]{1,0:T(8,128)(2,1)S(1)} %copy-done.3, ...), custom_call_target="tpu_custom_call" | custom-call | tf_op jit(solution)/shard_map/forward/pallas_call | solution.py:508
  129.7 1.7 collective-permute-start.24
  131.4 0.8 collective-permute-done.24
  132.2 9.0 %collective-permute-start.25 = (f32[2,128]{1,0:T(2,128)S(1)}, f32[2,128]{1,0:T(2,128)S(1)}, u32[]{:S(2)}, u32[]{:S(2)}) collective-permute-start(f32[2,128]{1,0:T(2,128)S(1)} %add.49), channel_id=1, source_target_pairs={{0,2},{1,3},{2,0},{3,1},{4,6},{5,7},{6,4},{7,5},{8,10},{9,11},{10,... | collective-permute-start | bytes 3080 | tf_op jit(solution)/shard_map/ppermute | solution.py:525
  141.2 1.0 collective-permute-done.25
  142.2 2.1 collective-permute-start.26
  144.3 3.4 %collective-permute-start.32 = (bf16[272,640]{1,0:T(8,128)(2,1)S(1)}, bf16[272,640]{1,0:T(8,128)(2,1)S(1)}, u32[]{:S(2)}, u32[]{:S(2)}) collective-permute-start(bf16[272,640]{1,0:T(8,128)(2,1)S(1)} %fusion.1.rest_0_.rest_2_), channel_id=1, source_target_pairs={{0,16},{8,24},{16,0},{24,8},{32,48},{40,56},{48,32},{56,40},{64,80... | collective-permute-start | bytes 1044488 | tf_op jit(solution)/shard_map/ppermute | solution.py:456
  147.7 0.9 collective-permute-start.33
  148.6 0.7 collective-permute-start.34
  149.3 1.3 collective-permute-start.28
  150.6 1.3 collective-permute-start.35
  152.0 0.9 upstream.1.rest_1_.rest_15_
  153.0 1.5 collective-permute-done.32.rest_6_.rest_8_
  154.5 1.3 collective-permute-start.36
  155.8 6.8 %collective-permute-done.33.rest_7_.rest_9_ = bf16[272,640]{1,0:T(8,128)(2,1)S(1)} collective-permute-done((bf16[272,640]{1,0:T(8,128)(2,1)S(1)}, bf16[272,640]{1,0:T(8,128)(2,1)S(1)}, u32[]{:S(2)}, u32[]{:S(2)}) %collective-permute-start.33) | collective-permute-done | bytes 348192 | tf_op jit(solution)/shard_map/ppermute | solution.py:456
  162.5 1.3 collective-permute-start.37
  163.8 4.8 %collective-permute-start.38 = (bf16[272,640]{1,0:T(8,128)(2,1)S(1)}, bf16[272,640]{1,0:T(8,128)(2,1)S(1)}, u32[]{:S(2)}, u32[]{:S(2)}) collective-permute-start(bf16[272,640]{1,0:T(8,128)(2,1)S(1)} %broadcast_select_fusion.1), channel_id=1, source_target_pairs={{48,32},{56,40},{80,64},{88,72},{112,96},{120,104},{176,160},{184,... | collective-permute-start | bytes 1044488 | tf_op jit(solution)/shard_map/ppermute | solution.py:456
  169.2 8.2 %collective-permute-done.35.rest_9_.rest_11_ = bf16[272,640]{1,0:T(8,128)(2,1)S(1)} collective-permute-done((bf16[272,640]{1,0:T(8,128)(2,1)S(1)}, bf16[272,640]{1,0:T(8,128)(2,1)S(1)}, u32[]{:S(2)}, u32[]{:S(2)}) %collective-permute-start.35) | collective-permute-done | bytes 348192 | tf_op jit(solution)/shard_map/ppermute | solution.py:456
  177.4 0.7 collective-permute-start.43
  178.2 10.4 %collective-permute-done.37.rest_11_.rest_13_ = bf16[272,640]{1,0:T(8,128)(2,1)S(1)} collective-permute-done((bf16[272,640]{1,0:T(8,128)(2,1)S(1)}, bf16[272,640]{1,0:T(8,128)(2,1)S(1)}, u32[]{:S(2)}, u32[]{:S(2)}) %collective-permute-start.37) | collective-permute-done | bytes 348192 | tf_op jit(solution)/shard_map/ppermute | solution.py:456
  188.6 1.9 collective-permute-start.40
  190.9 1.3 collective-permute-done.39.rest_16_
  192.2 0.7 collective-permute-start.46
  192.8 17.6 %collective-permute-done.40.rest_17_ = bf16[272,640]{1,0:T(8,128)(2,1)S(1)} collective-permute-done((bf16[272,640]{1,0:T(8,128)(2,1)S(1)}, bf16[272,640]{1,0:T(8,128)(2,1)S(1)}, u32[]{:S(2)}, u32[]{:S(2)}) %collective-permute-start.40) | collective-permute-done | bytes 348192 | tf_op jit(solution)/shard_map/ppermute | solution.py:456
  210.4 1.3 collective-permute-start.47
  211.7 4.5 %collective-permute-done.41.rest_18_ = bf16[272,640]{1,0:T(8,128)(2,1)S(1)} collective-permute-done((bf16[272,640]{1,0:T(8,128)(2,1)S(1)}, bf16[272,640]{1,0:T(8,128)(2,1)S(1)}, u32[]{:S(2)}, u32[]{:S(2)}) %collective-permute-start.41) | collective-permute-done | bytes 348192 | tf_op jit(solution)/shard_map/ppermute | solution.py:456
  216.2 1.3 collective-permute-start.48
  217.5 1.3 collective-permute-start.49
  218.8 1.3 collective-permute-start.50
  220.2 7.8 %grad_queries.1 = bf16[256,640]{1,0:T(8,128)(2,1)} custom-call(s32[12]{0:T(128)S(1)} %reshape.20.slots, s32[12]{0:T(128)S(1)} %reshape.21.counts, s32[13]{0:T(128)S(1)} %convert_element_type.12.used, bf16[256,640]{1,0:T(8,128)(2,1)S(1)} %copy-done.2, bf16[272,640]{1,0:T(8,128)(2,1)S(1)} %upstream.1.rest_1_.rest_15_, ...), custom_call_target="tpu_custom_call" | custom-call | tf_op jit(solution)/shard_map/grad_queries/pallas_call | solution.py:552
  228.0 0.8 naming.1.names
  228.8 16.7 %collective-permute-done.49.rest_26_ = bf16[272,640]{1,0:T(8,128)(2,1)S(1)} collective-permute-done((bf16[272,640]{1,0:T(8,128)(2,1)S(1)}, bf16[272,640]{1,0:T(8,128)(2,1)S(1)}, u32[]{:S(2)}, u32[]{:S(2)}) %collective-permute-start.49) | collective-permute-done | bytes 348192 | tf_op jit(solution)/shard_map/ppermute | solution.py:456
  245.5 10.6 %grad_keys_values.1 = (bf16[256,640]{1,0:T(8,128)(2,1)}, bf16[256,640]{1,0:T(8,128)(2,1)}) custom-call(s32[16,128]{1,0:T(8,128)S(1)} %naming.1.names, s32[2]{0:T(128)S(1)} %fusion.7.counts, bf16[256,640]{1,0:T(8,128)(2,1)S(1)} %copy-done, bf16[256,640]{1,0:T(8,128)(2,1)S(1)} %copy-done.1, bf16[272,640]{1,0:T(8,128)(2,1)S(1)} %fusion.1.rest_0_.rest_2_, ...), custom_call_target="tpu_custom_call" | custom-call | tf_op jit(solution)/shard_map/grad_keys_values/pallas_call | solution.py:564
  (83 shorter events, 3.3 us)
Async XLA Ops:
  0.6 18.8 %collective-permute-start = (bf16[256,640]{1,0:T(8,128)(2,1)}, bf16[256,640]{1,0:T(8,128)(2,1)S(1)}, u32[]{:S(2)}, u32[]{:S(2)}) collective-permute-start(bf16[256,640]{1,0:T(8,128)(2,1)} %rest_0_.5), channel_id=1, source_target_pairs={{0,128},{8,136},{16,144},{24,152},{32,160},{40,168},{48,176},{56,1... | collective-permute-start | bytes 983048 | tf_op jit(solution)/shard_map/ppermute | solution.py:456
  1.9 28.1 %collective-permute-start.1 = (bf16[256,640]{1,0:T(8,128)(2,1)}, bf16[256,640]{1,0:T(8,128)(2,1)S(1)}, u32[]{:S(2)}, u32[]{:S(2)}) collective-permute-start(bf16[256,640]{1,0:T(8,128)(2,1)} %rest_0_.5), channel_id=1, source_target_pairs={{64,128},{128,64},{72,136},{136,72},{80,144},{144,80},{88,152},{15... | collective-permute-start | bytes 983048 | tf_op jit(solution)/shard_map/ppermute | solution.py:456
  10.6 21.4 %collective-permute-start.2 = (bf16[256,640]{1,0:T(8,128)(2,1)}, bf16[256,640]{1,0:T(8,128)(2,1)S(1)}, u32[]{:S(2)}, u32[]{:S(2)}) collective-permute-start(bf16[256,640]{1,0:T(8,128)(2,1)} %rest_0_.5), channel_id=1, source_target_pairs={{0,64},{8,72},{16,80},{24,88},{32,96},{40,104},{48,112},{56,120},{... | collective-permute-start | bytes 983048 | tf_op jit(solution)/shard_map/ppermute | solution.py:456
  10.7 22.2 %collective-permute-start.3 = (bf16[256,640]{1,0:T(8,128)(2,1)}, bf16[256,640]{1,0:T(8,128)(2,1)S(1)}, u32[]{:S(2)}, u32[]{:S(2)}) collective-permute-start(bf16[256,640]{1,0:T(8,128)(2,1)} %rest_0_.5), channel_id=1, source_target_pairs={{0,32},{8,40},{16,48},{24,56},{32,0},{40,8},{48,16},{56,24},{64,96... | collective-permute-start | bytes 983048 | tf_op jit(solution)/shard_map/ppermute | solution.py:456
  11.2 28.0 %collective-permute-start.4 = (bf16[256,640]{1,0:T(8,128)(2,1)}, bf16[256,640]{1,0:T(8,128)(2,1)S(1)}, u32[]{:S(2)}, u32[]{:S(2)}) collective-permute-start(bf16[256,640]{1,0:T(8,128)(2,1)} %rest_0_.5), channel_id=1, source_target_pairs={{32,64},{64,32},{40,72},{72,40},{48,80},{80,48},{56,88},{88,56},{1... | collective-permute-start | bytes 983048 | tf_op jit(solution)/shard_map/ppermute | solution.py:456
  19.4 25.6 %collective-permute-start.5 = (bf16[256,640]{1,0:T(8,128)(2,1)}, bf16[256,640]{1,0:T(8,128)(2,1)S(1)}, u32[]{:S(2)}, u32[]{:S(2)}) collective-permute-start(bf16[256,640]{1,0:T(8,128)(2,1)} %rest_0_.5), channel_id=1, source_target_pairs={{0,16},{8,24},{16,0},{24,8},{32,48},{40,56},{48,32},{56,40},{64,80... | collective-permute-start | bytes 983048 | tf_op jit(solution)/shard_map/ppermute | solution.py:456
  30.0 15.1 %collective-permute-start.6 = (bf16[256,640]{1,0:T(8,128)(2,1)}, bf16[256,640]{1,0:T(8,128)(2,1)S(1)}, u32[]{:S(2)}, u32[]{:S(2)}) collective-permute-start(bf16[256,640]{1,0:T(8,128)(2,1)} %rest_0_.5), channel_id=1, source_target_pairs={{0,8},{8,0},{16,24},{24,16},{32,40},{40,32},{48,56},{56,48},{64,72... | collective-permute-start | bytes 983048 | tf_op jit(solution)/shard_map/ppermute | solution.py:456
  32.0 17.8 %collective-permute-start.7 = (bf16[256,640]{1,0:T(8,128)(2,1)}, bf16[256,640]{1,0:T(8,128)(2,1)S(1)}, u32[]{:S(2)}, u32[]{:S(2)}) collective-permute-start(bf16[256,640]{1,0:T(8,128)(2,1)} %rest_0_.5), channel_id=1, source_target_pairs={{8,16},{16,8},{24,32},{32,24},{40,48},{48,40},{56,64},{64,56},{72,... | collective-permute-start | bytes 983048 | tf_op jit(solution)/shard_map/ppermute | solution.py:456
  33.0 16.6 %copy-start.5 = (s32[2,6]{1,0:T(2,128)S(1)}, s32[2,6]{1,0:T(2,128)}, u32[]{:S(2)}) copy-start(s32[2,6]{1,0:T(2,128)} %param.13) | copy-start | bytes 148
  33.0 18.1 %collective-permute-start.12 = (bf16[256,640]{1,0:T(8,128)(2,1)}, bf16[256,640]{1,0:T(8,128)(2,1)}, u32[]{:S(2)}, u32[]{:S(2)}) collective-permute-start(bf16[256,640]{1,0:T(8,128)(2,1)} %rest_1_.3), channel_id=1, source_target_pairs={{0,128},{8,136},{16,144},{24,152},{32,160},{40,168},{48,176},{56,1... | collective-permute-start | bytes 983048 | tf_op jit(solution)/shard_map/ppermute | solution.py:456
  39.2 25.3 %collective-permute-start.13 = (bf16[256,640]{1,0:T(8,128)(2,1)}, bf16[256,640]{1,0:T(8,128)(2,1)}, u32[]{:S(2)}, u32[]{:S(2)}) collective-permute-start(bf16[256,640]{1,0:T(8,128)(2,1)} %rest_1_.3), channel_id=1, source_target_pairs={{64,128},{128,64},{72,136},{136,72},{80,144},{144,80},{88,152},{15... | collective-permute-start | bytes 983048 | tf_op jit(solution)/shard_map/ppermute | solution.py:456
  45.0 19.5 %collective-permute-start.14 = (bf16[256,640]{1,0:T(8,128)(2,1)}, bf16[256,640]{1,0:T(8,128)(2,1)}, u32[]{:S(2)}, u32[]{:S(2)}) collective-permute-start(bf16[256,640]{1,0:T(8,128)(2,1)} %rest_1_.3), channel_id=1, source_target_pairs={{0,64},{8,72},{16,80},{24,88},{32,96},{40,104},{48,112},{56,120},{... | collective-permute-start | bytes 983048 | tf_op jit(solution)/shard_map/ppermute | solution.py:456
  45.1 20.0 %collective-permute-start.15 = (bf16[256,640]{1,0:T(8,128)(2,1)}, bf16[256,640]{1,0:T(8,128)(2,1)S(1)}, u32[]{:S(2)}, u32[]{:S(2)}) collective-permute-start(bf16[256,640]{1,0:T(8,128)(2,1)} %rest_1_.3), channel_id=1, source_target_pairs={{0,32},{8,40},{16,48},{24,56},{32,0},{40,8},{48,16},{56,24},{64,96... | collective-permute-start | bytes 983048 | tf_op jit(solution)/shard_map/ppermute | solution.py:456
  49.7 0.8 copy-start.6
  49.8 16.6 %collective-permute-start.16 = (bf16[256,640]{1,0:T(8,128)(2,1)}, bf16[256,640]{1,0:T(8,128)(2,1)S(1)}, u32[]{:S(2)}, u32[]{:S(2)}) collective-permute-start(bf16[256,640]{1,0:T(8,128)(2,1)} %rest_1_.3), channel_id=1, source_target_pairs={{32,64},{64,32},{40,72},{72,40},{48,80},{80,48},{56,88},{88,56},{1... | collective-permute-start | bytes 983048 | tf_op jit(solution)/shard_map/ppermute | solution.py:456
  51.1 16.9 %collective-permute-start.17 = (bf16[256,640]{1,0:T(8,128)(2,1)}, bf16[256,640]{1,0:T(8,128)(2,1)S(1)}, u32[]{:S(2)}, u32[]{:S(2)}) collective-permute-start(bf16[256,640]{1,0:T(8,128)(2,1)} %rest_1_.3), channel_id=1, source_target_pairs={{0,16},{8,24},{16,0},{24,8},{32,48},{40,56},{48,32},{56,40},{64,80... | collective-permute-start | bytes 983048 | tf_op jit(solution)/shard_map/ppermute | solution.py:456
  64.4 15.3 %collective-permute-start.18 = (bf16[256,640]{1,0:T(8,128)(2,1)}, bf16[256,640]{1,0:T(8,128)(2,1)S(1)}, u32[]{:S(2)}, u32[]{:S(2)}) collective-permute-start(bf16[256,640]{1,0:T(8,128)(2,1)} %rest_1_.3), channel_id=1, source_target_pairs={{0,8},{8,0},{16,24},{24,16},{32,40},{40,32},{48,56},{56,48},{64,72... | collective-permute-start | bytes 983048 | tf_op jit(solution)/shard_map/ppermute | solution.py:456
  64.5 16.6 %collective-permute-start.19 = (bf16[256,640]{1,0:T(8,128)(2,1)}, bf16[256,640]{1,0:T(8,128)(2,1)S(1)}, u32[]{:S(2)}, u32[]{:S(2)}) collective-permute-start(bf16[256,640]{1,0:T(8,128)(2,1)} %rest_1_.3), channel_id=1, source_target_pairs={{8,16},{16,8},{24,32},{32,24},{40,48},{48,40},{56,64},{64,56},{72,... | collective-permute-start | bytes 983048 | tf_op jit(solution)/shard_map/ppermute | solution.py:456
  65.1 17.2 %collective-permute-start.8 = (bf16[256,640]{1,0:T(8,128)(2,1)S(1)}, bf16[256,640]{1,0:T(8,128)(2,1)S(1)}, u32[]{:S(2)}, u32[]{:S(2)}) collective-permute-start(bf16[256,640]{1,0:T(8,128)(2,1)S(1)} %collective-permute-done.rest_3_.rest_4_), channel_id=1, source_target_pairs={{224,128},{232,136},{240,144},{248,152},{0,96},{8,104},{16,112},{2... | collective-permute-start | bytes 983048 | tf_op jit(solution)/shard_map/ppermute | solution.py:456
  66.5 17.4 %copy-start.2 = (bf16[256,640]{1,0:T(8,128)(2,1)S(1)}, bf16[256,640]{1,0:T(8,128)(2,1)}, u32[]{:S(2)}) copy-start(bf16[256,640]{1,0:T(8,128)(2,1)} %rest_0_.4) | copy-start | bytes 983044
  66.5 19.6 %collective-permute-start.9 = (bf16[256,640]{1,0:T(8,128)(2,1)S(1)}, bf16[256,640]{1,0:T(8,128)(2,1)S(1)}, u32[]{:S(2)}, u32[]{:S(2)}) collective-permute-start(bf16[256,640]{1,0:T(8,128)(2,1)S(1)} %collective-permute-done.1.rest_4_.rest_5_), channel_id=1, source_target_pairs={{176,128},{184,136},{64,112},{72,120},{177,129},{185,137},{65,113}... | collective-permute-start | bytes 983048 | tf_op jit(solution)/shard_map/ppermute | solution.py:456
  68.0 40.4 %collective-permute-start.11 = (bf16[256,640]{1,0:T(8,128)(2,1)S(1)}, bf16[256,640]{1,0:T(8,128)(2,1)S(1)}, u32[]{:S(2)}, u32[]{:S(2)}) collective-permute-start(bf16[256,640]{1,0:T(8,128)(2,1)S(1)} %broadcast_select_fusion.3), channel_id=1, source_target_pairs={{48,32},{56,40},{80,64},{88,72},{112,96},{120,104},{176,160},{184,... | collective-permute-start | bytes 983048 | tf_op jit(solution)/shard_map/ppermute | solution.py:456
  79.8 28.6 %collective-permute-start.10 = (bf16[256,640]{1,0:T(8,128)(2,1)S(1)}, bf16[256,640]{1,0:T(8,128)(2,1)S(1)}, u32[]{:S(2)}, u32[]{:S(2)}) collective-permute-start(bf16[256,640]{1,0:T(8,128)(2,1)S(1)} %collective-permute-done.1.rest_4_.rest_5_), channel_id=1, source_target_pairs={{184,128},{64,120},{185,129},{65,121},{186,130},{66,122},{187,131}... | collective-permute-start | bytes 983048 | tf_op jit(solution)/shard_map/ppermute | solution.py:456
  81.1 31.9 %collective-permute-start.20 = (bf16[256,640]{1,0:T(8,128)(2,1)}, bf16[256,640]{1,0:T(8,128)(2,1)S(1)}, u32[]{:S(2)}, u32[]{:S(2)}) collective-permute-start(bf16[256,640]{1,0:T(8,128)(2,1)} %collective-permute-done.12.rest_16_.rest_17_), channel_id=1, source_target_pairs={{224,128},{232,136},{240,144},{248,152},{0,96},{8,104},{16,112},{2... | collective-permute-start | bytes 983048 | tf_op jit(solution)/shard_map/ppermute | solution.py:456
  82.4 30.6 %collective-permute-start.21 = (bf16[256,640]{1,0:T(8,128)(2,1)}, bf16[256,640]{1,0:T(8,128)(2,1)S(1)}, u32[]{:S(2)}, u32[]{:S(2)}) collective-permute-start(bf16[256,640]{1,0:T(8,128)(2,1)} %collective-permute-done.13.rest_17_.rest_18_), channel_id=1, source_target_pairs={{176,128},{184,136},{64,112},{72,120},{177,129},{185,137},{65,113}... | collective-permute-start | bytes 983048 | tf_op jit(solution)/shard_map/ppermute | solution.py:456
  86.1 29.3 %collective-permute-start.22 = (bf16[256,640]{1,0:T(8,128)(2,1)}, bf16[256,640]{1,0:T(8,128)(2,1)S(1)}, u32[]{:S(2)}, u32[]{:S(2)}) collective-permute-start(bf16[256,640]{1,0:T(8,128)(2,1)} %collective-permute-done.13.rest_17_.rest_18_), channel_id=1, source_target_pairs={{184,128},{64,120},{185,129},{65,121},{186,130},{66,122},{187,131}... | collective-permute-start | bytes 983048 | tf_op jit(solution)/shard_map/ppermute | solution.py:456
  88.1 34.9 %copy-start = (bf16[256,640]{1,0:T(8,128)(2,1)S(1)}, bf16[256,640]{1,0:T(8,128)(2,1)}, u32[]{:S(2)}) copy-start(bf16[256,640]{1,0:T(8,128)(2,1)} %rest_0_.5) | copy-start | bytes 983044
  88.1 34.9 %copy-start.1 = (bf16[256,640]{1,0:T(8,128)(2,1)S(1)}, bf16[256,640]{1,0:T(8,128)(2,1)}, u32[]{:S(2)}) copy-start(bf16[256,640]{1,0:T(8,128)(2,1)} %rest_1_.3) | copy-start | bytes 983044
  88.1 34.9 %copy-start.3 = (bf16[256,640]{1,0:T(8,128)(2,1)S(1)}, bf16[256,640]{1,0:T(8,128)(2,1)}, u32[]{:S(2)}) copy-start(bf16[256,640]{1,0:T(8,128)(2,1)} %rest_3_.2) | copy-start | bytes 983044
  108.3 36.0 %collective-permute-start.27 = (bf16[272,640]{1,0:T(8,128)(2,1)S(1)}, bf16[272,640]{1,0:T(8,128)(2,1)S(1)}, u32[]{:S(2)}, u32[]{:S(2)}) collective-permute-start(bf16[272,640]{1,0:T(8,128)(2,1)S(1)} %fusion.1.rest_0_.rest_2_), channel_id=1, source_target_pairs={{0,128},{8,136},{16,144},{24,152},{32,160},{40,168},{48,176},{56,1... | collective-permute-start | bytes 1044488 | tf_op jit(solution)/shard_map/ppermute | solution.py:456
  108.3 39.4 %collective-permute-start.29 = (bf16[272,640]{1,0:T(8,128)(2,1)S(1)}, bf16[272,640]{1,0:T(8,128)(2,1)S(1)}, u32[]{:S(2)}, u32[]{:S(2)}) collective-permute-start(bf16[272,640]{1,0:T(8,128)(2,1)S(1)} %fusion.1.rest_0_.rest_2_), channel_id=1, source_target_pairs={{0,64},{8,72},{16,80},{24,88},{32,96},{40,104},{48,112},{56,120},{... | collective-permute-start | bytes 1044488 | tf_op jit(solution)/shard_map/ppermute | solution.py:456
  113.0 35.7 %collective-permute-start.30 = (bf16[272,640]{1,0:T(8,128)(2,1)S(1)}, bf16[272,640]{1,0:T(8,128)(2,1)S(1)}, u32[]{:S(2)}, u32[]{:S(2)}) collective-permute-start(bf16[272,640]{1,0:T(8,128)(2,1)S(1)} %fusion.1.rest_0_.rest_2_), channel_id=1, source_target_pairs={{0,32},{8,40},{16,48},{24,56},{32,0},{40,8},{48,16},{56,24},{64,96... | collective-permute-start | bytes 1044488 | tf_op jit(solution)/shard_map/ppermute | solution.py:456
  113.0 36.3 %collective-permute-start.31 = (bf16[272,640]{1,0:T(8,128)(2,1)S(1)}, bf16[272,640]{1,0:T(8,128)(2,1)S(1)}, u32[]{:S(2)}, u32[]{:S(2)}) collective-permute-start(bf16[272,640]{1,0:T(8,128)(2,1)S(1)} %fusion.1.rest_0_.rest_2_), channel_id=1, source_target_pairs={{32,64},{64,32},{40,72},{72,40},{48,80},{80,48},{56,88},{88,56},{1... | collective-permute-start | bytes 1044488 | tf_op jit(solution)/shard_map/ppermute | solution.py:456
  115.3 7.6 %collective-permute-start.23 = (bf16[256,640]{1,0:T(8,128)(2,1)S(1)}, bf16[256,640]{1,0:T(8,128)(2,1)S(1)}, u32[]{:S(2)}, u32[]{:S(2)}) collective-permute-start(bf16[256,640]{1,0:T(8,128)(2,1)S(1)} %broadcast_select_fusion.2), channel_id=1, source_target_pairs={{48,32},{56,40},{80,64},{88,72},{112,96},{120,104},{176,160},{184,... | collective-permute-start | bytes 983048 | tf_op jit(solution)/shard_map/ppermute | solution.py:456
  129.7 2.5 collective-permute-start.24
  132.2 9.9 %collective-permute-start.25 = (f32[2,128]{1,0:T(2,128)S(1)}, f32[2,128]{1,0:T(2,128)S(1)}, u32[]{:S(2)}, u32[]{:S(2)}) collective-permute-start(f32[2,128]{1,0:T(2,128)S(1)} %add.49), channel_id=1, source_target_pairs={{0,2},{1,3},{2,0},{3,1},{4,6},{5,7},{6,4},{7,5},{8,10},{9,11},{10,... | collective-permute-start | bytes 3080 | tf_op jit(solution)/shard_map/ppermute | solution.py:525
  142.2 9.8 %copy-start.4 = (bf16[256,640]{1,0:T(8,128)(2,1)S(1)}, bf16[256,640]{1,0:T(8,128)(2,1)}, u32[]{:S(2)}) copy-start(bf16[256,640]{1,0:T(8,128)(2,1)} %rest_2_.3) | copy-start | bytes 983044
  142.2 8.5 %collective-permute-start.26 = (f32[2,128]{1,0:T(2,128)S(1)}, f32[2,128]{1,0:T(2,128)S(1)}, u32[]{:S(2)}, u32[]{:S(2)}) collective-permute-start(f32[2,128]{1,0:T(2,128)S(1)} %add.50), channel_id=1, source_target_pairs={{0,4},{1,5},{2,6},{3,7},{4,0},{5,1},{6,2},{7,3},{8,12},{9,13},{10,... | collective-permute-start | bytes 3080 | tf_op jit(solution)/shard_map/ppermute | solution.py:525
  144.3 10.2 %collective-permute-start.32 = (bf16[272,640]{1,0:T(8,128)(2,1)S(1)}, bf16[272,640]{1,0:T(8,128)(2,1)S(1)}, u32[]{:S(2)}, u32[]{:S(2)}) collective-permute-start(bf16[272,640]{1,0:T(8,128)(2,1)S(1)} %fusion.1.rest_0_.rest_2_), channel_id=1, source_target_pairs={{0,16},{8,24},{16,0},{24,8},{32,48},{40,56},{48,32},{56,40},{64,80... | collective-permute-start | bytes 1044488 | tf_op jit(solution)/shard_map/ppermute | solution.py:456
  147.7 14.8 %collective-permute-start.33 = (bf16[272,640]{1,0:T(8,128)(2,1)S(1)}, bf16[272,640]{1,0:T(8,128)(2,1)S(1)}, u32[]{:S(2)}, u32[]{:S(2)}) collective-permute-start(bf16[272,640]{1,0:T(8,128)(2,1)S(1)} %fusion.1.rest_0_.rest_2_), channel_id=1, source_target_pairs={{0,8},{8,0},{16,24},{24,16},{32,40},{40,32},{48,56},{56,48},{64,72... | collective-permute-start | bytes 1044488 | tf_op jit(solution)/shard_map/ppermute | solution.py:456
  148.6 15.2 %collective-permute-start.34 = (bf16[272,640]{1,0:T(8,128)(2,1)S(1)}, bf16[272,640]{1,0:T(8,128)(2,1)S(1)}, u32[]{:S(2)}, u32[]{:S(2)}) collective-permute-start(bf16[272,640]{1,0:T(8,128)(2,1)S(1)} %fusion.1.rest_0_.rest_2_), channel_id=1, source_target_pairs={{8,16},{16,8},{24,32},{32,24},{40,48},{48,40},{56,64},{64,56},{72,... | collective-permute-start | bytes 1044488 | tf_op jit(solution)/shard_map/ppermute | solution.py:456
  149.3 19.9 %collective-permute-start.28 = (bf16[272,640]{1,0:T(8,128)(2,1)S(1)}, bf16[272,640]{1,0:T(8,128)(2,1)S(1)}, u32[]{:S(2)}, u32[]{:S(2)}) collective-permute-start(bf16[272,640]{1,0:T(8,128)(2,1)S(1)} %collective-permute-done.27.rest_1_.rest_3_), channel_id=1, source_target_pairs={{192,128},{200,136},{208,144},{216,152},{224,160},{232,168},{240,1... | collective-permute-start | bytes 1044488 | tf_op jit(solution)/shard_map/ppermute | solution.py:456
  150.6 26.8 %collective-permute-start.35 = (bf16[272,640]{1,0:T(8,128)(2,1)S(1)}, bf16[272,640]{1,0:T(8,128)(2,1)S(1)}, u32[]{:S(2)}, u32[]{:S(2)}) collective-permute-start(bf16[272,640]{1,0:T(8,128)(2,1)S(1)} %collective-permute-done.27.rest_1_.rest_3_), channel_id=1, source_target_pairs={{224,128},{232,136},{240,144},{248,152},{0,96},{8,104},{16,112},{2... | collective-permute-start | bytes 1044488 | tf_op jit(solution)/shard_map/ppermute | solution.py:456
  154.5 23.6 %collective-permute-start.36 = (bf16[272,640]{1,0:T(8,128)(2,1)S(1)}, bf16[272,640]{1,0:T(8,128)(2,1)S(1)}, u32[]{:S(2)}, u32[]{:S(2)}) collective-permute-start(bf16[272,640]{1,0:T(8,128)(2,1)S(1)} %collective-permute-done.27.rest_1_.rest_3_), channel_id=1, source_target_pairs={{240,128},{248,136},{0,112},{8,120},{241,129},{249,137},{1,113},{9... | collective-permute-start | bytes 1044488 | tf_op jit(solution)/shard_map/ppermute | solution.py:456
  162.5 26.0 %collective-permute-start.37 = (bf16[272,640]{1,0:T(8,128)(2,1)S(1)}, bf16[272,640]{1,0:T(8,128)(2,1)S(1)}, u32[]{:S(2)}, u32[]{:S(2)}) collective-permute-start(bf16[272,640]{1,0:T(8,128)(2,1)S(1)} %collective-permute-done.27.rest_1_.rest_3_), channel_id=1, source_target_pairs={{248,128},{0,120},{249,129},{1,121},{250,130},{2,122},{251,131},{3... | collective-permute-start | bytes 1044488 | tf_op jit(solution)/shard_map/ppermute | solution.py:456
  163.8 26.6 %collective-permute-start.38 = (bf16[272,640]{1,0:T(8,128)(2,1)S(1)}, bf16[272,640]{1,0:T(8,128)(2,1)S(1)}, u32[]{:S(2)}, u32[]{:S(2)}) collective-permute-start(bf16[272,640]{1,0:T(8,128)(2,1)S(1)} %broadcast_select_fusion.1), channel_id=1, source_target_pairs={{48,32},{56,40},{80,64},{88,72},{112,96},{120,104},{176,160},{184,... | collective-permute-start | bytes 1044488 | tf_op jit(solution)/shard_map/ppermute | solution.py:456
  169.2 21.4 %collective-permute-start.42 = (bf16[272,640]{1,0:T(8,128)(2,1)S(1)}, bf16[272,640]{1,0:T(8,128)(2,1)S(1)}, u32[]{:S(2)}, u32[]{:S(2)}) collective-permute-start(bf16[272,640]{1,0:T(8,128)(2,1)S(1)} %upstream.1.rest_1_.rest_15_), channel_id=1, source_target_pairs={{0,32},{8,40},{16,48},{24,56},{32,0},{40,8},{48,16},{56,24},{64,96... | collective-permute-start | bytes 1044488 | tf_op jit(solution)/shard_map/ppermute | solution.py:456
  177.4 13.3 %collective-permute-start.43 = (bf16[272,640]{1,0:T(8,128)(2,1)S(1)}, bf16[272,640]{1,0:T(8,128)(2,1)S(1)}, u32[]{:S(2)}, u32[]{:S(2)}) collective-permute-start(bf16[272,640]{1,0:T(8,128)(2,1)S(1)} %upstream.1.rest_1_.rest_15_), channel_id=1, source_target_pairs={{32,64},{64,32},{40,72},{72,40},{48,80},{80,48},{56,88},{88,56},{1... | collective-permute-start | bytes 1044488 | tf_op jit(solution)/shard_map/ppermute | solution.py:456
  178.1 14.1 %collective-permute-start.39 = (bf16[272,640]{1,0:T(8,128)(2,1)S(1)}, bf16[272,640]{1,0:T(8,128)(2,1)S(1)}, u32[]{:S(2)}, u32[]{:S(2)}) collective-permute-start(bf16[272,640]{1,0:T(8,128)(2,1)S(1)} %upstream.1.rest_1_.rest_15_), channel_id=1, source_target_pairs={{0,128},{8,136},{16,144},{24,152},{32,160},{40,168},{48,176},{56,1... | collective-permute-start | bytes 1044488 | tf_op jit(solution)/shard_map/ppermute | solution.py:456
  188.6 21.8 %collective-permute-start.40 = (bf16[272,640]{1,0:T(8,128)(2,1)S(1)}, bf16[272,640]{1,0:T(8,128)(2,1)S(1)}, u32[]{:S(2)}, u32[]{:S(2)}) collective-permute-start(bf16[272,640]{1,0:T(8,128)(2,1)S(1)} %upstream.1.rest_1_.rest_15_), channel_id=1, source_target_pairs={{64,128},{128,64},{72,136},{136,72},{80,144},{144,80},{88,152},{15... | collective-permute-start | bytes 1044488 | tf_op jit(solution)/shard_map/ppermute | solution.py:456
  190.5 25.7 %collective-permute-start.41 = (bf16[272,640]{1,0:T(8,128)(2,1)S(1)}, bf16[272,640]{1,0:T(8,128)(2,1)S(1)}, u32[]{:S(2)}, u32[]{:S(2)}) collective-permute-start(bf16[272,640]{1,0:T(8,128)(2,1)S(1)} %upstream.1.rest_1_.rest_15_), channel_id=1, source_target_pairs={{0,64},{8,72},{16,80},{24,88},{32,96},{40,104},{48,112},{56,120},{... | collective-permute-start | bytes 1044488 | tf_op jit(solution)/shard_map/ppermute | solution.py:456
  190.6 26.9 %collective-permute-start.44 = (bf16[272,640]{1,0:T(8,128)(2,1)S(1)}, bf16[272,640]{1,0:T(8,128)(2,1)S(1)}, u32[]{:S(2)}, u32[]{:S(2)}) collective-permute-start(bf16[272,640]{1,0:T(8,128)(2,1)S(1)} %upstream.1.rest_1_.rest_15_), channel_id=1, source_target_pairs={{0,16},{8,24},{16,0},{24,8},{32,48},{40,56},{48,32},{56,40},{64,80... | collective-permute-start | bytes 1044488 | tf_op jit(solution)/shard_map/ppermute | solution.py:456
  190.7 28.1 %collective-permute-start.45 = (bf16[272,640]{1,0:T(8,128)(2,1)S(1)}, bf16[272,640]{1,0:T(8,128)(2,1)S(1)}, u32[]{:S(2)}, u32[]{:S(2)}) collective-permute-start(bf16[272,640]{1,0:T(8,128)(2,1)S(1)} %upstream.1.rest_1_.rest_15_), channel_id=1, source_target_pairs={{0,8},{8,0},{16,24},{24,16},{32,40},{40,32},{48,56},{56,48},{64,72... | collective-permute-start | bytes 1044488 | tf_op jit(solution)/shard_map/ppermute | solution.py:456
  192.2 36.6 %collective-permute-start.46 = (bf16[272,640]{1,0:T(8,128)(2,1)S(1)}, bf16[272,640]{1,0:T(8,128)(2,1)S(1)}, u32[]{:S(2)}, u32[]{:S(2)}) collective-permute-start(bf16[272,640]{1,0:T(8,128)(2,1)S(1)} %upstream.1.rest_1_.rest_15_), channel_id=1, source_target_pairs={{8,16},{16,8},{24,32},{32,24},{40,48},{48,40},{56,64},{64,56},{72,... | collective-permute-start | bytes 1044488 | tf_op jit(solution)/shard_map/ppermute | solution.py:456
  210.4 18.4 %collective-permute-start.47 = (bf16[272,640]{1,0:T(8,128)(2,1)S(1)}, bf16[272,640]{1,0:T(8,128)(2,1)S(1)}, u32[]{:S(2)}, u32[]{:S(2)}) collective-permute-start(bf16[272,640]{1,0:T(8,128)(2,1)S(1)} %collective-permute-done.39.rest_16_), channel_id=1, source_target_pairs={{224,128},{232,136},{240,144},{248,152},{0,96},{8,104},{16,112},{2... | collective-permute-start | bytes 1044488 | tf_op jit(solution)/shard_map/ppermute | solution.py:456
  216.2 12.6 %collective-permute-start.48 = (bf16[272,640]{1,0:T(8,128)(2,1)S(1)}, bf16[272,640]{1,0:T(8,128)(2,1)S(1)}, u32[]{:S(2)}, u32[]{:S(2)}) collective-permute-start(bf16[272,640]{1,0:T(8,128)(2,1)S(1)} %collective-permute-done.40.rest_17_), channel_id=1, source_target_pairs={{176,128},{184,136},{64,112},{72,120},{177,129},{185,137},{65,113}... | collective-permute-start | bytes 1044488 | tf_op jit(solution)/shard_map/ppermute | solution.py:456
  217.5 28.0 %collective-permute-start.49 = (bf16[272,640]{1,0:T(8,128)(2,1)S(1)}, bf16[272,640]{1,0:T(8,128)(2,1)S(1)}, u32[]{:S(2)}, u32[]{:S(2)}) collective-permute-start(bf16[272,640]{1,0:T(8,128)(2,1)S(1)} %collective-permute-done.40.rest_17_), channel_id=1, source_target_pairs={{184,128},{64,120},{185,129},{65,121},{186,130},{66,122},{187,131}... | collective-permute-start | bytes 1044488 | tf_op jit(solution)/shard_map/ppermute | solution.py:456
  218.8 26.7 %collective-permute-start.50 = (bf16[272,640]{1,0:T(8,128)(2,1)S(1)}, bf16[272,640]{1,0:T(8,128)(2,1)S(1)}, u32[]{:S(2)}, u32[]{:S(2)}) collective-permute-start(bf16[272,640]{1,0:T(8,128)(2,1)S(1)} %broadcast_select_fusion), channel_id=1, source_target_pairs={{48,32},{56,40},{80,64},{88,72},{112,96},{120,104},{176,160},{184,... | collective-permute-start | bytes 1044488 | tf_op jit(solution)/shard_map/ppermute | solution.py:456

commit v3 on v2

--- a/solution.py
+++ b/solution.py
@@ -238,32 +238,34 @@
         names[position : position + 1, :] = row.astype(jnp.int32)
 
 
-def key_kernel(names, counts, *rest, classes, scale):
-    keys_in, values_in = rest[:2]
-    query_refs, grad_refs = rest[2 : 2 + classes], rest[2 + classes : 2 + 2 * classes]
-    (
-        grad_keys,
-        grad_values,
+def key_kernel(names, counts, *rest, base, classes, scale):
+    sources = rest[: 2 if base == 0 else 4]
+    rest = rest[len(sources) :]
+    query_refs, grad_refs, rest = rest[:classes], rest[classes : 2 * classes], rest[2 * classes :]
+    if base == 0:
+        (acc_k, acc_v), rest = rest[:2], rest[2:]
+    else:
+        (grad_keys, grad_values, acc_k, acc_v), rest = rest[:4], rest[4:]
+    (
         keys,
         values,
         query_pool,
         grad_pool,
-        acc_k,
-        acc_v,
         entries,
         used,
         sems,
         query_sems,
         grad_sems,
-    ) = rest[2 + 2 * classes :]
+    ) = rest
+    targets = (keys, values) if base == 0 else (keys, values, acc_k, acc_v)
     rows, cols = keys.shape
     blocks = rows // BLK
     height = rows + TAIL
-    bring((keys_in, values_in), (keys, values), sems, 0, True)
+    bring(sources, targets, sems, 0, True)
     for position in range(classes):
-        total = names[position, 0]
+        total = names[base + position, 0]
         for place in range(1, blocks * blocks):
-            total = total + names[position, place]
+            total = total + names[base + position, place]
         used[position] = total
     fetch(query_refs, query_pool, query_sems, used, True)
     fetch(grad_refs, grad_pool, grad_sems, used, True)
@@ -271,16 +273,16 @@
     for block in range(blocks):
 
         def collect(entry, length, block=block):
-            hit = names[entry // blocks, (entry % blocks) * blocks + block]
+            hit = names[base + entry // blocks, (entry % blocks) * blocks + block]
             entries[block, length] = entry
             return length + hit
 
         length = lax.fori_loop(0, classes * blocks, collect, jnp.int32(0))
-        entries[block, length] = 0
         lengths.append(length)
-    acc_k[...] = jnp.zeros_like(acc_k)
-    acc_v[...] = jnp.zeros_like(acc_v)
-    bring((keys_in, values_in), (keys, values), sems, 0, False)
+    if base == 0:
+        acc_k[...] = jnp.zeros_like(acc_k)
+        acc_v[...] = jnp.zeros_like(acc_v)
+    bring(sources, targets, sems, 0, False)
     fetch(query_refs, query_pool, query_sems, used, False)
     fetch(grad_refs, grad_pool, grad_sems, used, False)
     row_in_block = lax.broadcasted_iota(jnp.int32, (BLK, cols), 0)
@@ -293,7 +295,7 @@
             for lane in range(WIDE):
                 index = chunk * WIDE + lane
                 live = index < length
-                entry = jnp.where(live, entries[block, jnp.minimum(index, length)], 0)
+                entry = entries[block, jnp.minimum(index, length - 1)]
                 position, part = entry // blocks, entry % blocks
                 places.append(
                     (
@@ -324,6 +326,8 @@
             return carry
 
         lax.fori_loop(0, (length + WIDE - 1) // WIDE, step, 0)
+        if base == 0:
+            continue
         valid = row_in_block < counts[block]
         grad_keys[key_rows, :] = jnp.where(valid, acc_k[key_rows, :] * scale, 0.0).astype(
             jnp.bfloat16
@@ -366,13 +370,13 @@
 
 DIRECT = [
     ("half", "own", flip(16)),
-    ("step8", "own", carry_pairs(8, any_pair)),
     ("flip8", "own", flip(8)),
     ("flip4", "own", flip(4)),
     ("step4", "own", carry_pairs(4, same_half)),
     ("flip2", "own", flip(2)),
     ("flip1", "own", flip(1)),
     ("step1", "own", carry_pairs(1, same_half)),
+    ("step8", "own", carry_pairs(8, any_pair)),
 ]
 RELAYED = [
     (
@@ -399,6 +403,7 @@
         + [(at(z, y, x), at(z, y, x + 2)) for z, y, x in GRID if y < 3 and x < 2],
     ),
 ]
+EARLY = len(DIRECT) + 1
 NAMES = ["own"] + [name for name, _, _ in DIRECT + RELAYED]
 LIGHT = [flow for flow in DIRECT if flow[0] != "step8"] + [
     (
@@ -561,28 +566,30 @@
         name="grad_queries",
     )(slots, counts, used, queries, grad, attn, *key_pool, *value_pool)
 
-    grad_keys, grad_values = pl.pallas_call(
-        functools.partial(key_kernel, classes=classes, scale=scale),
-        out_shape=(
-            jax.ShapeDtypeStruct((rows, cols), jnp.bfloat16),
-            jax.ShapeDtypeStruct((rows, cols), jnp.bfloat16),
-        ),
-        in_specs=[SMEM, SMEM] + [ANY] * (2 + 2 * classes),
-        out_specs=(VMEM, VMEM),
-        scratch_shapes=[shard(), shard()]
-        + [shard(height=classes * (rows + TAIL))] * 2
-        + [
-            shard(f32),
-            shard(f32),
-            pltpu.SMEM((blocks, 32), jnp.int32),
-            pltpu.SMEM((classes,), jnp.int32),
-            dma(2),
-            dma(classes),
-            dma(classes),
-        ],
-        compiler_params=params,
-        name="grad_keys_values",
-    )(names, own_counts, keys, values, *query_pool, *grad_pool)
+    def key_call(base, count, outs):
+        inputs = 2 if base == 0 else 4
+        return pl.pallas_call(
+            functools.partial(key_kernel, base=base, classes=count, scale=scale),
+            out_shape=(outs, outs),
+            in_specs=[SMEM, SMEM] + [ANY] * (inputs + 2 * count),
+            out_specs=(VMEM, VMEM),
+            scratch_shapes=([] if base == 0 else [shard(f32), shard(f32)])
+            + [shard(), shard()]
+            + [shard(height=count * (rows + TAIL))] * 2
+            + [
+                pltpu.SMEM((blocks, 32), jnp.int32),
+                pltpu.SMEM((count,), jnp.int32),
+                dma(inputs),
+                dma(count),
+                dma(count),
+            ],
+            compiler_params=params,
+        )
+
+    sums = key_call(0, EARLY, jax.ShapeDtypeStruct((rows, cols), f32))(names, own_counts, keys, values, *query_pool[:EARLY], *grad_pool[:EARLY])
+    grad_keys, grad_values = key_call(
+        EARLY, classes - EARLY, jax.ShapeDtypeStruct((rows, cols), jnp.bfloat16)
+    )(names, own_counts, keys, values, *sums, *query_pool[EARLY:], *grad_pool[EARLY:])
     return grad_queries, grad_keys, grad_values
 
 

time: 257 us -> 247 us (0.961)
  the two profiles are of different devices: /device:TPU:225 before, /device:TPU:20 now
where the time goes in v3:
time: 247 us; the launch traced here: 246 us
  starting transfers between devices  164 us (66%)
  waiting for transfers between devices  45.9 us (19%)
  Pallas kernels  30.5 us (12%)
    ppermute x48, starting transfers between devices, spread(): held[name] = lax.ppermute(held[sent], 'frame', pairs)  143 us
    ppermute x48, waiting for transfers between devices, spread(): held[name] = lax.ppermute(held[sent], 'frame', pairs)  43.2 us
    ppermute x3, starting transfers between devices, step(): lax.ppermute(squares, 'head', [(i, i ^ hop) for i in range(heads)])  21.2 us
    pallas_call x1, Pallas kernels, step(): key_call(0, EARLY, jax.ShapeDtypeStruct((rows, cols), f32))  9.71 us
    pallas_call x1, Pallas kernels, step(): pl.pallas_call(functools.partial(query_kernel, classes=classes, list_len=...  7.9 us
    pallas_call x1, Pallas kernels, step(): pl.pallas_call(functools.partial(forward_kernel, classes=classes, list_le...  6.85 us
  transfers between devices with their start and end apart: 51, of which 15 were waited for; matrix products, arithmetic and copies ran while one was open for 1% of the time, Pallas kernels for 11%

profile of v3, /device:TPU:20, one launch (start us, length us, event | category | flops | bytes accessed | tf_op | source)
XLA Modules:
  0.0 246.1 jit_solution(11982527835933316607)
XLA Ops:
  0.6 7.3 %collective-permute-start = (bf16[256,640]{1,0:T(8,128)(2,1)}, bf16[256,640]{1,0:T(8,128)(2,1)S(1)}, u32[]{:S(2)}, u32[]{:S(2)}) collective-permute-start(bf16[256,640]{1,0:T(8,128)(2,1)} %rest_0_.7), channel_id=1, source_target_pairs={{0,128},{8,136},{16,144},{24,152},{32,160},{40,168},{48,176},{56,1... | collective-permute-start | bytes 983048 | tf_op jit(solution)/shard_map/ppermute | solution.py:461
  8.2 2.2 collective-permute-start.2
  10.4 3.5 %collective-permute-start.3 = (bf16[256,640]{1,0:T(8,128)(2,1)}, bf16[256,640]{1,0:T(8,128)(2,1)S(1)}, u32[]{:S(2)}, u32[]{:S(2)}) collective-permute-start(bf16[256,640]{1,0:T(8,128)(2,1)} %rest_0_.7), channel_id=1, source_target_pairs={{32,64},{64,32},{40,72},{72,40},{48,80},{80,48},{56,88},{88,56},{1... | collective-permute-start | bytes 983048 | tf_op jit(solution)/shard_map/ppermute | solution.py:461
  13.9 0.6 collective-permute-start.4
  14.5 0.8 copy.11
  15.3 1.7 collective-permute-done.rest_3_.rest_4_
  17.0 1.2 collective-permute-start.5
  18.2 2.1 collective-permute-done.1.rest_4_.rest_5_
  20.2 2.4 collective-permute-start.6
  22.8 0.7 dynamic-slice_bitcast_fusion
  23.5 1.4 collective-permute-done.2.rest_5_.rest_6_
  24.8 8.6 %collective-permute-start.7 = (bf16[256,640]{1,0:T(8,128)(2,1)}, bf16[256,640]{1,0:T(8,128)(2,1)S(1)}, u32[]{:S(2)}, u32[]{:S(2)}) collective-permute-start(bf16[256,640]{1,0:T(8,128)(2,1)} %rest_0_.7), channel_id=1, source_target_pairs={{64,128},{128,64},{72,136},{136,72},{80,144},{144,80},{88,152},{15... | collective-permute-start | bytes 983048 | tf_op jit(solution)/shard_map/ppermute | solution.py:461
  33.8 2.2 collective-permute-start.13
  36.6 3.3 %collective-permute-start.15 = (bf16[256,640]{1,0:T(8,128)(2,1)}, bf16[256,640]{1,0:T(8,128)(2,1)S(1)}, u32[]{:S(2)}, u32[]{:S(2)}) collective-permute-start(bf16[256,640]{1,0:T(8,128)(2,1)} %rest_1_.5), channel_id=1, source_target_pairs={{32,64},{64,32},{40,72},{72,40},{48,80},{80,48},{56,88},{88,56},{1... | collective-permute-start | bytes 983048 | tf_op jit(solution)/shard_map/ppermute | solution.py:461
  40.2 3.8 %collective-permute-done.7.rest_10_.rest_11_ = bf16[256,640]{1,0:T(8,128)(2,1)S(1)} collective-permute-done((bf16[256,640]{1,0:T(8,128)(2,1)}, bf16[256,640]{1,0:T(8,128)(2,1)S(1)}, u32[]{:S(2)}, u32[]{:S(2)}) %collective-permute-start.7) | collective-permute-done | bytes 327712 | tf_op jit(solution)/shard_map/ppermute | solution.py:461
  44.0 1.8 collective-permute-start.16
  46.4 2.5 %collective-permute-done.12.rest_16_.rest_17_ = bf16[256,640]{1,0:T(8,128)(2,1)} collective-permute-done((bf16[256,640]{1,0:T(8,128)(2,1)}, bf16[256,640]{1,0:T(8,128)(2,1)}, u32[]{:S(2)}, u32[]{:S(2)}) %collective-permute-start.12) | collective-permute-done | bytes 327712 | tf_op jit(solution)/shard_map/ppermute | solution.py:461
  48.9 7.2 %collective-permute-start.17 = (bf16[256,640]{1,0:T(8,128)(2,1)}, bf16[256,640]{1,0:T(8,128)(2,1)S(1)}, u32[]{:S(2)}, u32[]{:S(2)}) collective-permute-start(bf16[256,640]{1,0:T(8,128)(2,1)} %rest_1_.5), channel_id=1, source_target_pairs={{0,8},{8,0},{16,24},{24,16},{32,40},{40,32},{48,56},{56,48},{64,72... | collective-permute-start | bytes 983048 | tf_op jit(solution)/shard_map/ppermute | solution.py:461
  56.1 3.4 %collective-permute-start.18 = (bf16[256,640]{1,0:T(8,128)(2,1)}, bf16[256,640]{1,0:T(8,128)(2,1)S(1)}, u32[]{:S(2)}, u32[]{:S(2)}) collective-permute-start(bf16[256,640]{1,0:T(8,128)(2,1)} %rest_1_.5), channel_id=1, source_target_pairs={{8,16},{16,8},{24,32},{32,24},{40,48},{48,40},{56,64},{64,56},{72,... | collective-permute-start | bytes 983048 | tf_op jit(solution)/shard_map/ppermute | solution.py:461
  59.5 5.3 %collective-permute-start.19 = (bf16[256,640]{1,0:T(8,128)(2,1)}, bf16[256,640]{1,0:T(8,128)(2,1)S(1)}, u32[]{:S(2)}, u32[]{:S(2)}) collective-permute-start(bf16[256,640]{1,0:T(8,128)(2,1)} %rest_1_.5), channel_id=1, source_target_pairs={{64,128},{128,64},{72,136},{136,72},{80,144},{144,80},{88,152},{15... | collective-permute-start | bytes 983048 | tf_op jit(solution)/shard_map/ppermute | solution.py:461
  64.9 0.7 collective-permute-start.8
  65.6 0.8 collective-permute-start.9
  66.5 6.6 %collective-permute-start.11 = (bf16[256,640]{1,0:T(8,128)(2,1)S(1)}, bf16[256,640]{1,0:T(8,128)(2,1)S(1)}, u32[]{:S(2)}, u32[]{:S(2)}) collective-permute-start(bf16[256,640]{1,0:T(8,128)(2,1)S(1)} %broadcast_select_fusion.3), channel_id=1, source_target_pairs={{48,32},{56,40},{80,64},{88,72},{112,96},{120,104},{176,160},{184,... | collective-permute-start | bytes 983048 | tf_op jit(solution)/shard_map/ppermute | solution.py:461
  73.1 0.7 collective-permute-start.10
  73.7 1.4 collective-permute-done.19.rest_23_.rest_24_
  75.1 0.7 collective-permute-start.20
  75.8 0.7 collective-permute-start.21
  76.7 0.7 collective-permute-start.22
  77.4 0.7 compare_convert_fusion.valid
  78.5 4.6 %collective-permute-done.11.rest_14_.rest_15_ = bf16[256,640]{1,0:T(8,128)(2,1)S(1)} collective-permute-done((bf16[256,640]{1,0:T(8,128)(2,1)S(1)}, bf16[256,640]{1,0:T(8,128)(2,1)S(1)}, u32[]{:S(2)}, u32[]{:S(2)}) %collective-permute-start.11) | collective-permute-done | bytes 327712 | tf_op jit(solution)/shard_map/ppermute | solution.py:461
  83.1 8.3 %collective-permute-start.28 = (bf16[272,640]{1,0:T(8,128)(2,1)S(1)}, bf16[272,640]{1,0:T(8,128)(2,1)S(1)}, u32[]{:S(2)}, u32[]{:S(2)}) collective-permute-start(bf16[272,640]{1,0:T(8,128)(2,1)S(1)} %fusion.1.rest_0_.rest_2_), channel_id=1, source_target_pairs={{0,64},{8,72},{16,80},{24,88},{32,96},{40,104},{48,112},{56,120},{... | collective-permute-start | bytes 1044488 | tf_op jit(solution)/shard_map/ppermute | solution.py:461
  91.4 2.5 %collective-permute-start.30 = (bf16[272,640]{1,0:T(8,128)(2,1)S(1)}, bf16[272,640]{1,0:T(8,128)(2,1)S(1)}, u32[]{:S(2)}, u32[]{:S(2)}) collective-permute-start(bf16[272,640]{1,0:T(8,128)(2,1)S(1)} %fusion.1.rest_0_.rest_2_), channel_id=1, source_target_pairs={{32,64},{64,32},{40,72},{72,40},{48,80},{80,48},{56,88},{88,56},{1... | collective-permute-start | bytes 1044488 | tf_op jit(solution)/shard_map/ppermute | solution.py:461
  94.1 12.9 %collective-permute-start.23 = (bf16[256,640]{1,0:T(8,128)(2,1)S(1)}, bf16[256,640]{1,0:T(8,128)(2,1)S(1)}, u32[]{:S(2)}, u32[]{:S(2)}) collective-permute-start(bf16[256,640]{1,0:T(8,128)(2,1)S(1)} %broadcast_select_fusion.2), channel_id=1, source_target_pairs={{48,32},{56,40},{80,64},{88,72},{112,96},{120,104},{176,160},{184,... | collective-permute-start | bytes 983048 | tf_op jit(solution)/shard_map/ppermute | solution.py:461
  107.0 5.0 %collective-permute-done.23.rest_27_.rest_28_ = bf16[256,640]{1,0:T(8,128)(2,1)S(1)} collective-permute-done((bf16[256,640]{1,0:T(8,128)(2,1)S(1)}, bf16[256,640]{1,0:T(8,128)(2,1)S(1)}, u32[]{:S(2)}, u32[]{:S(2)}) %collective-permute-start.23) | collective-permute-done | bytes 327712 | tf_op jit(solution)/shard_map/ppermute | solution.py:461
  112.0 6.9 %forward.1 = (f32[256,640]{1,0:T(8,128)S(1)}, f32[16,640]{1,0:T(8,128)S(1)}, f32[2,128]{1,0:T(2,128)S(1)}) custom-call(s32[12]{0:T(128)S(1)} %reshape.20.slots, s32[12]{0:T(128)S(1)} %reshape.21.counts, s32[13]{0:T(128)S(1)} %convert_element_type.12.used, bf16[256,640]{1,0:T(8,128)(2,1)S(1)} %copy-done.2, bf16[256,640]{1,0:T(8,128)(2,1)S(1)} %copy-done.3, ...), custom_call_target="tpu_custom_call" | custom-call | tf_op jit(solution)/shard_map/forward/pallas_call | solution.py:513
  119.0 1.1 collective-permute-done.24
  120.2 21.1 %collective-permute-start.25 = (f32[2,128]{1,0:T(2,128)S(1)}, f32[2,128]{1,0:T(2,128)S(1)}, u32[]{:S(2)}, u32[]{:S(2)}) collective-permute-start(f32[2,128]{1,0:T(2,128)S(1)} %add.49), channel_id=1, source_target_pairs={{0,2},{1,3},{2,0},{3,1},{4,6},{5,7},{6,4},{7,5},{8,10},{9,11},{10,... | collective-permute-start | bytes 3080 | tf_op jit(solution)/shard_map/ppermute | solution.py:530
  141.2 1.6 collective-permute-done.25
  142.8 3.4 %collective-permute-start.31 = (bf16[272,640]{1,0:T(8,128)(2,1)S(1)}, bf16[272,640]{1,0:T(8,128)(2,1)S(1)}, u32[]{:S(2)}, u32[]{:S(2)}) collective-permute-start(bf16[272,640]{1,0:T(8,128)(2,1)S(1)} %fusion.1.rest_0_.rest_2_), channel_id=1, source_target_pairs={{0,16},{8,24},{16,0},{24,8},{32,48},{40,56},{48,32},{56,40},{64,80... | collective-permute-start | bytes 1044488 | tf_op jit(solution)/shard_map/ppermute | solution.py:461
  146.2 2.7 %collective-permute-start.33 = (bf16[272,640]{1,0:T(8,128)(2,1)S(1)}, bf16[272,640]{1,0:T(8,128)(2,1)S(1)}, u32[]{:S(2)}, u32[]{:S(2)}) collective-permute-start(bf16[272,640]{1,0:T(8,128)(2,1)S(1)} %fusion.1.rest_0_.rest_2_), channel_id=1, source_target_pairs={{8,16},{16,8},{24,32},{32,24},{40,48},{48,40},{56,64},{64,56},{72,... | collective-permute-start | bytes 1044488 | tf_op jit(solution)/shard_map/ppermute | solution.py:461
  148.9 1.3 collective-permute-start.34
  150.2 0.7 collective-permute-start.35
  151.0 0.9 upstream.1.rest_1_.rest_11_
  151.9 3.5 %collective-permute-done.31.rest_5_.rest_7_ = bf16[272,640]{1,0:T(8,128)(2,1)S(1)} collective-permute-done((bf16[272,640]{1,0:T(8,128)(2,1)S(1)}, bf16[272,640]{1,0:T(8,128)(2,1)S(1)}, u32[]{:S(2)}, u32[]{:S(2)}) %collective-permute-start.31) | collective-permute-done | bytes 348192 | tf_op jit(solution)/shard_map/ppermute | solution.py:461
  155.4 0.7 collective-permute-start.36
  156.1 4.4 %collective-permute-done.32.rest_6_.rest_8_ = bf16[272,640]{1,0:T(8,128)(2,1)S(1)} collective-permute-done((bf16[272,640]{1,0:T(8,128)(2,1)S(1)}, bf16[272,640]{1,0:T(8,128)(2,1)S(1)}, u32[]{:S(2)}, u32[]{:S(2)}) %collective-permute-start.32) | collective-permute-done | bytes 348192 | tf_op jit(solution)/shard_map/ppermute | solution.py:461
  160.5 0.7 collective-permute-start.37
  161.2 8.8 %collective-permute-start.38 = (bf16[272,640]{1,0:T(8,128)(2,1)S(1)}, bf16[272,640]{1,0:T(8,128)(2,1)S(1)}, u32[]{:S(2)}, u32[]{:S(2)}) collective-permute-start(bf16[272,640]{1,0:T(8,128)(2,1)S(1)} %broadcast_select_fusion.1), channel_id=1, source_target_pairs={{48,32},{56,40},{80,64},{88,72},{112,96},{120,104},{176,160},{184,... | collective-permute-start | bytes 1044488 | tf_op jit(solution)/shard_map/ppermute | solution.py:461
  170.2 1.9 collective-permute-start.42
  172.3 3.0 %collective-permute-start.40 = (bf16[272,640]{1,0:T(8,128)(2,1)S(1)}, bf16[272,640]{1,0:T(8,128)(2,1)S(1)}, u32[]{:S(2)}, u32[]{:S(2)}) collective-permute-start(bf16[272,640]{1,0:T(8,128)(2,1)S(1)} %upstream.1.rest_1_.rest_11_), channel_id=1, source_target_pairs={{0,64},{8,72},{16,80},{24,88},{32,96},{40,104},{48,112},{56,120},{... | collective-permute-start | bytes 1044488 | tf_op jit(solution)/shard_map/ppermute | solution.py:461
  175.3 2.7 %collective-permute-done.38.rest_12_.rest_7_ = bf16[272,640]{1,0:T(8,128)(2,1)S(1)} collective-permute-done((bf16[272,640]{1,0:T(8,128)(2,1)S(1)}, bf16[272,640]{1,0:T(8,128)(2,1)S(1)}, u32[]{:S(2)}, u32[]{:S(2)}) %collective-permute-start.38) | collective-permute-done | bytes 348192 | tf_op jit(solution)/shard_map/ppermute | solution.py:461
  178.0 5.0 %collective-permute-start.46 = (bf16[272,640]{1,0:T(8,128)(2,1)S(1)}, bf16[272,640]{1,0:T(8,128)(2,1)S(1)}, u32[]{:S(2)}, u32[]{:S(2)}) collective-permute-start(bf16[272,640]{1,0:T(8,128)(2,1)S(1)} %upstream.1.rest_1_.rest_11_), channel_id=1, source_target_pairs={{64,128},{128,64},{72,136},{136,72},{80,144},{144,80},{88,152},{15... | collective-permute-start | bytes 1044488 | tf_op jit(solution)/shard_map/ppermute | solution.py:461
  183.1 8.9 %collective-permute-start.43 = (bf16[272,640]{1,0:T(8,128)(2,1)S(1)}, bf16[272,640]{1,0:T(8,128)(2,1)S(1)}, u32[]{:S(2)}, u32[]{:S(2)}) collective-permute-start(bf16[272,640]{1,0:T(8,128)(2,1)S(1)} %upstream.1.rest_1_.rest_11_), channel_id=1, source_target_pairs={{0,16},{8,24},{16,0},{24,8},{32,48},{40,56},{48,32},{56,40},{64,80... | collective-permute-start | bytes 1044488 | tf_op jit(solution)/shard_map/ppermute | solution.py:461
  192.0 2.6 %collective-permute-start.45 = (bf16[272,640]{1,0:T(8,128)(2,1)S(1)}, bf16[272,640]{1,0:T(8,128)(2,1)S(1)}, u32[]{:S(2)}, u32[]{:S(2)}) collective-permute-start(bf16[272,640]{1,0:T(8,128)(2,1)S(1)} %upstream.1.rest_1_.rest_11_), channel_id=1, source_target_pairs={{8,16},{16,8},{24,32},{32,24},{40,48},{48,40},{56,64},{64,56},{72,... | collective-permute-start | bytes 1044488 | tf_op jit(solution)/shard_map/ppermute | solution.py:461
  194.6 0.7 collective-permute-start.47
  195.3 8.3 %collective-permute-done.46.rest_19_ = bf16[272,640]{1,0:T(8,128)(2,1)S(1)} collective-permute-done((bf16[272,640]{1,0:T(8,128)(2,1)S(1)}, bf16[272,640]{1,0:T(8,128)(2,1)S(1)}, u32[]{:S(2)}, u32[]{:S(2)}) %collective-permute-start.46) | collective-permute-done | bytes 348192 | tf_op jit(solution)/shard_map/ppermute | solution.py:461
  203.6 0.7 collective-permute-start.48
  204.3 0.7 collective-permute-start.49
  205.0 1.6 collective-permute-done.44.rest_17_
  206.6 16.5 %collective-permute-start.50 = (bf16[272,640]{1,0:T(8,128)(2,1)S(1)}, bf16[272,640]{1,0:T(8,128)(2,1)S(1)}, u32[]{:S(2)}, u32[]{:S(2)}) collective-permute-start(bf16[272,640]{1,0:T(8,128)(2,1)S(1)} %broadcast_select_fusion), channel_id=1, source_target_pairs={{48,32},{56,40},{80,64},{88,72},{112,96},{120,104},{176,160},{184,... | collective-permute-start | bytes 1044488 | tf_op jit(solution)/shard_map/ppermute | solution.py:461
  223.2 7.9 %grad_queries.1 = bf16[256,640]{1,0:T(8,128)(2,1)} custom-call(s32[12]{0:T(128)S(1)} %reshape.20.slots, s32[12]{0:T(128)S(1)} %reshape.21.counts, s32[13]{0:T(128)S(1)} %convert_element_type.12.used, bf16[256,640]{1,0:T(8,128)(2,1)S(1)} %copy-done.2, bf16[272,640]{1,0:T(8,128)(2,1)S(1)} %upstream.1.rest_1_.rest_11_, ...), custom_call_target="tpu_custom_call" | custom-call | tf_op jit(solution)/shard_map/grad_queries/pallas_call | solution.py:557
  231.1 0.8 naming.1.names
  231.9 9.7 %shard_map.103 = (f32[256,640]{1,0:T(8,128)S(1)}, f32[256,640]{1,0:T(8,128)S(1)}) custom-call(s32[16,128]{1,0:T(8,128)S(1)} %naming.1.names, s32[2]{0:T(128)S(1)} %fusion.7.counts, bf16[256,640]{1,0:T(8,128)(2,1)S(1)} %copy-done, bf16[256,640]{1,0:T(8,128)(2,1)S(1)} %copy-done.1, bf16[272,640]{1,0:T(8,128)(2,1)S(1)} %fusion.1.rest_0_.rest_2_, ...), custom_call_target="tpu_custom_call" | custom-call | tf_op jit(solution)/shard_map/pallas_call | solution.py:589
  241.6 4.3 %shard_map.104 = (bf16[256,640]{1,0:T(8,128)(2,1)}, bf16[256,640]{1,0:T(8,128)(2,1)}) custom-call(s32[16,128]{1,0:T(8,128)S(1)} %naming.1.names, s32[2]{0:T(128)S(1)} %fusion.7.counts, bf16[256,640]{1,0:T(8,128)(2,1)S(1)} %copy-done, bf16[256,640]{1,0:T(8,128)(2,1)S(1)} %copy-done.1, f32[256,640]{1,0:T(8,128)S(1)} %get-tuple-element.27.rest_2_, ...), custom_call_target="tpu_custom_call" | custom-call | tf_op jit(solution)/shard_map/pallas_call | solution.py:590
  (84 shorter events, 3.3 us)
Async XLA Ops:
  0.6 16.3 %collective-permute-start = (bf16[256,640]{1,0:T(8,128)(2,1)}, bf16[256,640]{1,0:T(8,128)(2,1)S(1)}, u32[]{:S(2)}, u32[]{:S(2)}) collective-permute-start(bf16[256,640]{1,0:T(8,128)(2,1)} %rest_0_.7), channel_id=1, source_target_pairs={{0,128},{8,136},{16,144},{24,152},{32,160},{40,168},{48,176},{56,1... | collective-permute-start | bytes 983048 | tf_op jit(solution)/shard_map/ppermute | solution.py:461
  7.9 12.3 %collective-permute-start.1 = (bf16[256,640]{1,0:T(8,128)(2,1)}, bf16[256,640]{1,0:T(8,128)(2,1)S(1)}, u32[]{:S(2)}, u32[]{:S(2)}) collective-permute-start(bf16[256,640]{1,0:T(8,128)(2,1)} %rest_0_.7), channel_id=1, source_target_pairs={{0,64},{8,72},{16,80},{24,88},{32,96},{40,104},{48,112},{56,120},{... | collective-permute-start | bytes 983048 | tf_op jit(solution)/shard_map/ppermute | solution.py:461
  8.2 16.6 %collective-permute-start.2 = (bf16[256,640]{1,0:T(8,128)(2,1)}, bf16[256,640]{1,0:T(8,128)(2,1)S(1)}, u32[]{:S(2)}, u32[]{:S(2)}) collective-permute-start(bf16[256,640]{1,0:T(8,128)(2,1)} %rest_0_.7), channel_id=1, source_target_pairs={{0,32},{8,40},{16,48},{24,56},{32,0},{40,8},{48,16},{56,24},{64,96... | collective-permute-start | bytes 983048 | tf_op jit(solution)/shard_map/ppermute | solution.py:461
  10.4 23.3 %collective-permute-start.3 = (bf16[256,640]{1,0:T(8,128)(2,1)}, bf16[256,640]{1,0:T(8,128)(2,1)S(1)}, u32[]{:S(2)}, u32[]{:S(2)}) collective-permute-start(bf16[256,640]{1,0:T(8,128)(2,1)} %rest_0_.7), channel_id=1, source_target_pairs={{32,64},{64,32},{40,72},{72,40},{48,80},{80,48},{56,88},{88,56},{1... | collective-permute-start | bytes 983048 | tf_op jit(solution)/shard_map/ppermute | solution.py:461
  13.9 19.9 %collective-permute-start.4 = (bf16[256,640]{1,0:T(8,128)(2,1)}, bf16[256,640]{1,0:T(8,128)(2,1)S(1)}, u32[]{:S(2)}, u32[]{:S(2)}) collective-permute-start(bf16[256,640]{1,0:T(8,128)(2,1)} %rest_0_.7), channel_id=1, source_target_pairs={{0,16},{8,24},{16,0},{24,8},{32,48},{40,56},{48,32},{56,40},{64,80... | collective-permute-start | bytes 983048 | tf_op jit(solution)/shard_map/ppermute | solution.py:461
  17.0 19.1 %collective-permute-start.5 = (bf16[256,640]{1,0:T(8,128)(2,1)}, bf16[256,640]{1,0:T(8,128)(2,1)S(1)}, u32[]{:S(2)}, u32[]{:S(2)}) collective-permute-start(bf16[256,640]{1,0:T(8,128)(2,1)} %rest_0_.7), channel_id=1, source_target_pairs={{0,8},{8,0},{16,24},{24,16},{32,40},{40,32},{48,56},{56,48},{64,72... | collective-permute-start | bytes 983048 | tf_op jit(solution)/shard_map/ppermute | solution.py:461
  20.2 16.3 %collective-permute-start.6 = (bf16[256,640]{1,0:T(8,128)(2,1)}, bf16[256,640]{1,0:T(8,128)(2,1)S(1)}, u32[]{:S(2)}, u32[]{:S(2)}) collective-permute-start(bf16[256,640]{1,0:T(8,128)(2,1)} %rest_0_.7), channel_id=1, source_target_pairs={{8,16},{16,8},{24,32},{32,24},{40,48},{48,40},{56,64},{64,56},{72,... | collective-permute-start | bytes 983048 | tf_op jit(solution)/shard_map/ppermute | solution.py:461
  24.8 19.2 %collective-permute-start.7 = (bf16[256,640]{1,0:T(8,128)(2,1)}, bf16[256,640]{1,0:T(8,128)(2,1)S(1)}, u32[]{:S(2)}, u32[]{:S(2)}) collective-permute-start(bf16[256,640]{1,0:T(8,128)(2,1)} %rest_0_.7), channel_id=1, source_target_pairs={{64,128},{128,64},{72,136},{136,72},{80,144},{144,80},{88,152},{15... | collective-permute-start | bytes 983048 | tf_op jit(solution)/shard_map/ppermute | solution.py:461
  33.8 6.2 %copy-start.5 = (s32[2,6]{1,0:T(2,128)S(1)}, s32[2,6]{1,0:T(2,128)}, u32[]{:S(2)}) copy-start(s32[2,6]{1,0:T(2,128)} %param.13) | copy-start | bytes 148
  33.8 15.2 %collective-permute-start.12 = (bf16[256,640]{1,0:T(8,128)(2,1)}, bf16[256,640]{1,0:T(8,128)(2,1)}, u32[]{:S(2)}, u32[]{:S(2)}) collective-permute-start(bf16[256,640]{1,0:T(8,128)(2,1)} %rest_1_.5), channel_id=1, source_target_pairs={{0,128},{8,136},{16,144},{24,152},{32,160},{40,168},{48,176},{56,1... | collective-permute-start | bytes 983048 | tf_op jit(solution)/shard_map/ppermute | solution.py:461
  33.8 22.3 %collective-permute-start.13 = (bf16[256,640]{1,0:T(8,128)(2,1)}, bf16[256,640]{1,0:T(8,128)(2,1)}, u32[]{:S(2)}, u32[]{:S(2)}) collective-permute-start(bf16[256,640]{1,0:T(8,128)(2,1)} %rest_1_.5), channel_id=1, source_target_pairs={{0,64},{8,72},{16,80},{24,88},{32,96},{40,104},{48,112},{56,120},{... | collective-permute-start | bytes 983048 | tf_op jit(solution)/shard_map/ppermute | solution.py:461
  36.0 23.5 %collective-permute-start.14 = (bf16[256,640]{1,0:T(8,128)(2,1)}, bf16[256,640]{1,0:T(8,128)(2,1)S(1)}, u32[]{:S(2)}, u32[]{:S(2)}) collective-permute-start(bf16[256,640]{1,0:T(8,128)(2,1)} %rest_1_.5), channel_id=1, source_target_pairs={{0,32},{8,40},{16,48},{24,56},{32,0},{40,8},{48,16},{56,24},{64,96... | collective-permute-start | bytes 983048 | tf_op jit(solution)/shard_map/ppermute | solution.py:461
  36.6 28.3 %collective-permute-start.15 = (bf16[256,640]{1,0:T(8,128)(2,1)}, bf16[256,640]{1,0:T(8,128)(2,1)S(1)}, u32[]{:S(2)}, u32[]{:S(2)}) collective-permute-start(bf16[256,640]{1,0:T(8,128)(2,1)} %rest_1_.5), channel_id=1, source_target_pairs={{32,64},{64,32},{40,72},{72,40},{48,80},{80,48},{56,88},{88,56},{1... | collective-permute-start | bytes 983048 | tf_op jit(solution)/shard_map/ppermute | solution.py:461
  40.1 5.8 %copy-start.6 = (s32[64]{0:T(128)S(1)}, s32[64]{0:T(128)}, u32[]{:S(2)}) copy-start(s32[64]{0:T(128)} %param.14) | copy-start | bytes 772
  44.0 21.5 %collective-permute-start.16 = (bf16[256,640]{1,0:T(8,128)(2,1)}, bf16[256,640]{1,0:T(8,128)(2,1)}, u32[]{:S(2)}, u32[]{:S(2)}) collective-permute-start(bf16[256,640]{1,0:T(8,128)(2,1)} %rest_1_.5), channel_id=1, source_target_pairs={{0,16},{8,24},{16,0},{24,8},{32,48},{40,56},{48,32},{56,40},{64,80... | collective-permute-start | bytes 983048 | tf_op jit(solution)/shard_map/ppermute | solution.py:461
  48.9 17.5 %collective-permute-start.17 = (bf16[256,640]{1,0:T(8,128)(2,1)}, bf16[256,640]{1,0:T(8,128)(2,1)S(1)}, u32[]{:S(2)}, u32[]{:S(2)}) collective-permute-start(bf16[256,640]{1,0:T(8,128)(2,1)} %rest_1_.5), channel_id=1, source_target_pairs={{0,8},{8,0},{16,24},{24,16},{32,40},{40,32},{48,56},{56,48},{64,72... | collective-permute-start | bytes 983048 | tf_op jit(solution)/shard_map/ppermute | solution.py:461
  56.1 16.9 %collective-permute-start.18 = (bf16[256,640]{1,0:T(8,128)(2,1)}, bf16[256,640]{1,0:T(8,128)(2,1)S(1)}, u32[]{:S(2)}, u32[]{:S(2)}) collective-permute-start(bf16[256,640]{1,0:T(8,128)(2,1)} %rest_1_.5), channel_id=1, source_target_pairs={{8,16},{16,8},{24,32},{32,24},{40,48},{48,40},{56,64},{64,56},{72,... | collective-permute-start | bytes 983048 | tf_op jit(solution)/shard_map/ppermute | solution.py:461
  59.5 15.6 %collective-permute-start.19 = (bf16[256,640]{1,0:T(8,128)(2,1)}, bf16[256,640]{1,0:T(8,128)(2,1)S(1)}, u32[]{:S(2)}, u32[]{:S(2)}) collective-permute-start(bf16[256,640]{1,0:T(8,128)(2,1)} %rest_1_.5), channel_id=1, source_target_pairs={{64,128},{128,64},{72,136},{136,72},{80,144},{144,80},{88,152},{15... | collective-permute-start | bytes 983048 | tf_op jit(solution)/shard_map/ppermute | solution.py:461
  64.9 10.9 %collective-permute-start.8 = (bf16[256,640]{1,0:T(8,128)(2,1)S(1)}, bf16[256,640]{1,0:T(8,128)(2,1)S(1)}, u32[]{:S(2)}, u32[]{:S(2)}) collective-permute-start(bf16[256,640]{1,0:T(8,128)(2,1)S(1)} %collective-permute-done.rest_3_.rest_4_), channel_id=1, source_target_pairs={{224,128},{232,136},{240,144},{248,152},{0,96},{8,104},{16,112},{2... | collective-permute-start | bytes 983048 | tf_op jit(solution)/shard_map/ppermute | solution.py:461
  65.6 11.1 %copy-start.2 = (bf16[256,640]{1,0:T(8,128)(2,1)S(1)}, bf16[256,640]{1,0:T(8,128)(2,1)}, u32[]{:S(2)}) copy-start(bf16[256,640]{1,0:T(8,128)(2,1)} %rest_0_.5) | copy-start | bytes 983044
  65.6 11.1 %collective-permute-start.9 = (bf16[256,640]{1,0:T(8,128)(2,1)S(1)}, bf16[256,640]{1,0:T(8,128)(2,1)S(1)}, u32[]{:S(2)}, u32[]{:S(2)}) collective-permute-start(bf16[256,640]{1,0:T(8,128)(2,1)S(1)} %collective-permute-done.7.rest_10_.rest_11_), channel_id=1, source_target_pairs={{176,128},{184,136},{64,112},{72,120},{177,129},{185,137},{65,113}... | collective-permute-start | bytes 983048 | tf_op jit(solution)/shard_map/ppermute | solution.py:461
  66.5 16.7 %collective-permute-start.11 = (bf16[256,640]{1,0:T(8,128)(2,1)S(1)}, bf16[256,640]{1,0:T(8,128)(2,1)S(1)}, u32[]{:S(2)}, u32[]{:S(2)}) collective-permute-start(bf16[256,640]{1,0:T(8,128)(2,1)S(1)} %broadcast_select_fusion.3), channel_id=1, source_target_pairs={{48,32},{56,40},{80,64},{88,72},{112,96},{120,104},{176,160},{184,... | collective-permute-start | bytes 983048 | tf_op jit(solution)/shard_map/ppermute | solution.py:461
  73.1 5.1 %collective-permute-start.10 = (bf16[256,640]{1,0:T(8,128)(2,1)S(1)}, bf16[256,640]{1,0:T(8,128)(2,1)S(1)}, u32[]{:S(2)}, u32[]{:S(2)}) collective-permute-start(bf16[256,640]{1,0:T(8,128)(2,1)S(1)} %collective-permute-done.7.rest_10_.rest_11_), channel_id=1, source_target_pairs={{184,128},{64,120},{185,129},{65,121},{186,130},{66,122},{187,131}... | collective-permute-start | bytes 983048 | tf_op jit(solution)/shard_map/ppermute | solution.py:461
  75.1 16.3 %collective-permute-start.20 = (bf16[256,640]{1,0:T(8,128)(2,1)}, bf16[256,640]{1,0:T(8,128)(2,1)S(1)}, u32[]{:S(2)}, u32[]{:S(2)}) collective-permute-start(bf16[256,640]{1,0:T(8,128)(2,1)} %collective-permute-done.12.rest_16_.rest_17_), channel_id=1, source_target_pairs={{224,128},{232,136},{240,144},{248,152},{0,96},{8,104},{16,112},{2... | collective-permute-start | bytes 983048 | tf_op jit(solution)/shard_map/ppermute | solution.py:461
  75.8 15.6 %collective-permute-start.21 = (bf16[256,640]{1,0:T(8,128)(2,1)S(1)}, bf16[256,640]{1,0:T(8,128)(2,1)S(1)}, u32[]{:S(2)}, u32[]{:S(2)}) collective-permute-start(bf16[256,640]{1,0:T(8,128)(2,1)S(1)} %collective-permute-done.19.rest_23_.rest_24_), channel_id=1, source_target_pairs={{176,128},{184,136},{64,112},{72,120},{177,129},{185,137},{65,113}... | collective-permute-start | bytes 983048 | tf_op jit(solution)/shard_map/ppermute | solution.py:461
  76.7 17.3 %collective-permute-start.22 = (bf16[256,640]{1,0:T(8,128)(2,1)S(1)}, bf16[256,640]{1,0:T(8,128)(2,1)S(1)}, u32[]{:S(2)}, u32[]{:S(2)}) collective-permute-start(bf16[256,640]{1,0:T(8,128)(2,1)S(1)} %collective-permute-done.19.rest_23_.rest_24_), channel_id=1, source_target_pairs={{184,128},{64,120},{185,129},{65,121},{186,130},{66,122},{187,131}... | collective-permute-start | bytes 983048 | tf_op jit(solution)/shard_map/ppermute | solution.py:461
  78.1 33.9 %copy-start = (bf16[256,640]{1,0:T(8,128)(2,1)S(1)}, bf16[256,640]{1,0:T(8,128)(2,1)}, u32[]{:S(2)}) copy-start(bf16[256,640]{1,0:T(8,128)(2,1)} %rest_0_.7) | copy-start | bytes 983044
  78.1 33.9 %copy-start.1 = (bf16[256,640]{1,0:T(8,128)(2,1)S(1)}, bf16[256,640]{1,0:T(8,128)(2,1)}, u32[]{:S(2)}) copy-start(bf16[256,640]{1,0:T(8,128)(2,1)} %rest_1_.5) | copy-start | bytes 983044
  78.1 33.9 %copy-start.3 = (bf16[256,640]{1,0:T(8,128)(2,1)S(1)}, bf16[256,640]{1,0:T(8,128)(2,1)}, u32[]{:S(2)}) copy-start(bf16[256,640]{1,0:T(8,128)(2,1)} %rest_3_.2) | copy-start | bytes 983044
  78.2 64.6 %collective-permute-start.27 = (bf16[272,640]{1,0:T(8,128)(2,1)S(1)}, bf16[272,640]{1,0:T(8,128)(2,1)S(1)}, u32[]{:S(2)}, u32[]{:S(2)}) collective-permute-start(bf16[272,640]{1,0:T(8,128)(2,1)S(1)} %fusion.1.rest_0_.rest_2_), channel_id=1, source_target_pairs={{0,128},{8,136},{16,144},{24,152},{32,160},{40,168},{48,176},{56,1... | collective-permute-start | bytes 1044488 | tf_op jit(solution)/shard_map/ppermute | solution.py:461
  83.1 63.0 %collective-permute-start.28 = (bf16[272,640]{1,0:T(8,128)(2,1)S(1)}, bf16[272,640]{1,0:T(8,128)(2,1)S(1)}, u32[]{:S(2)}, u32[]{:S(2)}) collective-permute-start(bf16[272,640]{1,0:T(8,128)(2,1)S(1)} %fusion.1.rest_0_.rest_2_), channel_id=1, source_target_pairs={{0,64},{8,72},{16,80},{24,88},{32,96},{40,104},{48,112},{56,120},{... | collective-permute-start | bytes 1044488 | tf_op jit(solution)/shard_map/ppermute | solution.py:461
  91.4 54.7 %collective-permute-start.29 = (bf16[272,640]{1,0:T(8,128)(2,1)S(1)}, bf16[272,640]{1,0:T(8,128)(2,1)S(1)}, u32[]{:S(2)}, u32[]{:S(2)}) collective-permute-start(bf16[272,640]{1,0:T(8,128)(2,1)S(1)} %fusion.1.rest_0_.rest_2_), channel_id=1, source_target_pairs={{0,32},{8,40},{16,48},{24,56},{32,0},{40,8},{48,16},{56,24},{64,96... | collective-permute-start | bytes 1044488 | tf_op jit(solution)/shard_map/ppermute | solution.py:461
  91.4 57.4 %collective-permute-start.30 = (bf16[272,640]{1,0:T(8,128)(2,1)S(1)}, bf16[272,640]{1,0:T(8,128)(2,1)S(1)}, u32[]{:S(2)}, u32[]{:S(2)}) collective-permute-start(bf16[272,640]{1,0:T(8,128)(2,1)S(1)} %fusion.1.rest_0_.rest_2_), channel_id=1, source_target_pairs={{32,64},{64,32},{40,72},{72,40},{48,80},{80,48},{56,88},{88,56},{1... | collective-permute-start | bytes 1044488 | tf_op jit(solution)/shard_map/ppermute | solution.py:461
  94.1 18.0 %collective-permute-start.23 = (bf16[256,640]{1,0:T(8,128)(2,1)S(1)}, bf16[256,640]{1,0:T(8,128)(2,1)S(1)}, u32[]{:S(2)}, u32[]{:S(2)}) collective-permute-start(bf16[256,640]{1,0:T(8,128)(2,1)S(1)} %broadcast_select_fusion.2), channel_id=1, source_target_pairs={{48,32},{56,40},{80,64},{88,72},{112,96},{120,104},{176,160},{184,... | collective-permute-start | bytes 983048 | tf_op jit(solution)/shard_map/ppermute | solution.py:461
  118.9 1.2 collective-permute-start.24
  120.2 22.6 %collective-permute-start.25 = (f32[2,128]{1,0:T(2,128)S(1)}, f32[2,128]{1,0:T(2,128)S(1)}, u32[]{:S(2)}, u32[]{:S(2)}) collective-permute-start(f32[2,128]{1,0:T(2,128)S(1)} %add.49), channel_id=1, source_target_pairs={{0,2},{1,3},{2,0},{3,1},{4,6},{5,7},{6,4},{7,5},{8,10},{9,11},{10,... | collective-permute-start | bytes 3080 | tf_op jit(solution)/shard_map/ppermute | solution.py:530
  142.8 8.2 %copy-start.4 = (bf16[256,640]{1,0:T(8,128)(2,1)S(1)}, bf16[256,640]{1,0:T(8,128)(2,1)}, u32[]{:S(2)}) copy-start(bf16[256,640]{1,0:T(8,128)(2,1)} %rest_2_.3) | copy-start | bytes 983044
  142.8 7.4 %collective-permute-start.26 = (f32[2,128]{1,0:T(2,128)S(1)}, f32[2,128]{1,0:T(2,128)S(1)}, u32[]{:S(2)}, u32[]{:S(2)}) collective-permute-start(f32[2,128]{1,0:T(2,128)S(1)} %add.50), channel_id=1, source_target_pairs={{0,4},{1,5},{2,6},{3,7},{4,0},{5,1},{6,2},{7,3},{8,12},{9,13},{10,... | collective-permute-start | bytes 3080 | tf_op jit(solution)/shard_map/ppermute | solution.py:530
  142.8 12.7 %collective-permute-start.31 = (bf16[272,640]{1,0:T(8,128)(2,1)S(1)}, bf16[272,640]{1,0:T(8,128)(2,1)S(1)}, u32[]{:S(2)}, u32[]{:S(2)}) collective-permute-start(bf16[272,640]{1,0:T(8,128)(2,1)S(1)} %fusion.1.rest_0_.rest_2_), channel_id=1, source_target_pairs={{0,16},{8,24},{16,0},{24,8},{32,48},{40,56},{48,32},{56,40},{64,80... | collective-permute-start | bytes 1044488 | tf_op jit(solution)/shard_map/ppermute | solution.py:461
  146.2 14.4 %collective-permute-start.32 = (bf16[272,640]{1,0:T(8,128)(2,1)S(1)}, bf16[272,640]{1,0:T(8,128)(2,1)S(1)}, u32[]{:S(2)}, u32[]{:S(2)}) collective-permute-start(bf16[272,640]{1,0:T(8,128)(2,1)S(1)} %fusion.1.rest_0_.rest_2_), channel_id=1, source_target_pairs={{0,8},{8,0},{16,24},{24,16},{32,40},{40,32},{48,56},{56,48},{64,72... | collective-permute-start | bytes 1044488 | tf_op jit(solution)/shard_map/ppermute | solution.py:461
  146.2 15.1 %collective-permute-start.33 = (bf16[272,640]{1,0:T(8,128)(2,1)S(1)}, bf16[272,640]{1,0:T(8,128)(2,1)S(1)}, u32[]{:S(2)}, u32[]{:S(2)}) collective-permute-start(bf16[272,640]{1,0:T(8,128)(2,1)S(1)} %fusion.1.rest_0_.rest_2_), channel_id=1, source_target_pairs={{8,16},{16,8},{24,32},{32,24},{40,48},{48,40},{56,64},{64,56},{72,... | collective-permute-start | bytes 1044488 | tf_op jit(solution)/shard_map/ppermute | solution.py:461
  148.9 21.2 %collective-permute-start.34 = (bf16[272,640]{1,0:T(8,128)(2,1)S(1)}, bf16[272,640]{1,0:T(8,128)(2,1)S(1)}, u32[]{:S(2)}, u32[]{:S(2)}) collective-permute-start(bf16[272,640]{1,0:T(8,128)(2,1)S(1)} %collective-permute-done.27.rest_1_.rest_3_), channel_id=1, source_target_pairs={{192,128},{200,136},{208,144},{216,152},{224,160},{232,168},{240,1... | collective-permute-start | bytes 1044488 | tf_op jit(solution)/shard_map/ppermute | solution.py:461
  150.2 20.0 %collective-permute-start.35 = (bf16[272,640]{1,0:T(8,128)(2,1)S(1)}, bf16[272,640]{1,0:T(8,128)(2,1)S(1)}, u32[]{:S(2)}, u32[]{:S(2)}) collective-permute-start(bf16[272,640]{1,0:T(8,128)(2,1)S(1)} %collective-permute-done.27.rest_1_.rest_3_), channel_id=1, source_target_pairs={{224,128},{232,136},{240,144},{248,152},{0,96},{8,104},{16,112},{2... | collective-permute-start | bytes 1044488 | tf_op jit(solution)/shard_map/ppermute | solution.py:461
  155.4 16.7 %collective-permute-start.36 = (bf16[272,640]{1,0:T(8,128)(2,1)S(1)}, bf16[272,640]{1,0:T(8,128)(2,1)S(1)}, u32[]{:S(2)}, u32[]{:S(2)}) collective-permute-start(bf16[272,640]{1,0:T(8,128)(2,1)S(1)} %collective-permute-done.27.rest_1_.rest_3_), channel_id=1, source_target_pairs={{240,128},{248,136},{0,112},{8,120},{241,129},{249,137},{1,113},{9... | collective-permute-start | bytes 1044488 | tf_op jit(solution)/shard_map/ppermute | solution.py:461
  160.5 11.7 %collective-permute-start.37 = (bf16[272,640]{1,0:T(8,128)(2,1)S(1)}, bf16[272,640]{1,0:T(8,128)(2,1)S(1)}, u32[]{:S(2)}, u32[]{:S(2)}) collective-permute-start(bf16[272,640]{1,0:T(8,128)(2,1)S(1)} %collective-permute-done.27.rest_1_.rest_3_), channel_id=1, source_target_pairs={{248,128},{0,120},{249,129},{1,121},{250,130},{2,122},{251,131},{3... | collective-permute-start | bytes 1044488 | tf_op jit(solution)/shard_map/ppermute | solution.py:461
  161.2 16.8 %collective-permute-start.38 = (bf16[272,640]{1,0:T(8,128)(2,1)S(1)}, bf16[272,640]{1,0:T(8,128)(2,1)S(1)}, u32[]{:S(2)}, u32[]{:S(2)}) collective-permute-start(bf16[272,640]{1,0:T(8,128)(2,1)S(1)} %broadcast_select_fusion.1), channel_id=1, source_target_pairs={{48,32},{56,40},{80,64},{88,72},{112,96},{120,104},{176,160},{184,... | collective-permute-start | bytes 1044488 | tf_op jit(solution)/shard_map/ppermute | solution.py:461
  170.1 13.0 %collective-permute-start.41 = (bf16[272,640]{1,0:T(8,128)(2,1)S(1)}, bf16[272,640]{1,0:T(8,128)(2,1)S(1)}, u32[]{:S(2)}, u32[]{:S(2)}) collective-permute-start(bf16[272,640]{1,0:T(8,128)(2,1)S(1)} %upstream.1.rest_1_.rest_11_), channel_id=1, source_target_pairs={{0,32},{8,40},{16,48},{24,56},{32,0},{40,8},{48,16},{56,24},{64,96... | collective-permute-start | bytes 1044488 | tf_op jit(solution)/shard_map/ppermute | solution.py:461
  170.2 21.8 %collective-permute-start.42 = (bf16[272,640]{1,0:T(8,128)(2,1)S(1)}, bf16[272,640]{1,0:T(8,128)(2,1)S(1)}, u32[]{:S(2)}, u32[]{:S(2)}) collective-permute-start(bf16[272,640]{1,0:T(8,128)(2,1)S(1)} %upstream.1.rest_1_.rest_11_), channel_id=1, source_target_pairs={{32,64},{64,32},{40,72},{72,40},{48,80},{80,48},{56,88},{88,56},{1... | collective-permute-start | bytes 1044488 | tf_op jit(solution)/shard_map/ppermute | solution.py:461
  172.2 19.9 %collective-permute-start.39 = (bf16[272,640]{1,0:T(8,128)(2,1)S(1)}, bf16[272,640]{1,0:T(8,128)(2,1)S(1)}, u32[]{:S(2)}, u32[]{:S(2)}) collective-permute-start(bf16[272,640]{1,0:T(8,128)(2,1)S(1)} %upstream.1.rest_1_.rest_11_), channel_id=1, source_target_pairs={{0,128},{8,136},{16,144},{24,152},{32,160},{40,168},{48,176},{56,1... | collective-permute-start | bytes 1044488 | tf_op jit(solution)/shard_map/ppermute | solution.py:461
  172.3 22.4 %collective-permute-start.40 = (bf16[272,640]{1,0:T(8,128)(2,1)S(1)}, bf16[272,640]{1,0:T(8,128)(2,1)S(1)}, u32[]{:S(2)}, u32[]{:S(2)}) collective-permute-start(bf16[272,640]{1,0:T(8,128)(2,1)S(1)} %upstream.1.rest_1_.rest_11_), channel_id=1, source_target_pairs={{0,64},{8,72},{16,80},{24,88},{32,96},{40,104},{48,112},{56,120},{... | collective-permute-start | bytes 1044488 | tf_op jit(solution)/shard_map/ppermute | solution.py:461
  178.0 25.6 %collective-permute-start.46 = (bf16[272,640]{1,0:T(8,128)(2,1)S(1)}, bf16[272,640]{1,0:T(8,128)(2,1)S(1)}, u32[]{:S(2)}, u32[]{:S(2)}) collective-permute-start(bf16[272,640]{1,0:T(8,128)(2,1)S(1)} %upstream.1.rest_1_.rest_11_), channel_id=1, source_target_pairs={{64,128},{128,64},{72,136},{136,72},{80,144},{144,80},{88,152},{15... | collective-permute-start | bytes 1044488 | tf_op jit(solution)/shard_map/ppermute | solution.py:461
  183.1 21.2 %collective-permute-start.43 = (bf16[272,640]{1,0:T(8,128)(2,1)S(1)}, bf16[272,640]{1,0:T(8,128)(2,1)S(1)}, u32[]{:S(2)}, u32[]{:S(2)}) collective-permute-start(bf16[272,640]{1,0:T(8,128)(2,1)S(1)} %upstream.1.rest_1_.rest_11_), channel_id=1, source_target_pairs={{0,16},{8,24},{16,0},{24,8},{32,48},{40,56},{48,32},{56,40},{64,80... | collective-permute-start | bytes 1044488 | tf_op jit(solution)/shard_map/ppermute | solution.py:461
  192.0 14.6 %collective-permute-start.44 = (bf16[272,640]{1,0:T(8,128)(2,1)S(1)}, bf16[272,640]{1,0:T(8,128)(2,1)S(1)}, u32[]{:S(2)}, u32[]{:S(2)}) collective-permute-start(bf16[272,640]{1,0:T(8,128)(2,1)S(1)} %upstream.1.rest_1_.rest_11_), channel_id=1, source_target_pairs={{0,8},{8,0},{16,24},{24,16},{32,40},{40,32},{48,56},{56,48},{64,72... | collective-permute-start | bytes 1044488 | tf_op jit(solution)/shard_map/ppermute | solution.py:461
  192.0 39.9 %collective-permute-start.45 = (bf16[272,640]{1,0:T(8,128)(2,1)S(1)}, bf16[272,640]{1,0:T(8,128)(2,1)S(1)}, u32[]{:S(2)}, u32[]{:S(2)}) collective-permute-start(bf16[272,640]{1,0:T(8,128)(2,1)S(1)} %upstream.1.rest_1_.rest_11_), channel_id=1, source_target_pairs={{8,16},{16,8},{24,32},{32,24},{40,48},{48,40},{56,64},{64,56},{72,... | collective-permute-start | bytes 1044488 | tf_op jit(solution)/shard_map/ppermute | solution.py:461
  194.6 47.0 %collective-permute-start.47 = (bf16[272,640]{1,0:T(8,128)(2,1)S(1)}, bf16[272,640]{1,0:T(8,128)(2,1)S(1)}, u32[]{:S(2)}, u32[]{:S(2)}) collective-permute-start(bf16[272,640]{1,0:T(8,128)(2,1)S(1)} %collective-permute-done.39.rest_12_), channel_id=1, source_target_pairs={{224,128},{232,136},{240,144},{248,152},{0,96},{8,104},{16,112},{2... | collective-permute-start | bytes 1044488 | tf_op jit(solution)/shard_map/ppermute | solution.py:461
  203.6 38.0 %collective-permute-start.48 = (bf16[272,640]{1,0:T(8,128)(2,1)S(1)}, bf16[272,640]{1,0:T(8,128)(2,1)S(1)}, u32[]{:S(2)}, u32[]{:S(2)}) collective-permute-start(bf16[272,640]{1,0:T(8,128)(2,1)S(1)} %collective-permute-done.46.rest_19_), channel_id=1, source_target_pairs={{176,128},{184,136},{64,112},{72,120},{177,129},{185,137},{65,113}... | collective-permute-start | bytes 1044488 | tf_op jit(solution)/shard_map/ppermute | solution.py:461
  204.3 37.3 %collective-permute-start.49 = (bf16[272,640]{1,0:T(8,128)(2,1)S(1)}, bf16[272,640]{1,0:T(8,128)(2,1)S(1)}, u32[]{:S(2)}, u32[]{:S(2)}) collective-permute-start(bf16[272,640]{1,0:T(8,128)(2,1)S(1)} %collective-permute-done.46.rest_19_), channel_id=1, source_target_pairs={{184,128},{64,120},{185,129},{65,121},{186,130},{66,122},{187,131}... | collective-permute-start | bytes 1044488 | tf_op jit(solution)/shard_map/ppermute | solution.py:461
  206.6 35.0 %collective-permute-start.50 = (bf16[272,640]{1,0:T(8,128)(2,1)S(1)}, bf16[272,640]{1,0:T(8,128)(2,1)S(1)}, u32[]{:S(2)}, u32[]{:S(2)}) collective-permute-start(bf16[272,640]{1,0:T(8,128)(2,1)S(1)} %broadcast_select_fusion), channel_id=1, source_target_pairs={{48,32},{56,40},{80,64},{88,72},{112,96},{120,104},{176,160},{184,... | collective-permute-start | bytes 1044488 | tf_op jit(solution)/shard_map/ppermute | solution.py:461
